TPU v7x, 32 devices: a whole 2x2x4 slice. The times are simulated.
32 devices in a mesh: dp: 16 (over z, y, core), fsdp: 2 (over x).
Axes of the slice: x: 2, y: 2, z: 4, core: 2. Of those that a mesh axis runs over, the one named last changes fastest.
Arguments:
- tokens: bfloat16 [16384, 2048], P(('dp', 'fsdp')), may hold values from -6 to 6
- cotangent: bfloat16 [16384, 2048], P(('dp', 'fsdp')), may hold values from -6 to 6
- lengths: int32 [32], P(('dp', 'fsdp')), may hold values from 128 to 512, as said below
- widths: int32 [32], replicated, may hold values from 1 to 8
- norm_gain: float32 [2048], replicated, may hold values from 0.1 to 1.9
- w_zx: bfloat16 [2048, 2, 4096], P('dp', None, 'fsdp'), may hold values from -0.125 to 0.125
- w_bc: bfloat16 [2048, 256], P('dp'), may hold values from -0.125 to 0.125
- w_dt: bfloat16 [2048, 64], P('dp', 'fsdp'), may hold values from -0.125 to 0.125
- w_out: bfloat16 [4096, 2048], P('fsdp', 'dp'), may hold values from -0.125 to 0.125
- conv_w: float32 [4, 4352], replicated, may hold values from -3 to 3
- conv_b: float32 [4352], replicated, may hold values from -1.5 to 1.5
- dt_bias: float32 [64], replicated, may hold values from -4 to -2
- a_log: float32 [64], replicated, may hold values from -3 to 0.5
- d_skip: float32 [64], replicated, may hold values from 0.5 to 2
- gate_gain: float32 [4096], replicated, may hold values from 0.1 to 1.9
Outputs:
- output: bfloat16 [16384, 2048], P(('dp', 'fsdp'))
- input_grad: bfloat16 [16384, 2048], P(('dp', 'fsdp'))
- g_norm_gain: float32 [2048], replicated
- g_w_zx: float32 [2048, 2, 4096], P('dp', None, 'fsdp')
- g_w_bc: float32 [2048, 256], P('dp')
- g_w_dt: float32 [2048, 64], P('dp', 'fsdp')
- g_w_out: float32 [4096, 2048], P('fsdp', 'dp')
- g_conv_w: float32 [4, 4352], replicated
- g_conv_b: float32 [4352], replicated
- g_dt_bias: float32 [64], replicated
- g_a_log: float32 [64], replicated
- g_d_skip: float32 [64], replicated
- g_gate_gain: float32 [4096], replicated
Inputs may be any that keep to these rules, and one draw needn't show every extreme that they name: `lengths`: some sequence fills its whole slot of 512 positions, and some holds exactly 128.
All inputs are finite; a program needn't handle non-finite values.
Results may differ from a plain program's by a relative error of at most 0.018.
Values may be sent and summed in bfloat16 or wider, within the bound.
No kernel may reach another device: no remote copies, remote signals or barrier semaphores. Data moves between devices by JAX's collectives and lax.ppermute only.
A program may use at most 384 MiB of HBM per device.

v0:
```python
import jax
import jax.numpy as jnp
from jax import lax
from jax.sharding import PartitionSpec as P

HEADS = 64
HEAD_DIM = 64
STRETCH = 256


def low(values):
    rounded = lax.optimization_barrier(values.astype(jnp.bfloat16)).astype(jnp.float32)
    return values + lax.stop_gradient(rounded - values)


def normed_rows(values, gain):
    return values * lax.rsqrt(jnp.mean(values * values, axis=-1, keepdims=True) + 1e-05) * gain


def block_step(carry, packed):
    state_now, decay_rate = carry
    x_heads, b_mat, c_mat, steps_here = packed
    size = steps_here.shape[0]
    running = jnp.cumsum(-steps_here * decay_rate, axis=0)
    lower = jnp.arange(size)[:, None] >= jnp.arange(size)[None, :]
    spans = running.T[:, :, None] - running.T[:, None, :]
    decay = jnp.exp(jnp.where(lower[None], spans, 0.0)) * lower[None].astype(jnp.float32)
    gram = jnp.dot(
        c_mat, b_mat.T, precision=lax.Precision.HIGHEST, preferred_element_type=jnp.float32
    )
    mixing = low(gram[None] * decay * steps_here.T[:, None, :])
    intra = jnp.einsum("hts,hsp->htp", mixing, x_heads, precision=lax.Precision.HIGHEST)
    prior = low(state_now)
    inter = jnp.exp(running.T)[:, :, None] * jnp.einsum(
        "tn,hpn->htp", c_mat, prior, precision=lax.Precision.HIGHEST
    )
    tail = running[-1]
    factor = jnp.exp(tail[None, :] - running) * steps_here
    weighted = low(x_heads * factor.T[:, :, None])
    new_state = jnp.exp(tail)[:, None, None] * state_now + jnp.einsum(
        "hsp,sn->hpn", weighted, b_mat, precision=lax.Precision.HIGHEST
    )
    return ((new_state, decay_rate), intra + inter)


def mixer(xr, bc, dtr, params, limit, channel_base):
    conv_w, conv_b, dt_bias, a_log, d_skip = params
    slot = xr.shape[0]
    inner = xr.shape[1]
    heads = dtr.shape[1]
    head_dim = inner // heads
    state = bc.shape[1] // 2
    taps = conv_w.shape[0]
    total = conv_w.shape[1]
    tap_w = jnp.concatenate(
        [lax.dynamic_slice_in_dim(conv_w, channel_base, inner, 1), conv_w[:, total - 2 * state :]],
        axis=1,
    )
    tap_b = jnp.concatenate(
        [lax.dynamic_slice_in_dim(conv_b, channel_base, inner, 0), conv_b[total - 2 * state :]]
    )
    joined = jnp.concatenate([xr, bc], axis=1)
    padded = jnp.pad(joined, ((taps - 1, 0), (0, 0)))
    conv = tap_b + sum((tap_w[k] * padded[k : k + slot] for k in range(taps)))
    act = jax.nn.silu(conv)
    channel = jnp.arange(inner)
    used_mask = (channel < limit).astype(jnp.float32)
    x_used = low(act[:, :inner] * used_mask)
    b_all = low(act[:, inner : inner + state])
    c_all = low(act[:, inner + state :])
    steps = jax.nn.softplus(dtr + dt_bias)
    decay_rate = jnp.exp(a_log)
    blocks = slot // STRETCH
    x_blocks = x_used.reshape(blocks, STRETCH, heads, head_dim).transpose(0, 2, 1, 3)
    start = (jnp.zeros((heads, head_dim, state), jnp.float32), decay_rate)
    carried, y_blocks = lax.scan(
        jax.checkpoint(block_step),
        start,
        (
            x_blocks,
            b_all.reshape(blocks, STRETCH, state),
            c_all.reshape(blocks, STRETCH, state),
            steps.reshape(blocks, STRETCH, heads),
        ),
    )
    return y_blocks.transpose(0, 2, 1, 3).reshape(slot, inner) + x_used * jnp.repeat(
        d_skip, head_dim
    )


def gate_mix(values, gates):
    return values * jax.nn.silu(gates)


def dot_rows(left, right):
    return lax.dot_general(
        left, right, (((0,), (0,)), ((), ())), preferred_element_type=jnp.float32
    )


def dot_back(left, right):
    return lax.dot_general(
        left, right, (((1,), (1,)), ((), ())), preferred_element_type=jnp.float32
    )


def per_device(
    tokens,
    cotangent,
    lengths,
    widths,
    norm_gain,
    w_zx,
    w_bc,
    w_dt,
    w_out,
    conv_w,
    conv_b,
    dt_bias,
    a_log,
    d_skip,
    gate_gain,
):
    seq_count = lengths.shape[0]
    rows = tokens.shape[0]
    slot = rows // seq_count
    group_size = lax.axis_size("fsdp")
    fsdp_index = lax.axis_index("fsdp")
    dp_index = lax.axis_index("dp")
    params = (conv_w, conv_b, dt_bias, a_log, d_skip)
    rows_zx, rows_bc, rows_dt, rows_out = (
        lax.all_gather(w_zx, "dp", axis=0, tiled=True),
        lax.all_gather(w_bc, "dp", axis=0, tiled=True),
        lax.all_gather(w_dt, "dp", axis=0, tiled=True),
        lax.all_gather(w_out, "dp", axis=1, tiled=True),
    )
    u = tokens.astype(jnp.float32)
    normed = normed_rows(u, norm_gain).astype(jnp.bfloat16)
    valid = (jnp.arange(slot)[None, :] < lengths[:, None]).reshape(rows)
    d_branch = jnp.where(valid[:, None], cotangent, jnp.zeros_like(cotangent))
    whole_zx, whole_dt, whole_out = (
        lax.all_gather(rows_zx, "fsdp", axis=2, tiled=True),
        lax.all_gather(rows_dt, "fsdp", axis=1, tiled=True),
        lax.all_gather(rows_out, "fsdp", axis=0, tiled=True),
    )
    first_seq = (dp_index * group_size + fsdp_index) * seq_count
    channel_base = fsdp_index * 0
    inner_local = whole_zx.shape[2]
    heads_local = whole_dt.shape[1]
    flat = normed.shape[0]
    seq_widths = lax.dynamic_slice_in_dim(widths, first_seq, seq_count, 0)
    limits = seq_widths * (HEADS // 8) * HEAD_DIM
    counts = limits.astype(jnp.float32)[:, None]
    zx = jnp.einsum("td,dki->tki", normed, whole_zx, preferred_element_type=jnp.float32)
    bc = jnp.dot(normed, rows_bc, preferred_element_type=jnp.float32)
    dtr = jnp.dot(normed, whole_dt, preferred_element_type=jnp.float32)
    per_seq = (
        zx[:, 0].reshape(seq_count, slot, inner_local),
        zx[:, 1].reshape(seq_count, slot, inner_local),
        bc.reshape(seq_count, slot, bc.shape[1]),
        dtr.reshape(seq_count, slot, heads_local),
        limits,
    )

    def forward_one(packed):
        z, xr, bc_seq, dt_seq, limit = packed
        return gate_mix(mixer(xr, bc_seq, dt_seq, params, limit, channel_base), z)

    gated = lax.map(forward_one, per_seq)
    squares = jnp.sum(gated * gated, axis=-1)
    scale = lax.rsqrt(squares / counts + 1e-05)
    gnorm = (gated * scale[..., None] * gate_gain).reshape(flat, inner_local).astype(jnp.bfloat16)
    branch = jnp.dot(gnorm, whole_out, preferred_element_type=jnp.float32)
    output = (u + jnp.where(valid[:, None], branch, 0.0)).astype(jnp.bfloat16)
    g_w_out = dot_rows(gnorm, d_branch)
    d_gnorm = dot_back(d_branch, whole_out).reshape(seq_count, slot, inner_local)
    gain_grad = d_gnorm * gate_gain
    g_gate_local = jnp.sum(d_gnorm * gated * scale[..., None], axis=(0, 1))
    inner_sum = jnp.sum(gain_grad * gated, axis=-1)
    d_gated = (
        gain_grad * scale[..., None]
        - gated * (scale * scale * scale / counts * inner_sum)[..., None]
    )

    def backward_one(packed):
        z, xr, bc_seq, dt_seq, limit, grad = packed

        def local(xr_in, bc_in, dt_in, params_in):
            return mixer(xr_in, bc_in, dt_in, params_in, limit, channel_base)

        mixed, pull = jax.vjp(local, xr, bc_seq, dt_seq, params)
        unused, pull_gate = jax.vjp(gate_mix, mixed, z)
        d_mixed, d_gate = pull_gate(grad)
        d_mixed = d_mixed.astype(jnp.bfloat16).astype(jnp.float32)
        d_xr, d_bc, d_dt, d_params = pull(d_mixed)
        return (d_gate, d_xr, d_bc, d_dt, d_params)

    dz, dxr, dbc, ddt, dparams = lax.map(backward_one, per_seq + (d_gated,))
    dbc_flat = dbc.reshape(flat, dbc.shape[2])
    dzx_low = jnp.stack(
        [dz.reshape(flat, inner_local), dxr.reshape(flat, inner_local)], axis=1
    ).astype(jnp.bfloat16)
    dbc_low = dbc_flat.astype(jnp.bfloat16)
    ddt_low = ddt.reshape(flat, heads_local).astype(jnp.bfloat16)
    g_w_zx = jnp.einsum("td,tki->dki", normed, dzx_low, preferred_element_type=jnp.float32)
    g_w_bc = dot_rows(normed, dbc_low)
    g_w_dt = dot_rows(normed, ddt_low)
    d_normed = jnp.einsum(
        "tki,dki->td", dzx_low, whole_zx, preferred_element_type=jnp.float32
    ) + dot_back(ddt_low, whole_dt)
    d_normed = d_normed + dot_back(dbc_low, rows_bc)
    unused_rows, pull_norm = jax.vjp(normed_rows, u, norm_gain)
    d_u, d_norm_gain = pull_norm(d_normed)
    input_grad = (cotangent.astype(jnp.float32) + d_u).astype(jnp.bfloat16)
    g_zx, g_dt, g_out = (
        lax.psum_scatter(
            g_w_zx.astype(jnp.bfloat16), "fsdp", scatter_dimension=2, tiled=True
        ).astype(jnp.float32),
        lax.psum_scatter(
            g_w_dt.astype(jnp.bfloat16), "fsdp", scatter_dimension=1, tiled=True
        ).astype(jnp.float32),
        lax.psum_scatter(
            g_w_out.astype(jnp.bfloat16), "fsdp", scatter_dimension=0, tiled=True
        ).astype(jnp.float32),
    )
    g_bc = lax.psum(g_w_bc.astype(jnp.bfloat16), "fsdp").astype(jnp.float32)
    g_zx, g_bc, g_dt, g_out = (
        lax.psum_scatter(g_zx.astype(jnp.bfloat16), "dp", scatter_dimension=0, tiled=True).astype(
            jnp.float32
        ),
        lax.psum_scatter(g_bc.astype(jnp.bfloat16), "dp", scatter_dimension=0, tiled=True).astype(
            jnp.float32
        ),
        lax.psum_scatter(g_dt.astype(jnp.bfloat16), "dp", scatter_dimension=0, tiled=True).astype(
            jnp.float32
        ),
        lax.psum_scatter(g_out.astype(jnp.bfloat16), "dp", scatter_dimension=1, tiled=True).astype(
            jnp.float32
        ),
    )
    param_sums = tuple((jnp.sum(piece, axis=0) for piece in dparams))
    g_norm, g_taps, g_bias, g_dt_bias, g_a_log, g_skip, g_gate = lax.psum(
        (d_norm_gain,) + param_sums + (g_gate_local,), ("dp", "fsdp")
    )
    return (
        output,
        input_grad,
        g_norm,
        g_zx,
        g_bc,
        g_dt,
        g_out,
        g_taps,
        g_bias,
        g_dt_bias,
        g_a_log,
        g_skip,
        g_gate,
    )


def solution(mesh):
    in_specs = (
        P(("dp", "fsdp"), None),
        P(("dp", "fsdp"), None),
        P(("dp", "fsdp")),
        P(),
        P(),
        P("dp", None, "fsdp"),
        P("dp", None),
        P("dp", "fsdp"),
        P("fsdp", "dp"),
        P(),
        P(),
        P(),
        P(),
        P(),
        P(),
    )
    out_specs = (
        P(("dp", "fsdp"), None),
        P(("dp", "fsdp"), None),
        P(),
        P("dp", None, "fsdp"),
        P("dp", None),
        P("dp", "fsdp"),
        P("fsdp", "dp"),
        P(),
        P(),
        P(),
        P(),
        P(),
        P(),
    )
    return jax.shard_map(
        per_device, mesh=mesh, in_specs=in_specs, out_specs=out_specs, check_vma=False
    )
```

profile of v0, /device:TPU:0, one launch (start us, length us, event | category | flops | bytes accessed | tf_op | source)
XLA Modules:
  0.0 2583.8 jit_solution(8009933725492706169)
XLA Ops:
  11.3 129.1 %all-gather.6.cloned.1.call-done = bf16[2048,2,2048]{2,0,1:T(8,128)(2,1)} async-done(((bf16[128,2,2048]{2,0,1:T(8,128)(2,1)}), bf16[2048,2,2048]{2,0,1:T(8,128)(2,1)}) %all-gather.6.cloned.1.call-update) | async-done | bytes 16777232 | tf_op jit(solution)/shard_map/all_gather | solution.py:132
  181.4 76.6 %all-gather.12.cloned.1.call-done = bf16[2048,2048]{1,0:T(8,128)(2,1)} async-done(((bf16[2048,128]{1,0:T(8,128)(2,1)}), bf16[2048,2048]{1,0:T(8,128)(2,1)}) %all-gather.12.cloned.1.call-update) | async-done | bytes 8388624 | tf_op jit(solution)/shard_map/all_gather | solution.py:135
  258.2 387.9 %all-gather.8.cloned.1.call-done = bf16[2048,2,4096]{2,0,1:T(8,128)(2,1)} async-done(((bf16[2048,2,2048]{2,0,1:T(8,128)(2,1)}), bf16[2048,2,4096]{2,0,1:T(8,128)(2,1)}) %all-gather.8.cloned.1.call-update) | async-done | bytes 33554448 | tf_op jit(solution)/shard_map/all_gather | solution.py:142
  646.1 27.9 %fusion.168 = f32[512,2,4096]{2,0,1:T(8,128)} fusion(bf16[2048,2,4096]{2,0,1:T(8,128)(2,1)} %all-gather.8.cloned.1.call-done, bf16[512,2048]{1,0:T(8,128)(2,1)} %param.21, f32[2048]{0:T(1024)S(1)} %copy-done.36, f32[512]{0:T(512)S(1)} %fusion.180), kind=kOutput, calls=%fused_computation.292 | convolution fusion | flops 17184063488 | bytes 52439040 | tf_op jit(solution)/shard_map/td,dki->tki/dot_general | solution.py:154
  693.5 19.9 fusion.142
  760.9 85.9 %while.87 = (s32[]{:T(128)}, f32[64,64,128]{2,1,0:T(8,128)S(1)}, f32[2,64,256,64]{2,3,1,0:T(8,128)}, f32[2,256,64]{1,2,0:T(8,128)S(1)}, f32[64]{0:T(128)S(1)}, /...) while((s32[]{:T(128)}, f32[64,64,128]{2,1,0:T(8,128)S(1)}, ...), condition=%wide.region_4.5_spmd.clone, body=%wide.region_1.4_spmd.clone.sunk | while | flops 6616743936 | bytes 85535944 | solution.py:76
  771.5 22.8 fusion.286
  814.2 22.8 fusion.286
  915.4 92.8 %while.88 = (s32[]{:T(128)}, f32[64,64,128]{2,1,0:T(8,128)S(1)}, f32[2,64,256,64]{2,3,1,0:T(8,128)}, f32[2,64,64,128]{3,2,1,0:T(8,128)}, f32[2,64]{1,0:T(2,128)}...) while((s32[]{:T(128)}, f32[64,64,128]{2,1,0:T(8,128)S(1)}, ...), condition=%wide.region_9.10_spmd.clone, body=%wide.region_6.9_spmd.clone.sunk | while | flops 6617268224 | bytes 123219752 | solution.py:76
  929.4 22.8 fusion.298
  975.7 22.8 fusion.298
  1082.2 245.8 %while.89 = (s32[]{:T(128)}, f32[64,64,128]{2,1,0:T(8,128)}, f32[64]{0:T(128)S(1)}, f32[2,64,256,64]{2,3,1,0:T(8,128)}, f32[2,256,128]{2,1,0:T(8,128)}, /*index=...) while((s32[]{:T(128)}, f32[64,64,128]{2,1,0:T(8,128)}, ...), condition=%wide.region_25.26_spmd.clone, body=%wide.region_11.25_spmd.clone.sunk | while | flops 14927970304 | bytes 214517360 | solution.py:76
  1147.6 27.8 %fusion.318 = (f32[64,256]{1,0:T(8,128)S(1)}, f32[64,256]{1,0:T(8,128)S(1)}, f32[64,256]{1,0:T(8,128)S(1)}, f32[256,256]{1,0:T(8,128)S(1)}, bf16[64,256,256]{2,1,0:T(8,128)(2,1)S(1)}) fusion(f32[64,256]{1,0:T(8,128)} %copy-done.13, f32[256,256]{1,0:T(8,128)} %get-tuple-element.1351, f32[64,256]{1,0:T(8,128)} %copy.327, f32[256,256]{1,0:T(8,128)} %fusion.317, ...), kind=kOutput, calls=%fused_computation.135.clone.1 | convolution fusion | flops 3292413952 | bytes 17956864 | tf_op jit(solution)/shard_map/while/body/eval_jaxpr/transpose(jvp())/while/body/eval_jaxpr/checkpoint/hts,hsp->htp/dot_general | solution.py:32
  1266.8 27.9 %fusion.318 = (f32[64,256]{1,0:T(8,128)S(1)}, f32[64,256]{1,0:T(8,128)S(1)}, f32[64,256]{1,0:T(8,128)S(1)}, f32[256,256]{1,0:T(8,128)S(1)}, bf16[64,256,256]{2,1,0:T(8,128)(2,1)S(1)}) fusion(f32[64,256]{1,0:T(8,128)} %copy-done.13, f32[256,256]{1,0:T(8,128)} %get-tuple-element.1351, f32[64,256]{1,0:T(8,128)} %copy.327, f32[256,256]{1,0:T(8,128)} %fusion.317, ...), kind=kOutput, calls=%fused_computation.135.clone.1 | convolution fusion | flops 3292413952 | bytes 17956864 | tf_op jit(solution)/shard_map/while/body/eval_jaxpr/transpose(jvp())/while/body/eval_jaxpr/checkpoint/hts,hsp->htp/dot_general | solution.py:32
  1395.5 22.5 fusion.166
  1418.0 22.3 multiply_reduce_fusion.5
  1490.5 24.1 convolution_convert_fusion
  1517.6 190.4 %reduce-scatter.18.cloned.1.call-done = bf16[2048,2048]{1,0:T(8,128)(2,1)} async-done(((bf16[4096,2048]{1,0:T(8,128)(2,1)}), bf16[2048,2048]{1,0:T(8,128)(2,1)}) %reduce-scatter.18.cloned.1.call-update) | async-done | bytes 8388624 | tf_op jit(solution)/shard_map/reduce_scatter | solution.py:222
  1720.5 358.8 %reduce-scatter.12.cloned.1.call-done = bf16[2048,2,2048]{2,0,1:T(8,128)(2,1)} async-done(((bf16[2048,2,4096]{2,0,1:T(8,128)(2,1)}), bf16[2048,2,2048]{2,0,1:T(8,128)(2,1)}) %reduce-scatter.12.cloned.1.call-update) | async-done | bytes 16777232 | tf_op jit(solution)/shard_map/reduce_scatter | solution.py:216
  2087.0 26.9 %fusion.159 = (f32[2048]{0:T(1024)S(1)}, f32[512]{0:T(512)S(1)}, f32[512,2048]{1,0:T(8,128)}) fusion(bf16[512,2048]{1,0:T(8,128)(2,1)S(1)} %copy-done.10, f32[512]{0:T(512)S(1)} %copy-done.53, f32[2048]{0:T(1024)S(1)} %copy-done.37, f32[512,2048]{1,0:T(8,128)} %fusion.200, f32[512,2048]{1,0:T(8,128)} %fusion.199, ...), kind=kOutput, calls=%fused_computation.279 | convolution fusion | flops 17193498624 | bytes 56643584 | tf_op jit(solution)/shard_map/tki,dki->td/dot_general | solution.py:208
  2136.8 40.8 %all-reduce.15 = (f32[2048]{0:T(1024)}, f32[4352]{0:T(1024)}, f32[64]{0:T(128)}, f32[64]{0:T(128)}, f32[64]{0:T(128)}, /*index=5*/f32[4096]{0:T(1024)}) all-reduce(f32[2048]{0:T(1024)S(1)} %get-tuple-element.977, f32[4352]{0:T(1024)S(1)} %select_add_fusion.1, f32[64]{0:T(128)S(1)} %fusion.174, ...), channel_id=1, replica_groups=mesh['dp'=16,'fsdp'=2] {'dp','fsdp'}, use_global_device_ids=true, to_apply=%region_28.29 | all-reduce | flops 10688 | bytes 85504 | tf_op jit(solution)/shard_map/psum | solution.py:242
  2180.5 89.7 %reduce-scatter.24.cloned.1.call-done = bf16[128,2048]{1,0:T(8,128)(2,1)} async-done(((bf16[2048,2048]{1,0:T(8,128)(2,1)}), bf16[128,2048]{1,0:T(8,128)(2,1)}) %reduce-scatter.24.cloned.1.call-update) | async-done | bytes 524304
  2272.6 180.1 %reduce-scatter.14.cloned.1.call-done = bf16[128,2,2048]{2,0,1:T(8,128)(2,1)} async-done(((bf16[2048,2,2048]{2,0,1:T(8,128)(2,1)}), bf16[128,2,2048]{2,0,1:T(8,128)(2,1)}) %reduce-scatter.14.cloned.1.call-update) | async-done | bytes 1048592 | tf_op jit(solution)/shard_map/reduce_scatter | solution.py:228
  2456.3 119.2 %all-reduce.19.cloned.1.call-done = f32[4,4352]{1,0:T(4,128)} async-done(((f32[4,4352]{1,0:T(4,128)}), f32[4,4352]{1,0:T(4,128)}) %all-reduce.19.cloned.1.call-update) | async-done | bytes 69648 | tf_op jit(solution)/shard_map/psum | solution.py:242
  (536 shorter events, 692.6 us)
Async XLA Ops:
  7.2 133.2 %all-gather.6.cloned.1.call-start = ((), (), s32[]{:S(2)}) async-start(), calls=%async_computation.7 | async-start | bytes 17825792 | tf_op jit(solution)/shard_map/all_gather | solution.py:132
  9.8 168.9 %all-gather.10.cloned.1.call-start = ((), (), s32[]{:S(2)}) async-start(), calls=%async_computation.9 | async-start | bytes 1114112 | tf_op jit(solution)/shard_map/all_gather | solution.py:133
  10.5 247.4 %all-gather.12.cloned.1.call-start = ((), (), s32[]{:S(2)}) async-start(), calls=%async_computation.10 | async-start | bytes 8912896 | tf_op jit(solution)/shard_map/all_gather | solution.py:135
  11.3 634.9 %all-gather.8.cloned.1.call-start = ((), (), s32[]{:S(2)}) async-start(), calls=%async_computation.8 | async-start | bytes 50331648 | tf_op jit(solution)/shard_map/all_gather | solution.py:142
  140.5 867.8 %all-gather.14.cloned.1.call-start = ((), (), s32[]{:S(2)}) async-start(), calls=%async_computation.11 | async-start | bytes 25165824 | tf_op jit(solution)/shard_map/all_gather | solution.py:144
  170.8 475.4 %copy-start.52 = (f32[512]{0:T(512)}, f32[512]{0:T(512)S(1)}, u32[]{:S(2)}) copy-start(f32[512]{0:T(512)S(1)} %fusion.180) | copy-start | bytes 6148
  176.5 544.7 %copy-start.40 = (f32[4096]{0:T(1024)}, f32[4096]{0:T(1024)S(1)}, u32[]{:S(2)}) copy-start(f32[4096]{0:T(1024)S(1)} %fusion.179) | copy-start | bytes 49156
  177.3 516.2 %copy-start.42 = (f32[4352]{0:T(1024)}, f32[4352]{0:T(1024)S(1)}, u32[]{:S(2)}) copy-start(f32[4352]{0:T(1024)S(1)} %get-tuple-element.979) | copy-start | bytes 52228
  177.4 516.1 %copy-start.44 = (f32[4352]{0:T(1024)}, f32[4352]{0:T(1024)S(1)}, u32[]{:S(2)}) copy-start(f32[4352]{0:T(1024)S(1)} %get-tuple-element.980) | copy-start | bytes 52228
  177.4 516.1 %copy-start.46 = (f32[4352]{0:T(1024)}, f32[4352]{0:T(1024)S(1)}, u32[]{:S(2)}) copy-start(f32[4352]{0:T(1024)S(1)} %get-tuple-element.981) | copy-start | bytes 52228
  177.4 516.1 %copy-start.48 = (f32[4352]{0:T(1024)}, f32[4352]{0:T(1024)S(1)}, u32[]{:S(2)}) copy-start(f32[4352]{0:T(1024)S(1)} %get-tuple-element.982) | copy-start | bytes 52228
  181.4 504.6 %copy-start.23 = (f32[512,256]{1,0:T(8,128)}, f32[512,256]{1,0:T(8,128)S(1)}, u32[]{:S(2)}) copy-start(f32[512,256]{1,0:T(8,128)S(1)} %fusion.188) | copy-start | bytes 1572868
  258.0 1256.7 %reduce-scatter.16.cloned.1.call-start = ((), (), s32[]{:S(2)}) async-start(), calls=%async_computation.14 | async-start | bytes 393216 | tf_op jit(solution)/shard_map/reduce_scatter | solution.py:219
  911.1 114.9 %copy-start.67 = (f32[512]{0:T(512)}, f32[512]{0:T(512)S(1)}, u32[]{:S(2)}) copy-start(f32[512]{0:T(512)S(1)} %add_rsqrt_fusion) | copy-start | bytes 6148
  1082.2 248.0 %copy-start.37 = (f32[2048]{0:T(1024)S(1)}, f32[2048]{0:T(1024)}, u32[]{:S(2)}) copy-start(f32[2048]{0:T(1024)} %param.25) | copy-start | bytes 24580
  1082.2 248.0 %copy-start.53 = (f32[512]{0:T(512)S(1)}, f32[512]{0:T(512)}, u32[]{:S(2)}) copy-start(f32[512]{0:T(512)} %copy-done.52) | copy-start | bytes 6148
  1333.3 184.2 %reduce-scatter.20.cloned.1.call-start = ((), (), s32[]{:S(2)}) async-start(), calls=%async_computation.17 | async-start | bytes 1114112 | tf_op jit(solution)/shard_map/reduce_scatter | solution.py:231
  1459.0 249.0 %reduce-scatter.18.cloned.1.call-start = ((), (), s32[]{:S(2)}) async-start(), calls=%async_computation.15 | async-start | bytes 25165824 | tf_op jit(solution)/shard_map/reduce_scatter | solution.py:222
  1474.6 604.7 %reduce-scatter.12.cloned.1.call-start = ((), (), s32[]{:S(2)}) async-start(), calls=%async_computation.12 | async-start | bytes 50331648 | tf_op jit(solution)/shard_map/reduce_scatter | solution.py:216
  1514.6 663.0 %reduce-scatter.22.cloned.1.call-start = ((), (), s32[]{:S(2)}) async-start(), calls=%async_computation.19 | async-start | bytes 557056
  1516.6 662.4 %all-reduce.21.cloned.1.call-start = ((), (), s32[]{:S(2)}) async-start(), calls=%async_computation.18 | async-start | bytes 131072 | tf_op jit(solution)/shard_map/psum | solution.py:226
  1517.5 752.7 %reduce-scatter.24.cloned.1.call-start = ((), (), s32[]{:S(2)}) async-start(), calls=%async_computation.20 | async-start | bytes 8912896
  1720.4 732.3 %reduce-scatter.14.cloned.1.call-start = ((), (), s32[]{:S(2)}) async-start(), calls=%async_computation.13 | async-start | bytes 17825792 | tf_op jit(solution)/shard_map/reduce_scatter | solution.py:228
  2079.4 496.2 %all-reduce.19.cloned.1.call-start = ((), (), s32[]{:S(2)}) async-start(), calls=%async_computation.16 | async-start | bytes 139264 | tf_op jit(solution)/shard_map/psum | solution.py:242
  (103 other events, 1674.3 us)
Sparse Core Ops, SparseCore 0:
  10.8 129.6 all-gather.5
  142.6 36.1 all-gather.9
  180.9 77.0 all-gather.11
  259.4 386.7 all-gather.7
  647.5 198.8 all-gather.13
  1333.4 12.6 reduce-scatter.15
  1459.1 58.3 reduce-scatter.19
  1519.8 188.1 reduce-scatter.17
  1710.4 368.8 reduce-scatter.11
  2083.7 55.7 reduce-scatter.21
  2141.8 19.8 all-reduce.20
  2165.5 104.6 reduce-scatter.23
  2274.4 178.2 reduce-scatter.13
  2458.7 116.8 all-reduce.18
where the time goes:
time: 2590 us; the launch traced here: 2580 us
  waiting for transfers between devices  1540 us (59%)
  matrix products  435 us (17%)
  local copies, waits for them, and re-layouts  286 us (11%)
  other arithmetic  233 us (9%)
  blocking collectives  66 us (3%)
    all_gather x1, waiting for transfers between devices, per_device(): lax.all_gather(rows_zx, 'fsdp', axis=2, tiled=True)  388 us
    reduce_scatter x1, waiting for transfers between devices, per_device(): lax.psum_scatter(g_w_zx.astype(jnp.bfloat16), 'fsdp', scatter_dimension=2...  359 us
    reduce_scatter x1, waiting for transfers between devices, per_device(): lax.psum_scatter(g_w_out.astype(jnp.bfloat16), 'fsdp', scatter_dimension=...  190 us
    dot_general x8, matrix products, block_step(): jnp.einsum('hts,hsp->htp', mixing, x_heads, precision=lax.Precision.HIGHEST)  184 us
    reduce_scatter x1, waiting for transfers between devices, per_device(): lax.psum_scatter(g_zx.astype(jnp.bfloat16), 'dp', scatter_dimension=0, ti...  180 us
    all_gather x1, waiting for transfers between devices, per_device(): lax.all_gather(w_zx, 'dp', axis=0, tiled=True)  129 us
    psum x1, waiting for transfers between devices, per_device(): lax.psum((d_norm_gain,) + param_sums + (g_gate_local,), ('dp', 'fsdp'))  119 us
    unnamed x16, waiting for transfers between devices  91.3 us
  transfers between devices with their start and end apart: 14, of which 10 were waited for; matrix products, arithmetic and copies ran while one was open for 24% of the time, Pallas kernels for 0%

commit v1 on v0

v1 whole, which is shorter than its diff:
```python
import functools

import jax
import jax.numpy as jnp
from jax import lax
from jax.experimental import pallas as pl
from jax.experimental.pallas import tpu as pltpu
from jax.sharding import PartitionSpec as P

HEADS = 64
HEAD_DIM = 64
STRETCH = 256
LANES = 128
F32 = jnp.float32
BF16 = jnp.bfloat16
NEG = -1e30
HIGH = lax.Precision.HIGHEST


def dot_nn(a, b):
    return lax.dot_general(a, b, (((1,), (0,)), ((), ())), preferred_element_type=F32)


def dot_nt(a, b):
    return lax.dot_general(a, b, (((1,), (1,)), ((), ())), preferred_element_type=F32)


def dot_tn(a, b):
    return lax.dot_general(a, b, (((0,), (0,)), ((), ())), preferred_element_type=F32)


class Grid:
    def __init__(self):
        self.dp = lax.axis_size("dp")
        self.n = lax.axis_size("fsdp")
        chips = self.dp // 2
        self.zs = 4 if chips % 4 == 0 else 1
        self.ys = chips // self.zs
        index = lax.axis_index("dp")
        self.core = index % 2
        self.chip = index // 2
        self.z = self.chip // self.ys
        self.y = self.chip % self.ys
        self.j = lax.axis_index("fsdp")
        self.slots = self.zs * self.ys

    def _dp(self, value, move):
        pairs = []
        for i in range(self.dp):
            z, y, c = i // (2 * self.ys), (i // 2) % self.ys, i % 2
            z, y, c = move(z, y, c)
            pairs.append((i, (z * self.ys + y) * 2 + c))
        return lax.ppermute(value, "dp", pairs)

    def swap_core(self, value):
        return self._dp(value, lambda z, y, c: (z, y, 1 - c))

    def send_z(self, value, s):
        return self._dp(value, lambda z, y, c: ((z + s) % self.zs, y, c))

    def send_y(self, value, f):
        return self._dp(value, lambda z, y, c: (z, (y + f) % self.ys, c))

    def send_x(self, value, g):
        pairs = [(i, (i + g) % self.n) for i in range(self.n)]
        return lax.ppermute(value, "fsdp", pairs)

    def slot_chip(self, k):
        f, s = k // self.zs, k % self.zs
        return ((self.z - s) % self.zs) * self.ys + (self.y - f) % self.ys

    def chip_slot(self, b):
        return ((self.y - b % self.ys) % self.ys) * self.zs + (self.z - b // self.ys) % self.zs

    def gather(self, block):
        column = [block] + [self.send_z(block, s) for s in range(1, self.zs)]
        pieces = list(column)
        for f in range(1, self.ys):
            pieces += [self.send_y(piece, f) for piece in column]
        return pieces

    def scatter(self, pieces):
        total = None
        for s in list(range(1, self.zs)) + [0]:
            part = pieces[s].astype(F32)
            for f in range(1, self.ys):
                part = part + self.send_y(pieces[f * self.zs + s], -f).astype(F32)
            if s:
                part = self.send_z(part.astype(BF16), -s).astype(F32)
            total = part if total is None else total + part
        return total


def to_slots(grid, value, axis):
    size = value.shape[axis] // grid.slots
    return jnp.concatenate(
        [
            lax.dynamic_slice_in_dim(value, grid.slot_chip(k) * size, size, axis)
            for k in range(grid.slots)
        ],
        axis=axis,
    )


def from_slots(grid, value, axis):
    size = value.shape[axis] // grid.slots
    return jnp.concatenate(
        [
            lax.dynamic_slice_in_dim(value, grid.chip_slot(b) * size, size, axis)
            for b in range(grid.slots)
        ],
        axis=axis,
    )


def shift_down(value, by):
    if by == 0:
        return value
    rows = lax.broadcasted_iota(jnp.int32, value.shape, 0)
    return jnp.where(rows < by, 0.0, pltpu.roll(value, by, 0))


def shift_up(value, by):
    if by == 0:
        return value
    size = value.shape[0]
    rows = lax.broadcasted_iota(jnp.int32, value.shape, 0)
    return jnp.where(rows >= size - by, 0.0, pltpu.roll(value, size - by, 0))


def convolve(joined, taps, lanes):
    shifted = [shift_down(joined, 3 - k) for k in range(4)]
    total = taps[4:5, lanes]
    for k in range(4):
        total = total + taps[k : k + 1, lanes] * shifted[k]
    return shifted, total


def head_tables(dtr, heads):
    x = dtr + heads[0:1, :]
    dt = jnp.maximum(x, 0.0) + jnp.log1p(jnp.exp(-jnp.abs(x)))
    small = x < -30.0
    log_dt = jnp.where(small, x, jnp.log(dt))
    ratio = jnp.where(small, 1.0, jax.nn.sigmoid(x) / dt)
    rate = -dt * jnp.exp(heads[1:2, :])
    return log_dt, rate, ratio


def triangle(upper):
    rows = lax.broadcasted_iota(jnp.int32, (STRETCH, STRETCH), 0)
    cols = lax.broadcasted_iota(jnp.int32, (STRETCH, STRETCH), 1)
    return jnp.where(cols >= rows if upper else cols <= rows, 1.0, 0.0).astype(F32)


def dot_high(a, b):
    return jnp.dot(a, b, precision=HIGH, preferred_element_type=F32)


def pair_lanes(low, high, width=LANES):
    lane = lax.broadcasted_iota(jnp.int32, (low.shape[0], width), 1)
    return jnp.where(lane < HEAD_DIM, low, high)


def only(value, e):
    lane = lax.broadcasted_iota(jnp.int32, value.shape, 1)
    keep = (lane < HEAD_DIM) if e == 0 else (lane >= HEAD_DIM)
    return jnp.where(keep, value, jnp.zeros_like(value))


def fwd_kernel(limit_ref, xb_ref, taps_ref, heads_ref, skip_ref, y_ref, s1_ref, cm_ref):
    inner = y_ref.shape[1]
    q = pl.program_id(0)
    limit = limit_ref[q]
    half = STRETCH // 2
    lo, hi = slice(0, STRETCH), slice(STRETCH, 2 * STRETCH)
    bc = slice(inner, inner + 2 * LANES)
    _, conv = convolve(xb_ref[:, bc], taps_ref, bc)
    act = jax.nn.silu(conv).astype(BF16)
    bm, cm = act[:, :LANES], act[:, LANES:]
    log_dt, rate, _ = head_tables(xb_ref[:, inner + 2 * LANES :], heads_ref)
    tri = triangle(False)
    cum = jnp.concatenate([dot_high(tri, rate[lo]), dot_high(tri, rate[hi])], 0)
    late = cum - log_dt
    late_t = late.T
    tail = jnp.exp(cum[STRETCH - 1 : STRETCH] - late[lo])
    ecum = jnp.exp(cum[hi])
    grams = [dot_nt(cm[b], bm[b]) for b in (lo, hi)]
    mask = lax.broadcasted_iota(jnp.int32, (half, half), 0) >= lax.broadcasted_iota(
        jnp.int32, (half, half), 1
    )
    for p in range(inner // LANES):
        lanes = slice(p * LANES, (p + 1) * LANES)
        _, conv = convolve(xb_ref[:, lanes], taps_ref, lanes)
        channel = lax.broadcasted_iota(jnp.int32, (1, LANES), 1) + p * LANES
        xs = (jax.nn.silu(conv) * (channel < limit).astype(F32)).astype(BF16)
        h = 2 * p
        weights = pair_lanes(tail[:, h : h + 1], tail[:, h + 1 : h + 2])
        weighted = (xs[lo].astype(F32) * weights).astype(BF16)
        state = dot_tn(weighted, bm[lo]).astype(BF16)
        s1_ref[lanes, :] = state
        for b, gram in zip((lo, hi), grams):
            tops, lows = [], []
            xe = [only(xs[b], e) for e in (0, 1)]
            base = b.start
            for e in (0, 1):
                col = cum[b, h + e : h + e + 1]
                row = late_t[h + e : h + e + 1, b]
                top = jnp.exp(jnp.where(mask, col[:half] - row[:, :half], NEG))
                low0 = jnp.exp(col[half:] - row[:, :half])
                low1 = jnp.exp(jnp.where(mask, col[half:] - row[:, half:], NEG))
                tops.append((gram[:half, :half] * top).astype(BF16))
                lows.append((gram[half:, :half] * low0).astype(BF16))
                lows.append((gram[half:, half:] * low1).astype(BF16))
            y0 = dot_nn(
                jnp.concatenate(tops, 1), jnp.concatenate([xe[0][:half], xe[1][:half]], 0)
            )
            y1 = dot_nn(jnp.concatenate(lows, 1), jnp.concatenate(xe, 0))
            if base:
                inter = dot_nt(cm[b], state)
                inter = inter * pair_lanes(ecum[:, h : h + 1], ecum[:, h + 1 : h + 2])
                y0, y1 = y0 + inter[:half], y1 + inter[half:]
            skip = skip_ref[0:1, lanes] * xs[b].astype(F32)
            y_ref[pl.ds(base, half), lanes] = y0 + skip[:half]
            y_ref[pl.ds(base + half, half), lanes] = y1 + skip[half:]


def lane_sum(value, e):
    return jnp.sum(only(value, e), axis=1, keepdims=True)


def bwd_kernel(
    limit_ref,
    xb_ref,
    y_ref,
    dy_ref,
    s1_ref,
    taps_ref,
    heads_ref,
    skip_ref,
    dxb_ref,
    gch_ref,
    gh_ref,
    dg_ref,
    rs_ref,
):
    inner = y_ref.shape[1]
    q = pl.program_id(0)
    limit = limit_ref[q]
    half = STRETCH // 2
    lo, hi = slice(0, STRETCH), slice(STRETCH, 2 * STRETCH)
    bc = slice(inner, inner + 2 * LANES)

    @pl.when(q == 0)
    def _():
        gch_ref[...] = jnp.zeros_like(gch_ref)
        gh_ref[...] = jnp.zeros_like(gh_ref)

    dg_ref[...] = jnp.zeros_like(dg_ref)
    rs_ref[...] = jnp.zeros_like(rs_ref)
    shifted_bc, conv_bc = convolve(xb_ref[:, bc], taps_ref, bc)
    sig_bc = jax.nn.sigmoid(conv_bc)
    act = (conv_bc * sig_bc).astype(BF16)
    bm, cm = act[:, :LANES], act[:, LANES:]
    log_dt, rate, ratio = head_tables(xb_ref[:, inner + 2 * LANES :], heads_ref)
    tri = triangle(False)
    cum = jnp.concatenate([dot_high(tri, rate[lo]), dot_high(tri, rate[hi])], 0)
    late = cum - log_dt
    cum_t = cum.T
    tail = jnp.exp(cum[STRETCH - 1 : STRETCH] - late[lo])
    ecum = jnp.exp(cum[hi])
    grams = [dot_nt(bm[b], cm[b]) for b in (lo, hi)]
    mask = lax.broadcasted_iota(jnp.int32, (half, half), 1) >= lax.broadcasted_iota(
        jnp.int32, (half, half), 0
    )
    d_bm0 = jnp.zeros((STRETCH, LANES), F32)
    d_cm1 = jnp.zeros((STRETCH, LANES), F32)
    d_tail = jnp.zeros((1, LANES), F32)
    lane_of = lax.broadcasted_iota(jnp.int32, (1, LANES), 1)

    def conv_back(d_act, conv, sig, shifted, lanes):
        d_conv = d_act * (sig * (1.0 + conv * (1.0 - sig)))
        rows = [jnp.sum(d_conv * part, axis=0, keepdims=True) for part in shifted]
        rows.append(jnp.sum(d_conv, axis=0, keepdims=True))
        total = None
        for k in range(4):
            part = taps_ref[k : k + 1, lanes] * shift_up(d_conv, 3 - k)
            total = part if total is None else total + part
        dxb_ref[:, lanes] = total.astype(BF16)
        return rows

    for p in range(inner // LANES):
        lanes = slice(p * LANES, (p + 1) * LANES)
        h = 2 * p
        shifted, conv = convolve(xb_ref[:, lanes], taps_ref, lanes)
        sig = jax.nn.sigmoid(conv)
        channel = lane_of + p * LANES
        used = (channel < limit).astype(F32)
        xs = (conv * sig * used).astype(BF16)
        xf = xs.astype(F32)
        dy = dy_ref[:, lanes]
        dyf = dy.astype(F32)
        skip = skip_ref[0:1, lanes]
        d_prior = (dyf[hi] * pair_lanes(ecum[:, h : h + 1], ecum[:, h + 1 : h + 2])).astype(BF16)
        d_state = dot_tn(d_prior, cm[hi]).astype(BF16)
        weights = pair_lanes(tail[:, h : h + 1], tail[:, h + 1 : h + 2])
        weighted = (xf[lo] * weights).astype(BF16)
        d_from_state = dot_nt(bm[lo], d_state) * weights
        d_bm0 = d_bm0 + dot_nn(weighted, d_state)
        d_cm1 = d_cm1 + dot_nn(d_prior, s1_ref[lanes, :])
        columns = []
        for i, (b, gram) in enumerate(zip((lo, hi), grams)):
            tops, lows = [], []
            dye = [only(dy[b], e) for e in (0, 1)]
            for e in (0, 1):
                col = late[b, h + e : h + e + 1]
                row = cum_t[h + e : h + e + 1, b]
                top0 = jnp.exp(jnp.where(mask, row[:, :half] - col[:half], NEG))
                top1 = jnp.exp(row[:, half:] - col[:half])
                low = jnp.exp(jnp.where(mask, row[:, half:] - col[half:], NEG))
                xe = only(xs[b], e)
                d_top = dot_nt(xe[:half], dy[b])
                d_low = dot_nt(xe[half:], dy[b][half:])
                tops.append((gram[:half, :half] * top0).astype(BF16))
                tops.append((gram[:half, half:] * top1).astype(BF16))
                lows.append((gram[half:, half:] * low).astype(BF16))
                dg_ref[i, :half, :half] += d_top[:, :half] * top0
                dg_ref[i, :half, half:] += d_top[:, half:] * top1
                dg_ref[i, half:, half:] += d_low * low
            d0 = dot_nn(jnp.concatenate(tops, 1), jnp.concatenate(dye, 0))
            d1 = dot_nn(
                jnp.concatenate(lows, 1), jnp.concatenate([dye[0][half:], dye[1][half:]], 0)
            )
            columns += [d0, d1]
        d_x = jnp.concatenate(columns, 0)
        d_x = jnp.concatenate([d_x[lo] + d_from_state, d_x[hi]], 0)
        from_x = xf * d_x
        from_y = dyf * (y_ref[:, lanes] - skip * xf)
        state_sum = jnp.sum(xf[lo] * d_from_state, axis=0, keepdims=True)
        for e in (0, 1):
            here = lane_of == h + e
            rs_ref[0] = jnp.where(here, lane_sum(from_x, e), rs_ref[0])
            rs_ref[1] = jnp.where(here, lane_sum(from_y, e), rs_ref[1])
            d_tail = jnp.where(here, lane_sum(state_sum, e), d_tail)
        d_act = (d_x + skip * dyf) * used
        rows = conv_back(d_act, conv, sig, shifted, lanes)
        rows.append(jnp.sum(dyf * xf, axis=0, keepdims=True))
        for r, row in enumerate(rows):
            gch_ref[r : r + 1, lanes] += row

    d_bm, d_cm = [], []
    for i, b in enumerate((lo, hi)):
        d_gram = dg_ref[i].astype(BF16)
        d_bm.append(dot_nn(d_gram, cm[b]))
        d_cm.append(dot_tn(d_gram, bm[b]))
    d_bm[0] = d_bm[0] + d_bm0
    d_cm[1] = d_cm[1] + d_cm1
    d_act = jnp.concatenate([jnp.concatenate(d_bm, 0), jnp.concatenate(d_cm, 0)], 1)
    rows = conv_back(d_act, conv_bc, sig_bc, shifted_bc, bc)
    for r, row in enumerate(rows):
        gch_ref[r : r + 1, bc] += row

    from_x, from_y = rs_ref[0], rs_ref[1]
    d_cum = from_y - from_x
    row_of = lax.broadcasted_iota(jnp.int32, (STRETCH, 1), 0)
    first = d_cum[lo] + jnp.where(row_of == STRETCH - 1, d_tail, 0.0)
    tri_t = triangle(True)
    d_rate = jnp.concatenate([dot_high(tri_t, first), dot_high(tri_t, d_cum[hi])], 0)
    flow = rate * d_rate
    d_dt = (from_x + flow) * ratio
    dxb_ref[:, inner + 2 * LANES :] = d_dt.astype(BF16)
    gh_ref[0:1, :] += jnp.sum(d_dt, axis=0, keepdims=True)
    gh_ref[1:2, :] += jnp.sum(flow, axis=0, keepdims=True)


def run_fwd(limits, xb, taps, heads, skip, slot):
    rows, cols = xb.shape
    inner = cols - 3 * LANES
    seqs = rows // slot
    whole = lambda shape: pl.BlockSpec(shape, lambda q, *_: (0,) * len(shape))
    per = lambda width: pl.BlockSpec((slot, width), lambda q, *_: (q, 0))
    return pl.pallas_call(
        fwd_kernel,
        grid_spec=pltpu.PrefetchScalarGridSpec(
            num_scalar_prefetch=1,
            grid=(seqs,),
            in_specs=[per(cols), whole(taps.shape), whole(heads.shape), whole(skip.shape)],
            out_specs=[
                per(inner),
                pl.BlockSpec((inner, LANES), lambda q, *_: (q, 0)),
            ],
            scratch_shapes=[pltpu.VMEM((8, LANES), F32)],
        ),
        out_shape=[
            jax.ShapeDtypeStruct((rows, inner), F32),
            jax.ShapeDtypeStruct((seqs * inner, LANES), BF16),
        ],
        name="scan_forward",
    )(limits, xb, taps, heads, skip)


def run_bwd(limits, xb, y, dy, s1, taps, heads, skip, slot):
    rows, cols = xb.shape
    inner = cols - 3 * LANES
    seqs = rows // slot
    whole = lambda shape: pl.BlockSpec(shape, lambda q, *_: (0,) * len(shape))
    per = lambda width: pl.BlockSpec((slot, width), lambda q, *_: (q, 0))
    return pl.pallas_call(
        bwd_kernel,
        grid_spec=pltpu.PrefetchScalarGridSpec(
            num_scalar_prefetch=1,
            grid=(seqs,),
            in_specs=[
                per(cols),
                per(inner),
                per(inner),
                pl.BlockSpec((inner, LANES), lambda q, *_: (q, 0)),
                whole(taps.shape),
                whole(heads.shape),
                whole(skip.shape),
            ],
            out_specs=[per(cols), whole((8, cols)), whole((8, LANES))],
            scratch_shapes=[
                pltpu.VMEM((2, STRETCH, STRETCH), F32),
                pltpu.VMEM((2, 2 * STRETCH, LANES), F32),
            ],
        ),
        out_shape=[
            jax.ShapeDtypeStruct((rows, cols), BF16),
            jax.ShapeDtypeStruct((8, cols), F32),
            jax.ShapeDtypeStruct((8, LANES), F32),
        ],
        name="scan_backward",
    )(limits, xb, y, dy, s1, taps, heads, skip)


def per_device(
    tokens,
    cotangent,
    lengths,
    widths,
    norm_gain,
    w_zx,
    w_bc,
    w_dt,
    w_out,
    conv_w,
    conv_b,
    dt_bias,
    a_log,
    d_skip,
    gate_gain,
):
    grid = Grid()
    core, j, n = grid.core, grid.j, grid.n
    slot, width = tokens.shape
    assert lengths.shape[0] == 1 and slot == 2 * STRETCH
    rows_d = w_zx.shape[0]
    inner = w_zx.shape[2] // 2
    heads = w_dt.shape[1] // 2
    state2 = w_bc.shape[1]
    total = conv_w.shape[1]
    all_inner = total - state2
    part = j * 2 + core
    channel_base = part * inner
    head_base = part * heads
    cols = inner + 3 * LANES
    sent = inner + state2 + heads

    def halves(value, axis):
        size = value.shape[axis] // 2
        mine = lax.dynamic_slice_in_dim(value, core * size, size, axis)
        other = lax.dynamic_slice_in_dim(value, (1 - core) * size, size, axis)
        return mine, other

    def by_core(mine, other, axis):
        first = jnp.where(core == 0, mine, other)
        second = jnp.where(core == 0, other, mine)
        return jnp.concatenate([first, second], axis=axis)

    z_mine, z_other = halves(w_zx[:, 0], 1)
    x_mine, x_other = halves(w_zx[:, 1], 1)
    t_mine, t_other = halves(w_dt, 1)
    o_mine, o_other = halves(w_out.T, 1)
    x_mine = jnp.concatenate([x_mine, w_bc, t_mine], axis=1)
    x_other = jnp.concatenate([x_other, w_bc, t_other], axis=1)
    block_o = by_core(o_mine, grid.swap_core(o_other), 0)
    block_x = by_core(x_mine, grid.swap_core(x_other), 0)
    block_z = by_core(z_mine, grid.swap_core(z_other), 0)
    w_o = jnp.concatenate(grid.gather(block_o), axis=0)
    w_x = jnp.concatenate(grid.gather(block_x), axis=0)
    w_z = jnp.concatenate(grid.gather(block_z), axis=0)
    w_x = jnp.pad(w_x, ((0, 0), (0, cols - sent)))

    u = to_slots(grid, tokens, 1).astype(F32)
    cot = to_slots(grid, cotangent, 1)
    gain = to_slots(grid, norm_gain, 0)
    rstd = lax.rsqrt(jnp.mean(u * u, axis=-1, keepdims=True) + 1e-05)
    normed_own = (u * rstd * gain).astype(BF16)
    valid = (jnp.arange(slot) < lengths[0])[:, None]
    d_branch_own = jnp.where(valid, cot, jnp.zeros_like(cot))

    def share(value):
        near = [value] + [grid.send_x(value, g) for g in range(1, n)]
        pieces = []
        for piece in near:
            pieces += [piece, grid.swap_core(piece)]
        return jnp.concatenate(pieces, axis=0)

    def collect(value):
        value = value.reshape(n, 2, slot, width)
        here = value[:, 0].astype(F32) + grid.swap_core(value[:, 1]).astype(F32)
        out = here[0]
        for g in range(1, n):
            out = out + grid.send_x(here[g].astype(BF16), -g).astype(F32)
        return out

    normed = share(normed_own)
    d_branch = share(d_branch_own)
    index = lax.axis_index("dp")
    owners = []
    for g in range(n):
        for e in (0, 1):
            owners.append((index + e * (1 - 2 * core)) * n + (j - g) % n)
    seqs = len(owners)
    seq_width = jnp.stack([widths[o] for o in owners])
    used = seq_width * ((HEADS // 8) * HEAD_DIM)
    counts = jnp.repeat(used.astype(F32), slot)
    limits = jnp.clip(used - channel_base, 0, inner).astype(jnp.int32)

    taps = jnp.concatenate(
        [
            lax.dynamic_slice_in_dim(conv_w, channel_base, inner, 1),
            conv_w[:, all_inner:],
        ],
        axis=1,
    )
    bias = jnp.concatenate(
        [lax.dynamic_slice_in_dim(conv_b, channel_base, inner, 0), conv_b[all_inner:]]
    )
    taps = jnp.pad(jnp.concatenate([taps, bias[None]], 0), ((0, 3), (0, LANES)))
    own_heads = lambda v: lax.dynamic_slice_in_dim(v, head_base, heads, 0)
    head_rows = jnp.pad(
        jnp.stack([own_heads(dt_bias), own_heads(a_log)]), ((0, 6), (0, LANES - heads))
    )
    skip = jnp.broadcast_to(jnp.repeat(own_heads(d_skip), HEAD_DIM)[None], (8, inner))
    own_gain = lax.dynamic_slice_in_dim(gate_gain, channel_base, inner, 0)

    d_gnorm = dot_nn(d_branch, w_o)
    xb = dot_nn(normed, w_x)
    y, s1 = run_fwd(limits, xb, taps, head_rows, skip, slot)
    z = dot_nn(normed, w_z)
    sig = jax.nn.sigmoid(z)
    gated = y * (z * sig)
    weighted = d_gnorm * own_gain
    stats = jnp.stack([jnp.sum(gated * gated, axis=1), jnp.sum(weighted * gated, axis=1)])
    stats = stats.reshape(2, n, 2, slot)
    stats = stats + grid.swap_core(stats)[:, :, ::-1]
    whole = stats
    for g in range(1, n):
        whole = whole + jnp.roll(grid.send_x(stats, g), g, axis=1)
    stats = whole.reshape(2, seqs * slot)
    scale = lax.rsqrt(stats[0] / counts + 1e-05)
    pull = scale * scale * scale / counts * stats[1]
    gnorm = (gated * scale[:, None] * own_gain).astype(BF16)
    d_gated = weighted * scale[:, None] - gated * pull[:, None]
    g_gate = jnp.sum(d_gnorm * gated * scale[:, None], axis=0)
    silu = z * sig
    d_y = (d_gated * silu).astype(BF16)
    d_z = (d_gated * y * (sig * (1.0 + z * (1.0 - sig)))).astype(BF16)

    def reduce(grad):
        return grid.scatter(jnp.split(grad.astype(BF16), grid.slots, axis=0))

    g_o = reduce(dot_tn(d_branch, gnorm))
    g_z = reduce(dot_tn(normed, d_z))
    branch = collect(dot_nt(gnorm, w_o).astype(BF16))
    d_xb, g_channels, g_heads = run_bwd(limits, xb, y, d_y, s1, taps, head_rows, skip, slot)
    g_x = reduce(dot_tn(normed, d_xb)[:, :sent])
    d_normed_part = dot_nt(d_z, w_z) + dot_nt(d_xb, w_x)
    g_norm_part = jnp.sum(d_normed_part * normed.astype(F32), axis=0) / gain
    d_normed = collect(d_normed_part.astype(BF16))

    output = (u + jnp.where(valid, branch, 0.0)).astype(BF16)
    d_scaled = d_normed * gain
    back = jnp.mean(d_scaled * u, axis=-1, keepdims=True)
    d_u = d_scaled * rstd - u * (rstd * rstd * rstd * back)
    input_grad = (cot.astype(F32) + d_u).astype(BF16)
    output = from_slots(grid, output, 1)
    input_grad = from_slots(grid, input_grad, 1)

    def to_rows(value):
        mine = lax.dynamic_slice_in_dim(value, core * rows_d, rows_d, 0)
        other = lax.dynamic_slice_in_dim(value, (1 - core) * rows_d, rows_d, 0)
        return mine, grid.swap_core(other)

    z_rows = by_core(*to_rows(g_z), 1)
    o_rows = by_core(*to_rows(g_o), 1)
    x_mine, x_recv = to_rows(g_x)
    x_rows = by_core(x_mine[:, :inner], x_recv[:, :inner], 1)
    t_rows = by_core(x_mine[:, inner + state2 :], x_recv[:, inner + state2 :], 1)
    bc_rows = (x_mine + x_recv)[:, inner : inner + state2]
    bc_sum = bc_rows
    for g in range(1, n):
        bc_sum = bc_sum + grid.send_x(bc_rows, g)
    g_w_zx = jnp.stack([z_rows, x_rows], axis=1)

    conv_rows = jnp.zeros((5, total), F32)
    conv_rows = lax.dynamic_update_slice(conv_rows, g_channels[:5, :inner], (0, channel_base))
    conv_rows = lax.dynamic_update_slice(
        conv_rows, g_channels[:5, inner : inner + state2], (0, all_inner)
    )
    gate_row = lax.dynamic_update_slice(jnp.zeros((all_inner,), F32), g_gate, (channel_base,))
    g_skip = g_channels[5, :inner].reshape(heads, HEAD_DIM).sum(axis=1)
    head_parts = jnp.stack([g_heads[0, :heads], g_heads[1, :heads], g_skip])
    head_parts = lax.dynamic_update_slice(
        jnp.zeros((3, d_skip.shape[0]), F32), head_parts, (0, head_base)
    )
    flat = jnp.concatenate(
        [
            from_slots(grid, g_norm_part, 0),
            conv_rows.reshape(-1),
            gate_row,
            head_parts.reshape(-1),
        ]
    )
    size = flat.shape[0]
    flat = jnp.pad(flat, (0, -size % 1024)).reshape(-1, LANES)
    flat = lax.psum(flat, ("dp", "fsdp")).reshape(-1)[:size]
    ends = [width, width + 5 * total, width + 5 * total + all_inner]
    g_norm, g_conv, g_gate, g_small = jnp.split(flat, ends)
    g_conv = g_conv.reshape(5, total)
    g_small = g_small.reshape(3, -1)
    return (
        output,
        input_grad,
        g_norm,
        g_w_zx,
        bc_sum,
        t_rows,
        o_rows.T,
        g_conv[:4],
        g_conv[4],
        g_small[0],
        g_small[1],
        g_small[2],
        g_gate,
    )


def solution(mesh):
    in_specs = (
        P(("dp", "fsdp"), None),
        P(("dp", "fsdp"), None),
        P(("dp", "fsdp")),
        P(),
        P(),
        P("dp", None, "fsdp"),
        P("dp", None),
        P("dp", "fsdp"),
        P("fsdp", "dp"),
        P(),
        P(),
        P(),
        P(),
        P(),
        P(),
    )
    out_specs = (
        P(("dp", "fsdp"), None),
        P(("dp", "fsdp"), None),
        P(),
        P("dp", None, "fsdp"),
        P("dp", None),
        P("dp", "fsdp"),
        P("fsdp", "dp"),
        P(),
        P(),
        P(),
        P(),
        P(),
        P(),
    )
    return jax.shard_map(
        per_device, mesh=mesh, in_specs=in_specs, out_specs=out_specs, check_vma=False
    )
```

time: 2590 us -> 1000 us (0.39)
  waiting for transfers between devices: 1540 us -> 392 us
  matrix products: 435 us -> 156 us
  local copies, waits for them, and re-layouts: 286 us -> 104 us
  starting transfers between devices: 0.74 us -> 170 us
  other arithmetic: 233 us -> 71.3 us
  Pallas kernels: 0 us -> 80.7 us
  blocking collectives: 66 us -> 0 us
    reduce_scatter x5 -> x0, waiting for transfers between devices: 730 us -> none  [the longest x1 359 us: per_device(): lax.psum_scatter(g_w_zx.astype(jnp.bfloat16), 'fsdp', scatter_dimension=2...]
    all_gather x5 -> x0, waiting for transfers between devices: 595 us -> none  [the longest x1 388 us: per_device(): lax.all_gather(rows_zx, 'fsdp', axis=2, tiled=True)]
    ppermute x0 -> x61, waiting for transfers between devices: none -> 296 us  [the longest x55 217 us: _dp(): return lax.ppermute(value, 'dp', pairs)]
    dot_general x48 -> x9, matrix products: 435 us -> 156 us  [the longest x3 60.3 us: dot_nn(): lax.dot_general(a, b, (((1,), (0,)), ((), ())), preferred_element_type=F32)]
    ppermute x0 -> x61, starting transfers between devices: none -> 170 us  [the longest x55 163 us: _dp(): return lax.ppermute(value, 'dp', pairs)]
    reshape x14 -> x3, local copies, waits for them, and re-layouts: 105 us -> 0.75 us  [the longest x1 0.65 us: per_device(): flat = jnp.pad(flat, (0, -size % 1024)).reshape(-1, LANES)]
    unnamed x16 -> x1, waiting for transfers between devices: 91.3 us -> 0.02 us
    pallas_call x0 -> x2, Pallas kernels: none -> 80.7 us  [the longest x1 55.7 us: run_bwd(): pl.pallas_call(bwd_kernel, grid_spec=pltpu.PrefetchScalarGridSpec(num_sca...]
  transfers between devices with their start and end apart: 14 -> 62, of which waited for: 10 -> 24; matrix products, arithmetic and copies ran while one was open for 24% -> 26% of each run, Pallas kernels for 0% -> 8%
where the time goes in v1:
time: 1000 us; the launch traced here: 990 us
  waiting for transfers between devices  392 us (39%)
  starting transfers between devices  170 us (17%)
  matrix products  156 us (16%)
  local copies, waits for them, and re-layouts  104 us (10%)
  Pallas kernels  80.7 us (8%)
  other arithmetic  71.3 us (7%)
  between operations  16.3 us (2%)
    ppermute x55, waiting for transfers between devices, _dp(): return lax.ppermute(value, 'dp', pairs)  217 us
    ppermute x55, starting transfers between devices, _dp(): return lax.ppermute(value, 'dp', pairs)  163 us
    psum x1, waiting for transfers between devices, per_device(): flat = lax.psum(flat, ('dp', 'fsdp')).reshape(-1)[:size]  96.2 us
    ppermute x6, waiting for transfers between devices, send_x(): return lax.ppermute(value, 'fsdp', pairs)  78.7 us
    dot_general x3, matrix products, dot_nn(): lax.dot_general(a, b, (((1,), (0,)), ((), ())), preferred_element_type=F32)  60.3 us
    pallas_call x1, Pallas kernels, run_bwd(): pl.pallas_call(bwd_kernel, grid_spec=pltpu.PrefetchScalarGridSpec(num_sca...  55.7 us
    unnamed x172, local copies, waits for them, and re-layouts  54.5 us
    dot_general x3, matrix products, dot_nt(): lax.dot_general(a, b, (((1,), (1,)), ((), ())), preferred_element_type=F32)  50 us
  transfers between devices with their start and end apart: 62, of which 24 were waited for; matrix products, arithmetic and copies ran while one was open for 26% of the time, Pallas kernels for 8%

profile of v1, /device:TPU:0, one launch (start us, length us, event | category | flops | bytes accessed | tf_op | source)
XLA Modules:
  0.0 990.1 jit_solution(17482263399240691385)
XLA Ops:
  79.0 20.9 %collective-permute-start.23 = (bf16[256,1024]{0,1:T(8,128)(2,1)}, bf16[256,1024]{0,1:T(8,128)(2,1)}, u32[]{:S(2)}, u32[]{:S(2)}) collective-permute-start(bf16[256,1024]{0,1:T(8,128)(2,1)} %pad_maximum_fusion.7), channel_id=1, source_target_pairs={{0,8},{2,10},{4,12},{6,14},{8,16},{10,18},{12,20},{14,22},{16,24},... | collective-permute-start | bytes 1572872 | tf_op jit(solution)/shard_map/ppermute | solution.py:53
  102.2 29.0 %collective-permute-start.25 = (bf16[256,1024]{0,1:T(8,128)(2,1)}, bf16[256,1024]{0,1:T(8,128)(2,1)}, u32[]{:S(2)}, u32[]{:S(2)}) collective-permute-start(bf16[256,1024]{0,1:T(8,128)(2,1)} %pad_maximum_fusion.7), channel_id=1, source_target_pairs={{0,24},{2,26},{4,28},{6,30},{8,0},{10,2},{12,4},{14,6},{16,8},{18,... | collective-permute-start | bytes 1572872 | tf_op jit(solution)/shard_map/ppermute | solution.py:53
  151.9 13.7 %collective-permute-done.25 = bf16[256,1024]{0,1:T(8,128)(2,1)} collective-permute-done((bf16[256,1024]{0,1:T(8,128)(2,1)}, bf16[256,1024]{0,1:T(8,128)(2,1)}, u32[]{:S(2)}, u32[]{:S(2)}) %collective-permute-start.25) | collective-permute-done | bytes 524320 | tf_op jit(solution)/shard_map/ppermute | solution.py:53
  178.2 21.5 %collective-permute-done.5 = bf16[256,1296]{0,1:T(8,128)(2,1)S(1)} collective-permute-done((bf16[256,1296]{0,1:T(8,128)(2,1)S(1)}, bf16[256,1296]{0,1:T(8,128)(2,1)S(1)}, u32[]{:S(2)}, u32[]{:S(2)}) %collective-permute-start.5) | collective-permute-done | bytes 663584 | tf_op jit(solution)/shard_map/ppermute | solution.py:53
  201.2 12.6 %collective-permute-done.6 = bf16[256,1296]{0,1:T(8,128)(2,1)S(1)} collective-permute-done((bf16[256,1296]{0,1:T(8,128)(2,1)S(1)}, bf16[256,1296]{0,1:T(8,128)(2,1)S(1)}, u32[]{:S(2)}, u32[]{:S(2)}) %collective-permute-start.6) | collective-permute-done | bytes 663584 | tf_op jit(solution)/shard_map/ppermute | solution.py:53
  291.0 13.2 %collective-permute-done.10 = bf16[256,1296]{0,1:T(8,128)(2,1)S(1)} collective-permute-done((bf16[256,1296]{0,1:T(8,128)(2,1)S(1)}, bf16[256,1296]{0,1:T(8,128)(2,1)S(1)}, u32[]{:S(2)}, u32[]{:S(2)}) %collective-permute-start.10) | collective-permute-done | bytes 663584 | tf_op jit(solution)/shard_map/ppermute | solution.py:53
  306.7 22.1 %fusion.3.xb_ref = f32[2048,1408]{1,0:T(8,128)} fusion(bf16[2048,1296]{0,1:T(8,128)(2,1)} %copy-done.31, bf16[512,2048]{1,0:T(8,128)(2,1)} %collective-permute-done.2, bf16[512,2048]{1,0:T(8,128)(2,1)} %collective-permute-done.1, bf16[512,2048]{1,0:T(8,128)(2,1)} %collective-permute-done, bf16[512,2048]{1,0:T(8,128)(2,1)} %fusion.7), kind=kOutput, calls=%fused_computation.24 | convolution fusion | flops 11844714496 | bytes 25231360 | tf_op jit(solution)/shard_map/dot_general | solution.py:21
  329.4 25.0 %scan_forward.1 = (f32[2048,1024]{1,0:T(8,128)}, bf16[4096,128]{1,0:T(8,128)(2,1)}) custom-call(s32[4]{0:T(128)} %subtract_clamp_fusion.limit_ref, f32[2048,1408]{1,0:T(8,128)} %fusion.3.xb_ref, f32[8,1408]{1,0:T(8,128)} %select_maximum_fusion.taps_ref, f32[8,128]{1,0:T(8,128)} %select_maximum_fusion.2.heads_ref, f32[8,1024]{1,0:T(8,128)} %broadcast_in_dim.61.skip_ref), custom_call_target="tpu_custom_call" | custom-call | tf_op jit(solution)/shard_map/scan_forward/pallas_call | solution.py:381
  354.5 16.7 %fusion.30 = f32[2048,1024]{1,0:T(8,128)} fusion(bf16[2048,1024]{0,1:T(8,128)(2,1)} %constant_dynamic-update-slice_fusion.10, bf16[512,2048]{1,0:T(8,128)(2,1)} %collective-permute-done.2, bf16[512,2048]{1,0:T(8,128)(2,1)} %collective-permute-done.1, bf16[512,2048]{1,0:T(8,128)(2,1)} %collective-permute-done, bf16[512,2048]{1,0:T(8,128)(2,1)} %fusion.7), kind=kOutput, calls=%fused_computation.221 | convolution fusion | flops 8623489024 | bytes 20971520 | tf_op jit(solution)/shard_map/dot_general | solution.py:21
  371.1 21.5 %multiply_reduce_fusion.2 = (f32[2048]{0:T(1024)S(1)}, f32[2048]{0:T(1024)S(1)}, f32[2048,1024]{1,0:T(8,128)}, f32[2048,1024]{1,0:T(8,128)}) fusion(f32[1024]{0:T(1024)S(1)} %dynamic_slice.269, f32[2048,1024]{1,0:T(8,128)} %get-tuple-element.18.y_ref, f32[2048,1024]{1,0:T(8,128)} %fusion.30, bf16[2048,1024]{0,1:T(8,128)(2,1)} %constant_dynamic-update-slice_fusion.19, ...), kind=kOutput, calls=%fused_computation.10 | convolution fusion | flops 8644456448 | bytes 46157824 | tf_op jit(solution)/shard_map/dot_general | solution.py:21
  398.1 14.6 %convolution_convert_fusion = bf16[2048,2048]{1,0:T(8,128)(2,1)} fusion(bf16[2048,1024]{0,1:T(8,128)(2,1)} %constant_dynamic-update-slice_fusion.19, f32[2048,1024]{1,0:T(8,128)} %get-tuple-element.66, f32[2048]{0:T(1024)S(1)} %get-tuple-element.123, f32[1024]{0:T(1024)S(1)} %dynamic_slice.269), kind=kOutput, calls=%fused_computation.19 | convolution fusion | flops 8600420352 | bytes 20983808 | tf_op jit(solution)/shard_map/dot_general | solution.py:25
  412.7 14.6 %convolution_convert_fusion.2 = bf16[2048,1024]{0,1:T(8,128)(2,1)S(1)} fusion(bf16[512,2048]{1,0:T(8,128)(2,1)} %collective-permute-done.21, bf16[512,2048]{1,0:T(8,128)(2,1)} %collective-permute-done.20, bf16[512,2048]{1,0:T(8,128)(2,1)} %collective-permute-done.19, bf16[512,2048]{1,0:T(8,128)(2,1)} %broadcast_select_fusion, ...), kind=kOutput, calls=%fused_computation.46 | convolution fusion | flops 8631877632 | bytes 20983808 | tf_op jit(solution)/shard_map/dot_general | solution.py:29
  432.9 16.2 %multiply_convert_fusion.1 = (bf16[2048,1024]{1,0:T(8,128)(2,1)}, bf16[2048,1024]{1,0:T(8,128)(2,1)}, f32[1024]{0:T(1024)S(1)}) fusion(f32[2048,1024]{1,0:T(8,128)} %fusion.30, f32[2048,1024]{1,0:T(8,128)} %get-tuple-element.18.y_ref, f32[2048,1024]{1,0:T(8,128)} %get-tuple-element.66, f32[2048]{0:T(1024)S(1)} %get-tuple-element.122, ...), kind=kLoop, calls=%fused_computation.7 | loop fusion | flops 41942016 | bytes 41967616 | tf_op jit(solution)/shard_map/convert_element_type | solution.py:569
  449.1 12.6 %convolution_convert_fusion.3 = bf16[2048,1024]{0,1:T(8,128)(2,1)S(1)} fusion(bf16[2048,1024]{1,0:T(8,128)(2,1)} %get-tuple-element.75, bf16[512,2048]{1,0:T(8,128)(2,1)} %collective-permute-done.2, bf16[512,2048]{1,0:T(8,128)(2,1)} %collective-permute-done.1, bf16[512,2048]{1,0:T(8,128)(2,1)} %collective-permute-done, bf16[512,2048]{1,0:T(8,128)(2,1)} %fusion.7), kind=kOutput, calls=%fused_computation.47 | convolution fusion | flops 8625586176 | bytes 16777216 | tf_op jit(solution)/shard_map/dot_general | solution.py:29
  466.6 55.7 %scan_backward.1 = (bf16[2048,1408]{1,0:T(8,128)(2,1)}, f32[8,1408]{1,0:T(8,128)}, f32[8,128]{1,0:T(8,128)}) custom-call(s32[4]{0:T(128)} %subtract_clamp_fusion.limit_ref, f32[2048,1408]{1,0:T(8,128)} %fusion.3.xb_ref, f32[2048,1024]{1,0:T(8,128)} %get-tuple-element.18.y_ref, bf16[2048,1024]{1,0:T(8,128)(2,1)} %get-tuple-element.76.dy_ref, ...), custom_call_target="tpu_custom_call" | custom-call | tf_op jit(solution)/shard_map/scan_backward/pallas_call | solution.py:407
  525.7 19.2 %fusion.1 = f32[2048,2048]{1,0:T(8,128)} fusion(bf16[2048,1408]{1,0:T(8,128)(2,1)} %get-tuple-element.20, bf16[2048,1296]{0,1:T(8,128)(2,1)} %copy-done.31), kind=kOutput, calls=%fused_computation.22 | convolution fusion | flops 11811160064 | bytes 27852800 | tf_op jit(solution)/shard_map/dot_general | solution.py:25
  545.0 16.2 %multiply_reduce_fusion = (f32[2048]{0:T(1024)S(1)}, bf16[2048,2048]{1,0:T(8,128)(2,1)}) fusion(bf16[512,2048]{1,0:T(8,128)(2,1)} %collective-permute-done.2, bf16[512,2048]{1,0:T(8,128)(2,1)} %collective-permute-done.1, bf16[512,2048]{1,0:T(8,128)(2,1)} %collective-permute-done, bf16[512,2048]{1,0:T(8,128)(2,1)} %fusion.7, f32[2048,2048]{1,0:T(8,128)} %fusion.1, ...), kind=kOutput, calls=%fused_computation | convolution fusion | flops 8640264192 | bytes 41951232 | tf_op jit(solution)/shard_map/dot_general | solution.py:25
  567.7 18.1 %convolution_convert_fusion.1 = bf16[2048,1408]{0,1:T(8,128)(2,1)} fusion(bf16[2048,1408]{1,0:T(8,128)(2,1)} %get-tuple-element.20, bf16[512,2048]{1,0:T(8,128)(2,1)} %collective-permute-done.2, bf16[512,2048]{1,0:T(8,128)(2,1)} %collective-permute-done.1, bf16[512,2048]{1,0:T(8,128)(2,1)} %collective-permute-done, bf16[512,2048]{1,0:T(8,128)(2,1)} %fusion.7), kind=kOutput, calls=%fused_computation.20 | convolution fusion | flops 11847598080 | bytes 19922944 | tf_op jit(solution)/shard_map/dot_general | solution.py:29
  596.4 96.2 %all-reduce.6.cloned.1.call-done = f32[224,128]{1,0:T(8,128)} async-done(((f32[224,128]{1,0:T(8,128)}), f32[224,128]{1,0:T(8,128)}) %all-reduce.6.cloned.1.call-update) | async-done | bytes 114704 | tf_op jit(solution)/shard_map/psum | solution.py:628
  761.5 23.2 %collective-permute-start.41 = (bf16[256,1024]{0,1:T(8,128)(2,1)S(1)}, bf16[256,1024]{0,1:T(8,128)(2,1)S(1)}, u32[]{:S(2)}, u32[]{:S(2)}) collective-permute-start(bf16[256,1024]{0,1:T(8,128)(2,1)S(1)} %get-tuple-element.95), channel_id=1, source_target_pairs={{0,8},{2,10},{4,12},{6,14},{8,16},{10,18},{12,20},{14,22},{16,24},... | collective-permute-start | bytes 1572872 | tf_op jit(solution)/shard_map/ppermute | solution.py:53
  786.9 19.6 %collective-permute-done.39 = bf16[256,1024]{0,1:T(8,128)(2,1)S(1)} collective-permute-done((bf16[256,1024]{0,1:T(8,128)(2,1)S(1)}, bf16[256,1024]{0,1:T(8,128)(2,1)S(1)}, u32[]{:S(2)}, u32[]{:S(2)}) %collective-permute-start.39) | collective-permute-done | bytes 524320 | tf_op jit(solution)/shard_map/ppermute | solution.py:53
  806.5 29.4 %collective-permute-start.49 = (bf16[256,1296]{0,1:T(8,128)(2,1)S(1)}, bf16[256,1296]{0,1:T(8,128)(2,1)S(1)}, u32[]{:S(2)}, u32[]{:S(2)}) collective-permute-start(bf16[256,1296]{0,1:T(8,128)(2,1)S(1)} %get-tuple-element.81), channel_id=1, source_target_pairs={{0,8},{2,10},{4,12},{6,14},{8,16},{10,18},{12,20},{14,22},{16,24},... | collective-permute-start | bytes 1990664 | tf_op jit(solution)/shard_map/ppermute | solution.py:53
  837.9 25.4 %collective-permute-done.47 = bf16[256,1296]{0,1:T(8,128)(2,1)S(1)} collective-permute-done((bf16[256,1296]{0,1:T(8,128)(2,1)S(1)}, bf16[256,1296]{0,1:T(8,128)(2,1)S(1)}, u32[]{:S(2)}, u32[]{:S(2)}) %collective-permute-start.47) | collective-permute-done | bytes 663584 | tf_op jit(solution)/shard_map/ppermute | solution.py:53
  894.3 75.5 %collective-permute-done.52 = f32[128,256]{0,1:T(8,128)S(1)} collective-permute-done((f32[128,256]{0,1:T(8,128)S(1)}, f32[128,256]{0,1:T(8,128)S(1)}, u32[]{:S(2)}, u32[]{:S(2)}) %collective-permute-start.52) | collective-permute-done | bytes 131104 | tf_op jit(solution)/shard_map/ppermute | solution.py:66
  (401 shorter events, 341.2 us)
Async XLA Ops:
  7.2 685.4 %all-reduce.6.cloned.1.call-start = ((), (), s32[]{:S(2)}) async-start(), calls=%async_computation | async-start | bytes 229376 | tf_op jit(solution)/shard_map/psum | solution.py:628
  28.1 201.2 %collective-permute-start.1 = (bf16[512,2048]{1,0:T(8,128)(2,1)}, bf16[512,2048]{1,0:T(8,128)(2,1)}, u32[]{:S(2)}, u32[]{:S(2)}) collective-permute-start(bf16[512,2048]{1,0:T(8,128)(2,1)} %fusion.7), channel_id=1, source_target_pairs={{0,1},{1,0},{2,3},{3,2},{4,5},{5,4},{6,7},{7,6},{8,9},{9,8},{10,11... | collective-permute-start | bytes 6291464 | tf_op jit(solution)/shard_map/ppermute | solution.py:66
  70.1 62.8 %collective-permute-start.15 = (bf16[256,1024]{0,1:T(8,128)(2,1)}, bf16[256,1024]{0,1:T(8,128)(2,1)}, u32[]{:S(2)}, u32[]{:S(2)}) collective-permute-start(bf16[256,1024]{0,1:T(8,128)(2,1)} %pad_maximum_fusion.6), channel_id=1, source_target_pairs={{0,4},{2,6},{4,0},{6,2},{8,12},{10,14},{12,8},{14,10},{16,20},{18,... | collective-permute-start | bytes 1572872 | tf_op jit(solution)/shard_map/ppermute | solution.py:53
  102.2 63.4 %collective-permute-start.25 = (bf16[256,1024]{0,1:T(8,128)(2,1)}, bf16[256,1024]{0,1:T(8,128)(2,1)}, u32[]{:S(2)}, u32[]{:S(2)}) collective-permute-start(bf16[256,1024]{0,1:T(8,128)(2,1)} %pad_maximum_fusion.7), channel_id=1, source_target_pairs={{0,24},{2,26},{4,28},{6,30},{8,0},{10,2},{12,4},{14,6},{16,8},{18,... | collective-permute-start | bytes 1572872 | tf_op jit(solution)/shard_map/ppermute | solution.py:53
  223.2 83.5 %collective-permute-start = (bf16[512,2048]{1,0:T(8,128)(2,1)}, bf16[512,2048]{1,0:T(8,128)(2,1)}, u32[]{:S(2)}, u32[]{:S(2)}) collective-permute-start(bf16[512,2048]{1,0:T(8,128)(2,1)} %fusion.7), channel_id=1, source_target_pairs={{0,2},{2,0},{4,6},{6,4},{8,10},{10,8},{12,14},{14,12},{16,18},{18,... | collective-permute-start | bytes 6291464 | tf_op jit(solution)/shard_map/ppermute | solution.py:53
  228.8 75.6 %collective-permute-start.20 = (bf16[512,2048]{1,0:T(8,128)(2,1)S(1)}, bf16[512,2048]{1,0:T(8,128)(2,1)}, u32[]{:S(2)}, u32[]{:S(2)}) collective-permute-start(bf16[512,2048]{1,0:T(8,128)(2,1)S(1)} %copy-done.10), channel_id=1, source_target_pairs={{0,1},{1,0},{2,3},{3,2},{4,5},{5,4},{6,7},{7,6},{8,9},{9,8},{10,11... | collective-permute-start | bytes 6291464 | tf_op jit(solution)/shard_map/ppermute | solution.py:66
  229.3 77.4 %collective-permute-start.2 = (bf16[512,2048]{1,0:T(8,128)(2,1)}, bf16[512,2048]{1,0:T(8,128)(2,1)}, u32[]{:S(2)}, u32[]{:S(2)}) collective-permute-start(bf16[512,2048]{1,0:T(8,128)(2,1)} %collective-permute-done.1), channel_id=1, source_target_pairs={{0,2},{2,0},{4,6},{6,4},{8,10},{10,8},{12,14},{14,12},{16,18},{18,... | collective-permute-start | bytes 6291464 | tf_op jit(solution)/shard_map/ppermute | solution.py:53
  290.9 80.2 %collective-permute-start.19 = (bf16[512,2048]{1,0:T(8,128)(2,1)S(1)}, bf16[512,2048]{1,0:T(8,128)(2,1)}, u32[]{:S(2)}, u32[]{:S(2)}) collective-permute-start(bf16[512,2048]{1,0:T(8,128)(2,1)S(1)} %copy-done.10), channel_id=1, source_target_pairs={{0,2},{2,0},{4,6},{6,4},{8,10},{10,8},{12,14},{14,12},{16,18},{18,... | collective-permute-start | bytes 6291464 | tf_op jit(solution)/shard_map/ppermute | solution.py:53
  306.7 64.4 %collective-permute-start.21 = (bf16[512,2048]{1,0:T(8,128)(2,1)}, bf16[512,2048]{1,0:T(8,128)(2,1)}, u32[]{:S(2)}, u32[]{:S(2)}) collective-permute-start(bf16[512,2048]{1,0:T(8,128)(2,1)} %collective-permute-done.20), channel_id=1, source_target_pairs={{0,2},{2,0},{4,6},{6,4},{8,10},{10,8},{12,14},{14,12},{16,18},{18,... | collective-permute-start | bytes 6291464 | tf_op jit(solution)/shard_map/ppermute | solution.py:53
  428.8 161.7 %collective-permute-start.53 = (bf16[256,1024]{0,1:T(8,128)(2,1)}, bf16[256,1024]{0,1:T(8,128)(2,1)}, u32[]{:S(2)}, u32[]{:S(2)}) collective-permute-start(bf16[256,1024]{0,1:T(8,128)(2,1)} %get-tuple-element.90), channel_id=1, source_target_pairs={{0,4},{2,6},{4,0},{6,2},{8,12},{10,14},{12,8},{14,10},{16,20},{18,... | collective-permute-start | bytes 1572872 | tf_op jit(solution)/shard_map/ppermute | solution.py:53
  430.3 160.8 %collective-permute-start.55 = (bf16[256,1024]{0,1:T(8,128)(2,1)}, bf16[256,1024]{0,1:T(8,128)(2,1)}, u32[]{:S(2)}, u32[]{:S(2)}) collective-permute-start(bf16[256,1024]{0,1:T(8,128)(2,1)} %get-tuple-element.93), channel_id=1, source_target_pairs={{0,4},{2,6},{4,0},{6,2},{8,12},{10,14},{12,8},{14,10},{16,20},{18,... | collective-permute-start | bytes 1572872 | tf_op jit(solution)/shard_map/ppermute | solution.py:53
  430.9 165.0 %collective-permute-start.57 = (bf16[256,1024]{0,1:T(8,128)(2,1)}, bf16[256,1024]{0,1:T(8,128)(2,1)}, u32[]{:S(2)}, u32[]{:S(2)}) collective-permute-start(bf16[256,1024]{0,1:T(8,128)(2,1)} %get-tuple-element.92), channel_id=1, source_target_pairs={{0,4},{2,6},{4,0},{6,2},{8,12},{10,14},{12,8},{14,10},{16,20},{18,... | collective-permute-start | bytes 1572872 | tf_op jit(solution)/shard_map/ppermute | solution.py:53
  432.4 263.1 %collective-permute-start.59 = (bf16[256,1024]{0,1:T(8,128)(2,1)}, bf16[256,1024]{0,1:T(8,128)(2,1)S(1)}, u32[]{:S(2)}, u32[]{:S(2)}) collective-permute-start(bf16[256,1024]{0,1:T(8,128)(2,1)} %get-tuple-element.91), channel_id=1, source_target_pairs={{0,4},{2,6},{4,0},{6,2},{8,12},{10,14},{12,8},{14,10},{16,20},{18,... | collective-permute-start | bytes 1572872 | tf_op jit(solution)/shard_map/ppermute | solution.py:53
  465.1 231.8 %collective-permute-start.36 = (bf16[256,1024]{0,1:T(8,128)(2,1)}, bf16[256,1024]{0,1:T(8,128)(2,1)S(1)}, u32[]{:S(2)}, u32[]{:S(2)}) collective-permute-start(bf16[256,1024]{0,1:T(8,128)(2,1)} %get-tuple-element.97), channel_id=1, source_target_pairs={{0,4},{2,6},{4,0},{6,2},{8,12},{10,14},{12,8},{14,10},{16,20},{18,... | collective-permute-start | bytes 1572872 | tf_op jit(solution)/shard_map/ppermute | solution.py:53
  590.6 107.0 %collective-permute-start.38 = (bf16[256,1024]{0,1:T(8,128)(2,1)}, bf16[256,1024]{0,1:T(8,128)(2,1)S(1)}, u32[]{:S(2)}, u32[]{:S(2)}) collective-permute-start(bf16[256,1024]{0,1:T(8,128)(2,1)} %get-tuple-element.100), channel_id=1, source_target_pairs={{0,4},{2,6},{4,0},{6,2},{8,12},{10,14},{12,8},{14,10},{16,20},{18,... | collective-permute-start | bytes 1572872 | tf_op jit(solution)/shard_map/ppermute | solution.py:53
  591.1 109.2 %collective-permute-start.40 = (bf16[256,1024]{0,1:T(8,128)(2,1)}, bf16[256,1024]{0,1:T(8,128)(2,1)S(1)}, u32[]{:S(2)}, u32[]{:S(2)}) collective-permute-start(bf16[256,1024]{0,1:T(8,128)(2,1)} %get-tuple-element.99), channel_id=1, source_target_pairs={{0,4},{2,6},{4,0},{6,2},{8,12},{10,14},{12,8},{14,10},{16,20},{18,... | collective-permute-start | bytes 1572872 | tf_op jit(solution)/shard_map/ppermute | solution.py:53
  595.8 105.9 %collective-permute-start.42 = (bf16[256,1024]{0,1:T(8,128)(2,1)}, bf16[256,1024]{0,1:T(8,128)(2,1)S(1)}, u32[]{:S(2)}, u32[]{:S(2)}) collective-permute-start(bf16[256,1024]{0,1:T(8,128)(2,1)} %get-tuple-element.98), channel_id=1, source_target_pairs={{0,4},{2,6},{4,0},{6,2},{8,12},{10,14},{12,8},{14,10},{16,20},{18,... | collective-permute-start | bytes 1572872 | tf_op jit(solution)/shard_map/ppermute | solution.py:53
  700.3 168.1 %collective-permute-start.34 = (bf16[2,512,2048]{2,1,0:T(8,128)(2,1)}, bf16[2,512,2048]{2,1,0:T(8,128)(2,1)}, u32[]{:S(2)}, u32[]{:S(2)}) collective-permute-start(bf16[2,512,2048]{2,1,0:T(8,128)(2,1)} %slice_bitcast_fusion.1), channel_id=1, source_target_pairs={{0,2},{2,0},{4,6},{6,4},{8,10},{10,8},{12,14},{14,12},{16,18},{18,... | collective-permute-start | bytes 12582920 | tf_op jit(solution)/shard_map/ppermute | solution.py:53
  756.1 119.7 %collective-permute-start.32 = (bf16[2,512,2048]{2,1,0:T(8,128)(2,1)S(1)}, bf16[2,512,2048]{2,1,0:T(8,128)(2,1)}, u32[]{:S(2)}, u32[]{:S(2)}) collective-permute-start(bf16[2,512,2048]{2,1,0:T(8,128)(2,1)S(1)} %copy-done.8), channel_id=1, source_target_pairs={{0,2},{2,0},{4,6},{6,4},{8,10},{10,8},{12,14},{14,12},{16,18},{18,... | collective-permute-start | bytes 12582920 | tf_op jit(solution)/shard_map/ppermute | solution.py:53
  806.5 56.8 %collective-permute-start.47 = (bf16[256,1296]{0,1:T(8,128)(2,1)S(1)}, bf16[256,1296]{0,1:T(8,128)(2,1)S(1)}, u32[]{:S(2)}, u32[]{:S(2)}) collective-permute-start(bf16[256,1296]{0,1:T(8,128)(2,1)S(1)} %get-tuple-element.82), channel_id=1, source_target_pairs={{0,16},{2,18},{4,20},{6,22},{8,24},{10,26},{12,28},{14,30},{16,0},... | collective-permute-start | bytes 1990664 | tf_op jit(solution)/shard_map/ppermute | solution.py:53
  806.5 56.8 %collective-permute-start.49 = (bf16[256,1296]{0,1:T(8,128)(2,1)S(1)}, bf16[256,1296]{0,1:T(8,128)(2,1)S(1)}, u32[]{:S(2)}, u32[]{:S(2)}) collective-permute-start(bf16[256,1296]{0,1:T(8,128)(2,1)S(1)} %get-tuple-element.81), channel_id=1, source_target_pairs={{0,8},{2,10},{4,12},{6,14},{8,16},{10,18},{12,20},{14,22},{16,24},... | collective-permute-start | bytes 1990664 | tf_op jit(solution)/shard_map/ppermute | solution.py:53
  874.3 96.3 %collective-permute-start.35 = (bf16[512,2048]{1,0:T(8,128)(2,1)}, bf16[512,2048]{1,0:T(8,128)(2,1)}, u32[]{:S(2)}, u32[]{:S(2)}) collective-permute-start(bf16[512,2048]{1,0:T(8,128)(2,1)} %fusion.18), channel_id=1, source_target_pairs={{0,1},{1,0},{2,3},{3,2},{4,5},{5,4},{6,7},{7,6},{8,9},{9,8},{10,11... | collective-permute-start | bytes 6291464 | tf_op jit(solution)/shard_map/ppermute | solution.py:66
  882.9 91.6 %collective-permute-start.33 = (bf16[512,2048]{1,0:T(8,128)(2,1)}, bf16[512,2048]{1,0:T(8,128)(2,1)}, u32[]{:S(2)}, u32[]{:S(2)}) collective-permute-start(bf16[512,2048]{1,0:T(8,128)(2,1)} %fusion.17), channel_id=1, source_target_pairs={{0,1},{1,0},{2,3},{3,2},{4,5},{5,4},{6,7},{7,6},{8,9},{9,8},{10,11... | collective-permute-start | bytes 6291464 | tf_op jit(solution)/shard_map/ppermute | solution.py:66
  885.6 84.2 %collective-permute-start.52 = (f32[128,256]{0,1:T(8,128)S(1)}, f32[128,256]{0,1:T(8,128)S(1)}, u32[]{:S(2)}, u32[]{:S(2)}) collective-permute-start(f32[128,256]{0,1:T(8,128)S(1)} %slice_add_fusion), channel_id=1, source_target_pairs={{0,1},{1,0},{2,3},{3,2},{4,5},{5,4},{6,7},{7,6},{8,9},{9,8},{10,11... | collective-permute-start | bytes 393224 | tf_op jit(solution)/shard_map/ppermute | solution.py:66
  (88 other events, 2224.7 us)
Sparse Core Ops, SparseCore 0:
  563.0 129.5 all-reduce.5

commit v2 on v1

--- a/solution.py
+++ b/solution.py
@@ -69,48 +69,62 @@
         f, s = k // self.zs, k % self.zs
         return ((self.z - s) % self.zs) * self.ys + (self.y - f) % self.ys
 
-    def chip_slot(self, b):
-        return ((self.y - b % self.ys) % self.ys) * self.zs + (self.z - b // self.ys) % self.zs
-
-    def gather(self, block):
-        column = [block] + [self.send_z(block, s) for s in range(1, self.zs)]
-        pieces = list(column)
-        for f in range(1, self.ys):
-            pieces += [self.send_y(piece, f) for piece in column]
-        return pieces
-
-    def scatter(self, pieces):
-        total = None
-        for s in list(range(1, self.zs)) + [0]:
-            part = pieces[s].astype(F32)
-            for f in range(1, self.ys):
-                part = part + self.send_y(pieces[f * self.zs + s], -f).astype(F32)
-            if s:
-                part = self.send_z(part.astype(BF16), -s).astype(F32)
-            total = part if total is None else total + part
-        return total
-
-
-def to_slots(grid, value, axis):
-    size = value.shape[axis] // grid.slots
-    return jnp.concatenate(
-        [
-            lax.dynamic_slice_in_dim(value, grid.slot_chip(k) * size, size, axis)
-            for k in range(grid.slots)
-        ],
-        axis=axis,
-    )
-
-
-def from_slots(grid, value, axis):
-    size = value.shape[axis] // grid.slots
-    return jnp.concatenate(
-        [
-            lax.dynamic_slice_in_dim(value, grid.chip_slot(b) * size, size, axis)
-            for b in range(grid.slots)
-        ],
-        axis=axis,
-    )
+    def all_sum(self, value, axis, bits):
+        for bit in bits:
+            size = self.dp if axis == "dp" else self.n
+            value = value + lax.ppermute(value, axis, [(i, i ^ bit) for i in range(size)])
+        return value
+
+    def dp_bits(self):
+        return [1 << i for i in range(1, self.dp.bit_length() - 1)]
+
+    def fsdp_bits(self):
+        return [1 << i for i in range(self.n.bit_length() - 1)]
+
+
+def gather_blocks(grid, block):
+    rows = block.shape[0]
+    out = jnp.zeros((grid.slots * rows,) + block.shape[1:], block.dtype)
+    piece = block
+    for s in range(grid.zs):
+        moved = grid.send_z(piece, 1) if s + 1 < grid.zs else None
+        for f in range(grid.ys):
+            here = grid.send_y(piece, f) if f else piece
+            out = lax.dynamic_update_slice_in_dim(
+                out, here, grid.slot_chip(f * grid.zs + s) * rows, 0
+            )
+        piece = moved
+    return out
+
+
+def scatter_blocks(grid, value):
+    rows = value.shape[0] // grid.slots
+    total = None
+    for s in range(grid.zs - 1, -1, -1):
+        piece = lambda f: lax.dynamic_slice_in_dim(
+            value, grid.slot_chip(f * grid.zs + s) * rows, rows, 0
+        )
+        part = piece(0).astype(F32)
+        for f in range(1, grid.ys):
+            part = part + grid.send_y(piece(f), -f).astype(F32)
+        if total is not None:
+            part = part + grid.send_z(total.astype(BF16), -1).astype(F32)
+        total = part
+    return total
+
+
+def core_groups(grid):
+    return [list(range(c, grid.dp, 2)) for c in (0, 1)]
+
+
+def gather_all(grid, block):
+    return lax.all_gather(block, "dp", axis=0, tiled=True, axis_index_groups=core_groups(grid))
+
+
+def scatter_all(grid, value):
+    return lax.psum_scatter(
+        value, "dp", scatter_dimension=0, tiled=True, axis_index_groups=core_groups(grid)
+    ).astype(F32)
 
 
 def shift_down(value, by):
@@ -167,10 +181,10 @@
     return jnp.where(keep, value, jnp.zeros_like(value))
 
 
-def fwd_kernel(limit_ref, xb_ref, taps_ref, heads_ref, skip_ref, y_ref, s1_ref, cm_ref):
+def fwd_kernel(waits, limit_ref, xb_ref, taps_ref, heads_ref, skip_ref, *refs):
+    y_ref, s1_ref = refs[waits:]
     inner = y_ref.shape[1]
-    q = pl.program_id(0)
-    limit = limit_ref[q]
+    limit = limit_ref[pl.program_id(0)]
     half = STRETCH // 2
     lo, hi = slice(0, STRETCH), slice(STRETCH, 2 * STRETCH)
     bc = slice(inner, inner + 2 * LANES)
@@ -228,24 +242,12 @@
     return jnp.sum(only(value, e), axis=1, keepdims=True)
 
 
-def bwd_kernel(
-    limit_ref,
-    xb_ref,
-    y_ref,
-    dy_ref,
-    s1_ref,
-    taps_ref,
-    heads_ref,
-    skip_ref,
-    dxb_ref,
-    gch_ref,
-    gh_ref,
-    dg_ref,
-    rs_ref,
-):
+def bwd_kernel(first, extra, limit_ref, xb_ref, y_ref, dy_ref, s1_ref, taps_ref, *refs):
+    heads_ref, skip_ref = refs[:2]
+    dxb_ref, gch_ref, gh_ref, dg_ref, rs_ref = refs[2 + extra :]
     inner = y_ref.shape[1]
     q = pl.program_id(0)
-    limit = limit_ref[q]
+    limit = limit_ref[q + first]
     half = STRETCH // 2
     lo, hi = slice(0, STRETCH), slice(STRETCH, 2 * STRETCH)
     bc = slice(inner, inner + 2 * LANES)
@@ -372,52 +374,69 @@
     gh_ref[1:2, :] += jnp.sum(flow, axis=0, keepdims=True)
 
 
-def run_fwd(limits, xb, taps, heads, skip, slot):
+def run_fwd(limits, xb, taps, heads, skip, slot, waits=()):
     rows, cols = xb.shape
     inner = cols - 3 * LANES
     seqs = rows // slot
     whole = lambda shape: pl.BlockSpec(shape, lambda q, *_: (0,) * len(shape))
     per = lambda width: pl.BlockSpec((slot, width), lambda q, *_: (q, 0))
     return pl.pallas_call(
-        fwd_kernel,
+        functools.partial(fwd_kernel, len(waits)),
         grid_spec=pltpu.PrefetchScalarGridSpec(
             num_scalar_prefetch=1,
             grid=(seqs,),
-            in_specs=[per(cols), whole(taps.shape), whole(heads.shape), whole(skip.shape)],
+            in_specs=[per(cols), whole(taps.shape), whole(heads.shape), whole(skip.shape)]
+            + [pl.BlockSpec(memory_space=pl.ANY)] * len(waits),
             out_specs=[
                 per(inner),
                 pl.BlockSpec((inner, LANES), lambda q, *_: (q, 0)),
             ],
-            scratch_shapes=[pltpu.VMEM((8, LANES), F32)],
         ),
         out_shape=[
             jax.ShapeDtypeStruct((rows, inner), F32),
             jax.ShapeDtypeStruct((seqs * inner, LANES), BF16),
         ],
         name="scan_forward",
-    )(limits, xb, taps, heads, skip)
-
-
-def run_bwd(limits, xb, y, dy, s1, taps, heads, skip, slot):
+    )(limits, xb, taps, heads, skip, *waits)
+
+
+def tie_kernel(*refs):
+    pass
+
+
+def tie(value, *waits):
+    return pl.pallas_call(
+        tie_kernel,
+        in_specs=[pl.BlockSpec(memory_space=pl.ANY)] * (1 + len(waits)),
+        out_specs=pl.BlockSpec(memory_space=pl.ANY),
+        out_shape=jax.ShapeDtypeStruct(value.shape, value.dtype),
+        input_output_aliases={0: 0},
+        name="order",
+    )(value, *waits)
+
+
+def run_bwd(limits, xb, y, dy, s1, taps, heads, skip, slot, first, count, d_xb=None, waits=()):
     rows, cols = xb.shape
     inner = cols - 3 * LANES
-    seqs = rows // slot
     whole = lambda shape: pl.BlockSpec(shape, lambda q, *_: (0,) * len(shape))
-    per = lambda width: pl.BlockSpec((slot, width), lambda q, *_: (q, 0))
+    per = lambda width: pl.BlockSpec((slot, width), lambda q, *_: (q + first, 0))
+    aliased = d_xb is not None
+    kernel = functools.partial(bwd_kernel, first, aliased + len(waits))
     return pl.pallas_call(
-        bwd_kernel,
+        kernel,
         grid_spec=pltpu.PrefetchScalarGridSpec(
             num_scalar_prefetch=1,
-            grid=(seqs,),
+            grid=(count,),
             in_specs=[
                 per(cols),
                 per(inner),
                 per(inner),
-                pl.BlockSpec((inner, LANES), lambda q, *_: (q, 0)),
+                pl.BlockSpec((inner, LANES), lambda q, *_: (q + first, 0)),
                 whole(taps.shape),
                 whole(heads.shape),
                 whole(skip.shape),
-            ],
+            ]
+            + [pl.BlockSpec(memory_space=pl.ANY)] * (aliased + len(waits)),
             out_specs=[per(cols), whole((8, cols)), whole((8, LANES))],
             scratch_shapes=[
                 pltpu.VMEM((2, STRETCH, STRETCH), F32),
@@ -429,8 +448,91 @@
             jax.ShapeDtypeStruct((8, cols), F32),
             jax.ShapeDtypeStruct((8, LANES), F32),
         ],
+        input_output_aliases={8: 0} if aliased else {},
         name="scan_backward",
-    )(limits, xb, y, dy, s1, taps, heads, skip)
+    )(limits, xb, y, dy, s1, taps, heads, skip, *([d_xb] if aliased else []), *waits)
+
+
+def prepare_kernel(length_ref, u_ref, cot_ref, gain_ref, normed_ref, branch_ref):
+    rows, _ = u_ref.shape
+    u = u_ref[...].astype(F32)
+    rstd = lax.rsqrt(jnp.mean(u * u, axis=-1, keepdims=True) + 1e-05)
+    row = lax.broadcasted_iota(jnp.int32, (rows, 1), 0) + pl.program_id(0) * rows
+    valid = row < length_ref[0]
+    normed_ref[...] = (u * rstd * gain_ref[...]).astype(BF16)
+    branch_ref[...] = jnp.where(valid, cot_ref[...].astype(F32), 0.0).astype(BF16)
+
+
+def run_prepare(lengths, tokens, cotangent, gain):
+    slot, width = tokens.shape
+    step = slot // 4
+    per = pl.BlockSpec((step, width), lambda i, *_: (i, 0))
+    return pl.pallas_call(
+        prepare_kernel,
+        grid_spec=pltpu.PrefetchScalarGridSpec(
+            num_scalar_prefetch=1,
+            grid=(4,),
+            in_specs=[per, per, pl.BlockSpec((1, width), lambda i, *_: (0, 0))],
+            out_specs=[per, per],
+        ),
+        out_shape=[jax.ShapeDtypeStruct((slot, width), BF16)] * 2,
+        name="prepare_rows",
+    )(lengths, tokens, cotangent, gain)
+
+
+def output_kernel(count, length_ref, u_ref, *refs):
+    parts, out_ref = refs[:count], refs[count]
+    rows, _ = u_ref.shape
+    row = lax.broadcasted_iota(jnp.int32, (rows, 1), 0) + pl.program_id(0) * rows
+    total = parts[0][...].astype(F32)
+    for part in parts[1:]:
+        total = total + part[...].astype(F32)
+    total = jnp.where(row < length_ref[0], total, 0.0)
+    out_ref[...] = (u_ref[...].astype(F32) + total).astype(BF16)
+
+
+def grad_kernel(count, u_ref, cot_ref, gain_ref, *refs):
+    parts, out_ref = refs[:count], refs[count]
+    u = u_ref[...].astype(F32)
+    rstd = lax.rsqrt(jnp.mean(u * u, axis=-1, keepdims=True) + 1e-05)
+    total = parts[0][...].astype(F32)
+    for part in parts[1:]:
+        total = total + part[...].astype(F32)
+    total = total * gain_ref[...]
+    back = jnp.mean(total * u, axis=-1, keepdims=True)
+    grad = total * rstd - u * (rstd * rstd * rstd * back)
+    out_ref[...] = (cot_ref[...].astype(F32) + grad).astype(BF16)
+
+
+def run_output(lengths, tokens, parts):
+    slot, width = tokens.shape
+    step = slot // 4
+    per = pl.BlockSpec((step, width), lambda i, *_: (i, 0))
+    return pl.pallas_call(
+        functools.partial(output_kernel, len(parts)),
+        grid_spec=pltpu.PrefetchScalarGridSpec(
+            num_scalar_prefetch=1,
+            grid=(4,),
+            in_specs=[per] * (1 + len(parts)),
+            out_specs=per,
+        ),
+        out_shape=jax.ShapeDtypeStruct((slot, width), BF16),
+        name="layer_output",
+    )(lengths, tokens, *parts)
+
+
+def run_grad(tokens, cotangent, gain, parts):
+    slot, width = tokens.shape
+    step = slot // 8
+    per = pl.BlockSpec((step, width), lambda i: (i, 0))
+    return pl.pallas_call(
+        functools.partial(grad_kernel, len(parts)),
+        grid=(8,),
+        in_specs=[per, per, pl.BlockSpec((1, width), lambda i: (0, 0))] + [per] * len(parts),
+        out_specs=per,
+        out_shape=jax.ShapeDtypeStruct((slot, width), BF16),
+        name="input_gradient",
+    )(tokens, cotangent, gain, *parts)
 
 
 def per_device(
@@ -477,50 +579,44 @@
         second = jnp.where(core == 0, other, mine)
         return jnp.concatenate([first, second], axis=axis)
 
-    z_mine, z_other = halves(w_zx[:, 0], 1)
+    gain_row = norm_gain[None]
+    normed_own, d_branch_own = run_prepare(lengths, tokens, cotangent, gain_row)
+
     x_mine, x_other = halves(w_zx[:, 1], 1)
     t_mine, t_other = halves(w_dt, 1)
-    o_mine, o_other = halves(w_out.T, 1)
     x_mine = jnp.concatenate([x_mine, w_bc, t_mine], axis=1)
     x_other = jnp.concatenate([x_other, w_bc, t_other], axis=1)
+    block_x = by_core(x_mine, grid.swap_core(x_other), 0)
+    z_mine, z_other = halves(w_zx[:, 0], 1)
+    block_z = by_core(z_mine, grid.swap_core(z_other), 0)
+    o_mine, o_other = halves(w_out.T, 1)
     block_o = by_core(o_mine, grid.swap_core(o_other), 0)
-    block_x = by_core(x_mine, grid.swap_core(x_other), 0)
-    block_z = by_core(z_mine, grid.swap_core(z_other), 0)
-    w_o = jnp.concatenate(grid.gather(block_o), axis=0)
-    w_x = jnp.concatenate(grid.gather(block_x), axis=0)
-    w_z = jnp.concatenate(grid.gather(block_z), axis=0)
+    w_x = gather_blocks(grid, block_x)
+    w_z = gather_all(grid, block_z)
+    w_o = gather_all(grid, block_o)
     w_x = jnp.pad(w_x, ((0, 0), (0, cols - sent)))
 
-    u = to_slots(grid, tokens, 1).astype(F32)
-    cot = to_slots(grid, cotangent, 1)
-    gain = to_slots(grid, norm_gain, 0)
-    rstd = lax.rsqrt(jnp.mean(u * u, axis=-1, keepdims=True) + 1e-05)
-    normed_own = (u * rstd * gain).astype(BF16)
-    valid = (jnp.arange(slot) < lengths[0])[:, None]
-    d_branch_own = jnp.where(valid, cot, jnp.zeros_like(cot))
+    order = [(g, e) for g in range(n - 1, -1, -1) for e in (1, 0)]
+    index = lax.axis_index("dp")
+    owners = [(index + e * (1 - 2 * core)) * n + (j - g) % n for g, e in order]
 
     def share(value):
         near = [value] + [grid.send_x(value, g) for g in range(1, n)]
-        pieces = []
-        for piece in near:
-            pieces += [piece, grid.swap_core(piece)]
-        return jnp.concatenate(pieces, axis=0)
-
-    def collect(value):
-        value = value.reshape(n, 2, slot, width)
-        here = value[:, 0].astype(F32) + grid.swap_core(value[:, 1]).astype(F32)
-        out = here[0]
-        for g in range(1, n):
-            out = out + grid.send_x(here[g].astype(BF16), -g).astype(F32)
-        return out
+        far = [grid.swap_core(piece) for piece in near]
+        pieces = [far[g] if e else near[g] for g, e in order]
+        return lax.optimization_barrier(jnp.concatenate(pieces, axis=0))
+
+    def collect(parts):
+        kept = []
+        for i in range(0, len(parts), 2):
+            g = order[i][0]
+            there = grid.swap_core(parts[i])
+            both = parts[i + 1].astype(F32) + there.astype(F32)
+            kept.append(grid.send_x(both.astype(BF16), -g) if g else both)
+        return kept
 
     normed = share(normed_own)
     d_branch = share(d_branch_own)
-    index = lax.axis_index("dp")
-    owners = []
-    for g in range(n):
-        for e in (0, 1):
-            owners.append((index + e * (1 - 2 * core)) * n + (j - g) % n)
     seqs = len(owners)
     seq_width = jnp.stack([widths[o] for o in owners])
     used = seq_width * ((HEADS // 8) * HEAD_DIM)
@@ -545,48 +641,67 @@
     skip = jnp.broadcast_to(jnp.repeat(own_heads(d_skip), HEAD_DIM)[None], (8, inner))
     own_gain = lax.dynamic_slice_in_dim(gate_gain, channel_base, inner, 0)
 
-    d_gnorm = dot_nn(d_branch, w_o)
+    rows_of = lambda value, i: value[i * slot : (i + 1) * slot]
     xb = dot_nn(normed, w_x)
-    y, s1 = run_fwd(limits, xb, taps, head_rows, skip, slot)
+    scan = (taps, head_rows, skip, slot)
+    y, s1 = run_fwd(limits, xb, *scan)
     z = dot_nn(normed, w_z)
     sig = jax.nn.sigmoid(z)
     gated = y * (z * sig)
+
+    def group_sum(rows):
+        rows = rows.reshape(n, 2, slot)
+        rows = rows + grid.swap_core(rows)[:, ::-1]
+        total = rows
+        for g in range(1, n):
+            total = total + jnp.roll(grid.send_x(rows, g), -g, axis=0)
+        return total.reshape(seqs * slot)
+
+    scale = lax.rsqrt(group_sum(jnp.sum(gated * gated, axis=1)) / counts + 1e-05)
+    gnorm = (gated * scale[:, None] * own_gain).astype(BF16)
+
+    g_o_part = dot_tn(d_branch, gnorm).astype(BF16)
+    g_o = scatter_all(grid, g_o_part)
+    d_gnorm = dot_nn(d_branch, w_o)
     weighted = d_gnorm * own_gain
-    stats = jnp.stack([jnp.sum(gated * gated, axis=1), jnp.sum(weighted * gated, axis=1)])
-    stats = stats.reshape(2, n, 2, slot)
-    stats = stats + grid.swap_core(stats)[:, :, ::-1]
-    whole = stats
-    for g in range(1, n):
-        whole = whole + jnp.roll(grid.send_x(stats, g), g, axis=1)
-    stats = whole.reshape(2, seqs * slot)
-    scale = lax.rsqrt(stats[0] / counts + 1e-05)
-    pull = scale * scale * scale / counts * stats[1]
-    gnorm = (gated * scale[:, None] * own_gain).astype(BF16)
+    inner_sum = group_sum(jnp.sum(weighted * gated, axis=1))
+    pull = scale * scale * scale / counts * inner_sum
     d_gated = weighted * scale[:, None] - gated * pull[:, None]
     g_gate = jnp.sum(d_gnorm * gated * scale[:, None], axis=0)
     silu = z * sig
     d_y = (d_gated * silu).astype(BF16)
     d_z = (d_gated * y * (sig * (1.0 + z * (1.0 - sig)))).astype(BF16)
-
-    def reduce(grad):
-        return grid.scatter(jnp.split(grad.astype(BF16), grid.slots, axis=0))
-
-    g_o = reduce(dot_tn(d_branch, gnorm))
-    g_z = reduce(dot_tn(normed, d_z))
-    branch = collect(dot_nt(gnorm, w_o).astype(BF16))
-    d_xb, g_channels, g_heads = run_bwd(limits, xb, y, d_y, s1, taps, head_rows, skip, slot)
-    g_x = reduce(dot_tn(normed, d_xb)[:, :sent])
-    d_normed_part = dot_nt(d_z, w_z) + dot_nt(d_xb, w_x)
-    g_norm_part = jnp.sum(d_normed_part * normed.astype(F32), axis=0) / gain
-    d_normed = collect(d_normed_part.astype(BF16))
-
-    output = (u + jnp.where(valid, branch, 0.0)).astype(BF16)
-    d_scaled = d_normed * gain
-    back = jnp.mean(d_scaled * u, axis=-1, keepdims=True)
-    d_u = d_scaled * rstd - u * (rstd * rstd * rstd * back)
-    input_grad = (cot.astype(F32) + d_u).astype(BF16)
-    output = from_slots(grid, output, 1)
-    input_grad = from_slots(grid, input_grad, 1)
+    g_z_part = dot_tn(normed, d_z).astype(BF16)
+    g_z = scatter_all(grid, g_z_part)
+
+    def back(i):
+        part = dot_nt(rows_of(d_z, i), w_z) + dot_nt(rows_of(d_xb, i), w_x)
+        return jnp.sum(part * rows_of(normed, i).astype(F32), axis=0), part.astype(BF16)
+
+    far = seqs - 2
+    d_normed, branch, g_norm_part = [], [], 0.0
+    d_xb, g_channels, g_heads = run_bwd(
+        limits, xb, y, d_y, s1, *scan, 0, far, None, (g_o_part, g_z_part)
+    )
+    ahead = [back(i) for i in range(far)]
+    for i in range(0, far, 2):
+        both = ahead[i + 1][1].astype(F32) + grid.swap_core(ahead[i][1]).astype(F32)
+        d_normed.append(both.astype(BF16))
+    d_xb, more_channels, more_heads = run_bwd(
+        limits, xb, y, d_y, s1, *scan, far, 2, d_xb, tuple(d_normed)
+    )
+    d_normed = [grid.send_x(d_normed[i], -order[2 * i][0]) for i in range(len(d_normed))]
+    g_channels, g_heads = g_channels + more_channels, g_heads + more_heads
+    g_x_part = dot_tn(normed, d_xb)[:, :sent].astype(BF16)
+    g_x = scatter_blocks(grid, g_x_part)
+    out_rows = [dot_nt(rows_of(gnorm, i), w_o).astype(BF16) for i in range(seqs)]
+    branch = collect(out_rows)
+    ahead += [back(i) for i in range(far, seqs)]
+    d_normed.append(ahead[far + 1][1].astype(F32) + grid.swap_core(ahead[far][1]).astype(F32))
+    g_norm_part = sum(part[0] for part in ahead)
+
+    output = run_output(lengths, tokens, branch)
+    input_grad = run_grad(tokens, cotangent, gain_row, d_normed)
 
     def to_rows(value):
         mine = lax.dynamic_slice_in_dim(value, core * rows_d, rows_d, 0)
@@ -604,28 +719,36 @@
         bc_sum = bc_sum + grid.send_x(bc_rows, g)
     g_w_zx = jnp.stack([z_rows, x_rows], axis=1)
 
-    conv_rows = jnp.zeros((5, total), F32)
-    conv_rows = lax.dynamic_update_slice(conv_rows, g_channels[:5, :inner], (0, channel_base))
-    conv_rows = lax.dynamic_update_slice(
-        conv_rows, g_channels[:5, inner : inner + state2], (0, all_inner)
-    )
-    gate_row = lax.dynamic_update_slice(jnp.zeros((all_inner,), F32), g_gate, (channel_base,))
     g_skip = g_channels[5, :inner].reshape(heads, HEAD_DIM).sum(axis=1)
     head_parts = jnp.stack([g_heads[0, :heads], g_heads[1, :heads], g_skip])
-    head_parts = lax.dynamic_update_slice(
-        jnp.zeros((3, d_skip.shape[0]), F32), head_parts, (0, head_base)
-    )
-    flat = jnp.concatenate(
-        [
-            from_slots(grid, g_norm_part, 0),
-            conv_rows.reshape(-1),
-            gate_row,
-            head_parts.reshape(-1),
-        ]
-    )
+    mine = [
+        g_channels[:5].reshape(-1),
+        g_gate,
+        g_norm_part / norm_gain,
+        head_parts.reshape(-1),
+    ]
+    sizes = [piece.shape[0] for piece in mine]
+    flat = jnp.concatenate(mine)
+    flat = jnp.pad(flat, (0, -flat.shape[0] % 1024)).reshape(-1, LANES)
+    flat = grid.all_sum(flat, "dp", grid.dp_bits()).reshape(-1)
+    own_conv = flat[: sizes[0]].reshape(5, cols)
+    own_gate = flat[sizes[0] : sizes[0] + sizes[1]]
+    own_norm = flat[sizes[0] + sizes[1] : sum(sizes[:3])]
+    own_heads_sum = flat[sum(sizes[:3]) : sum(sizes)].reshape(3, heads)
+    conv_rows = jnp.zeros((5, total), F32)
+    conv_rows = lax.dynamic_update_slice(conv_rows, own_conv[:, :inner], (0, channel_base))
+    conv_rows = lax.dynamic_update_slice(
+        conv_rows, own_conv[:, inner : inner + state2], (0, all_inner)
+    )
+    gate_row = lax.dynamic_update_slice(jnp.zeros((all_inner,), F32), own_gate, (channel_base,))
+    head_all = lax.dynamic_update_slice(
+        jnp.zeros((3, d_skip.shape[0]), F32), own_heads_sum, (0, head_base)
+    )
+    flat = jnp.concatenate([own_norm, conv_rows.reshape(-1), gate_row, head_all.reshape(-1)])
     size = flat.shape[0]
     flat = jnp.pad(flat, (0, -size % 1024)).reshape(-1, LANES)
-    flat = lax.psum(flat, ("dp", "fsdp")).reshape(-1)[:size]
+    flat = grid.all_sum(flat, "dp", [1])
+    flat = grid.all_sum(flat, "fsdp", grid.fsdp_bits()).reshape(-1)[:size]
     ends = [width, width + 5 * total, width + 5 * total + all_inner]
     g_norm, g_conv, g_gate, g_small = jnp.split(flat, ends)
     g_conv = g_conv.reshape(5, total)

time: 1000 us -> 603 us (0.60)
  waiting for transfers between devices: 392 us -> 118 us
  starting transfers between devices: 170 us -> 38.8 us
  local copies, waits for them, and re-layouts: 104 us -> 74.6 us
  Pallas kernels: 80.7 us -> 105 us
  matrix products: 156 us -> 177 us
    ppermute x55 -> x30, starting transfers between devices: 163 us -> 27.5 us  [_dp(): return lax.ppermute(value, 'dp', pairs)]
    ppermute x55 -> x30, waiting for transfers between devices: 217 us -> 103 us  [_dp(): return lax.ppermute(value, 'dp', pairs)]
    psum x1 -> x0, waiting for transfers between devices: 96.2 us -> none  [per_device(): flat = lax.psum(flat, ('dp', 'fsdp')).reshape(-1)[:size]]
    ppermute x6 -> x7, waiting for transfers between devices: 78.7 us -> 10.2 us  [send_x(): return lax.ppermute(value, 'fsdp', pairs)]
    unnamed x172 -> x82, local copies, waits for them, and re-layouts: 54.5 us -> 11.4 us
    dot_general x3 -> x12, matrix products: 50 us -> 82.6 us  [dot_nt(): lax.dot_general(a, b, (((1,), (1,)), ((), ())), preferred_element_type=F32)]
    pallas_call x2 -> x6, Pallas kernels: 80.7 us -> 105 us  [the longest x2 61.2 us: run_bwd(): pl.pallas_call(kernel, grid_spec=pltpu.PrefetchScalarGridSpec(num_scalar_...]
    ppermute x0 -> x14, local copies, waits for them, and re-layouts: none -> 18.3 us  [_dp(): return lax.ppermute(value, 'dp', pairs)]
  transfers between devices with their start and end apart: 62 -> 46, of which waited for: 24 -> 14; matrix products, arithmetic and copies ran while one was open for 26% -> 43% of each run, Pallas kernels for 8% -> 18%
where the time goes in v2:
time: 603 us; the launch traced here: 594 us
  matrix products  177 us (29%)
  waiting for transfers between devices  118 us (20%)
  Pallas kernels  105 us (17%)
  local copies, waits for them, and re-layouts  74.6 us (12%)
  other arithmetic  65.2 us (11%)
  starting transfers between devices  38.8 us (6%)
  between operations  15.7 us (3%)
    ppermute x30, waiting for transfers between devices, _dp(): return lax.ppermute(value, 'dp', pairs)  103 us
    dot_general x12, matrix products, dot_nt(): lax.dot_general(a, b, (((1,), (1,)), ((), ())), preferred_element_type=F32)  82.6 us
    pallas_call x2, Pallas kernels, run_bwd(): pl.pallas_call(kernel, grid_spec=pltpu.PrefetchScalarGridSpec(num_scalar_...  61.2 us
    dot_general x3, matrix products, dot_nn(): lax.dot_general(a, b, (((1,), (0,)), ((), ())), preferred_element_type=F32)  53.1 us
    dot_general x3, matrix products, dot_tn(): lax.dot_general(a, b, (((0,), (0,)), ((), ())), preferred_element_type=F32)  41.3 us
    ppermute x30, starting transfers between devices, _dp(): return lax.ppermute(value, 'dp', pairs)  27.5 us
    pallas_call x1, Pallas kernels, run_fwd(): pl.pallas_call(functools.partial(fwd_kernel, len(waits)), grid_spec=pltpu...  25 us
    ppermute x14, local copies, waits for them, and re-layouts, _dp(): return lax.ppermute(value, 'dp', pairs)  18.3 us
  transfers between devices with their start and end apart: 46, of which 14 were waited for; matrix products, arithmetic and copies ran while one was open for 43% of the time, Pallas kernels for 18%

profile of v2, /device:TPU:0, one launch (start us, length us, event | category | flops | bytes accessed | tf_op | source)
XLA Modules:
  0.0 594.4 jit_solution(3551489303233150658)
XLA Ops:
  39.5 23.9 %collective-permute-done.5 = bf16[256,1296]{0,1:T(8,128)(2,1)} collective-permute-done((bf16[256,1296]{0,1:T(8,128)(2,1)S(1)}, bf16[256,1296]{0,1:T(8,128)(2,1)}, u32[]{:S(2)}, u32[]{:S(2)}) %collective-permute-start.5) | collective-permute-done | bytes 663584 | tf_op jit(solution)/shard_map/ppermute | solution.py:53
  66.5 7.1 %collective-permute-done = bf16[512,2048]{1,0:T(8,128)(2,1)} collective-permute-done((bf16[512,2048]{1,0:T(8,128)(2,1)}, bf16[512,2048]{1,0:T(8,128)(2,1)}, u32[]{:S(2)}, u32[]{:S(2)}) %collective-permute-start) | collective-permute-done | bytes 2097184 | tf_op jit(solution)/shard_map/ppermute | solution.py:66
  76.3 20.3 %collective-permute-done.7 = bf16[256,1296]{0,1:T(8,128)(2,1)} collective-permute-done((bf16[256,1296]{0,1:T(8,128)(2,1)}, bf16[256,1296]{0,1:T(8,128)(2,1)}, u32[]{:S(2)}, u32[]{:S(2)}) %collective-permute-start.7) | collective-permute-done | bytes 663584 | tf_op jit(solution)/shard_map/ppermute | solution.py:53
  103.8 24.1 %collective-permute-done.9 = bf16[256,1296]{0,1:T(8,128)(2,1)} collective-permute-done((bf16[256,1296]{0,1:T(8,128)(2,1)}, bf16[256,1296]{0,1:T(8,128)(2,1)}, u32[]{:S(2)}, u32[]{:S(2)}) %collective-permute-start.9) | collective-permute-done | bytes 663584 | tf_op jit(solution)/shard_map/ppermute | solution.py:53
  136.8 12.4 %collective-permute-done.10 = bf16[256,1296]{0,1:T(8,128)(2,1)} collective-permute-done((bf16[256,1296]{0,1:T(8,128)(2,1)}, bf16[256,1296]{0,1:T(8,128)(2,1)}, u32[]{:S(2)}, u32[]{:S(2)}) %collective-permute-start.10) | collective-permute-done | bytes 663584 | tf_op jit(solution)/shard_map/ppermute | solution.py:53
  156.1 19.0 %fusion.9.xb_ref = f32[2048,1408]{1,0:T(8,128)} fusion(bf16[2048,2048]{1,0:T(8,128)(2,1)S(1)} %pad_maximum_fusion, bf16[2048,1296]{1,0:T(8,128)(2,1)} %constant_dynamic-update-slice_fusion.1), kind=kOutput, calls=%fused_computation.30 | convolution fusion | flops 11811160064 | bytes 25231360 | tf_op jit(solution)/shard_map/dot_general | solution.py:21
  175.7 25.0 %scan_forward.1 = (f32[2048,1024]{1,0:T(8,128)}, bf16[4096,128]{1,0:T(8,128)(2,1)}) custom-call(s32[4]{0:T(128)} %subtract_clamp_fusion.limit_ref, f32[2048,1408]{1,0:T(8,128)} %fusion.9.xb_ref, f32[8,1408]{1,0:T(8,128)} %select_maximum_fusion.3.taps_ref, f32[8,128]{1,0:T(8,128)} %select_maximum_fusion.8.heads_ref.refs_0_, ...), custom_call_target="tpu_custom_call" | custom-call | tf_op jit(solution)/shard_map/scan_forward/pallas_call | solution.py:383
  200.8 18.0 %multiply_reduce_fusion.2 = (f32[2048]{0:T(1024)S(1)}, f32[2048,1024]{1,0:T(8,128)}, f32[2048,1024]{1,0:T(8,128)}) fusion(f32[2048,1024]{1,0:T(8,128)} %get-tuple-element.24.y_ref, bf16[2048,2048]{1,0:T(8,128)(2,1)} %copy-done.2, bf16[2048,1024]{1,0:T(8,128)(2,1)} %all-gather.3.cloned.1.call-done), kind=kOutput, calls=%fused_computation.9 | convolution fusion | flops 8604612608 | bytes 37756928 | tf_op jit(solution)/shard_map/dot_general | solution.py:21
  221.7 6.6 %pad_maximum_fusion.1 = bf16[2048,2048]{1,0:T(8,128)(2,1)} fusion(bf16[512,2048]{1,0:T(8,128)(2,1)S(1)} %copy-done.11, bf16[512,2048]{1,0:T(8,128)(2,1)} %collective-permute-done.20, bf16[512,2048]{1,0:T(8,128)(2,1)} %collective-permute-done.18, bf16[512,2048]{1,0:T(8,128)(2,1)} %collective-permute-done.19), kind=kLoop, calls=%fused_computation.2 | loop fusion | flops 33554432 | bytes 16777216 | tf_op jit(solution)/shard_map/concatenate | solution.py:607
  228.3 16.1 %multiply_reduce_fusion = (f32[1024]{0:T(1024)S(1)}, f32[2048]{0:T(1024)S(1)}, f32[2048,1024]{1,0:T(8,128)}) fusion(f32[2048,1024]{1,0:T(8,128)} %get-tuple-element.94, f32[2048]{0:T(1024)S(1)} %add_rsqrt_fusion, f32[1024]{0:T(1024)S(1)} %dynamic_slice.123, bf16[2048,2048]{1,0:T(8,128)(2,1)} %pad_maximum_fusion.1, ...), kind=kOutput, calls=%fused_computation.3 | convolution fusion | flops 8602514432 | bytes 29384704 | tf_op jit(solution)/shard_map/dot_general | solution.py:21
  249.6 16.4 %multiply_convert_fusion = (bf16[2048,1024]{1,0:T(8,128)(2,1)}, bf16[2048,1024]{1,0:T(8,128)(2,1)}, bf16[2048,1024]{1,0:T(8,128)(2,1)S(1)}) fusion(f32[2048,1024]{1,0:T(8,128)} %get-tuple-element.94, f32[2048]{0:T(1024)S(1)} %fusion.45, f32[2048]{0:T(1024)S(1)} %add_rsqrt_fusion, f32[2048,1024]{1,0:T(8,128)} %get-tuple-element.141, ...), kind=kLoop, calls=%fused_computation.4 | loop fusion | flops 41943040 | bytes 46157824 | tf_op jit(solution)/shard_map/convert_element_type | solution.py:672
  268.1 11.3 %convolution_convert_fusion.1.refs_2_ = bf16[2048,1024]{1,0:T(8,128)(2,1)} fusion(bf16[2048,2048]{1,0:T(8,128)(2,1)S(1)} %copy-done.3, bf16[2048,1024]{1,0:T(8,128)(2,1)S(1)} %get-tuple-element.97), kind=kOutput, calls=%fused_computation.21 | convolution fusion | flops 8592031744 | bytes 16777216 | tf_op jit(solution)/shard_map/dot_general | solution.py:29
  279.5 14.0 %convolution_convert_fusion.refs_3_ = bf16[2048,1024]{1,0:T(8,128)(2,1)} fusion(bf16[2048,2048]{1,0:T(8,128)(2,1)} %copy-done.2, bf16[2048,1024]{1,0:T(8,128)(2,1)} %get-tuple-element.96), kind=kOutput, calls=%fused_computation.20 | convolution fusion | flops 8592031744 | bytes 16777216 | tf_op jit(solution)/shard_map/dot_general | solution.py:29
  293.4 30.7 %scan_backward.2 = (bf16[2048,1408]{1,0:T(8,128)(2,1)}, f32[8,1408]{1,0:T(8,128)}, f32[8,128]{1,0:T(8,128)}) custom-call(s32[4]{0:T(128)} %subtract_clamp_fusion.limit_ref, f32[2048,1408]{1,0:T(8,128)} %fusion.9.xb_ref, f32[2048,1024]{1,0:T(8,128)} %get-tuple-element.24.y_ref, bf16[2048,1024]{1,0:T(8,128)(2,1)} %get-tuple-element.95.dy_ref, ...), custom_call_target="tpu_custom_call" | custom-call | tf_op jit(solution)/shard_map/scan_backward/pallas_call | solution.py:425
  329.1 9.4 %fusion.61 = (bf16[512,2048]{1,0:T(8,128)(2,1)}, f32[512,2048]{1,0:T(8,128)}) fusion(f32[512,2048]{1,0:T(8,128)S(1)} %fusion.32, bf16[2048,1296]{1,0:T(8,128)(2,1)} %constant_dynamic-update-slice_fusion.1, bf16[2048,1408]{1,0:T(8,128)(2,1)} %get-tuple-element.27.refs_2_), kind=kOutput, calls=%fused_computation.169 | convolution fusion | flops 2954887168 | bytes 17694720 | tf_op jit(solution)/shard_map/dot_general | solution.py:25
  366.6 30.4 %scan_backward.3 = (bf16[2048,1408]{1,0:T(8,128)(2,1)}, f32[8,1408]{1,0:T(8,128)}, f32[8,128]{1,0:T(8,128)}) custom-call(s32[4]{0:T(128)} %subtract_clamp_fusion.limit_ref, f32[2048,1408]{1,0:T(8,128)} %fusion.9.xb_ref, f32[2048,1024]{1,0:T(8,128)} %get-tuple-element.24.y_ref, ...), custom_call_target="tpu_custom_call", output_to_operand_aliasing={{0}: (8, {})} | custom-call | tf_op jit(solution)/shard_map/scan_backward/pallas_call | solution.py:425
  398.9 9.9 %fusion.20 = f32[512,2048]{1,0:T(8,128)} fusion(f32[512,2048]{1,0:T(8,128)} %fusion.28, bf16[2048,1296]{1,0:T(8,128)(2,1)} %constant_dynamic-update-slice_fusion.1, bf16[2048,1408]{1,0:T(8,128)(2,1)} %get-tuple-element.28), kind=kOutput, calls=%fused_computation.35 | convolution fusion | flops 2953838592 | bytes 15597568 | tf_op jit(solution)/shard_map/dot_general | solution.py:25
  408.8 14.3 %multiply_reduce_fusion.5 = (f32[2048]{0:T(1024)S(1)}, f32[2048]{0:T(1024)S(1)}, f32[2048]{0:T(1024)S(1)}, f32[2048]{0:T(1024)S(1)}, bf16[512,2048]{1,0:T(8,128)(2,1)}, /*index=5*/bf16[512,2048]{1,0:T(8,128)(2,1)}) fusion(f32[512,2048]{1,0:T(8,128)S(1)} %copy-done.1, bf16[2048,2048]{1,0:T(8,128)(2,1)} %copy-done.2, f32[512,2048]{1,0:T(8,128)} %fusion.20, ...), kind=kOutput, calls=%fused_computation.14 | convolution fusion | flops 2968510464 | bytes 36601856 | tf_op jit(solution)/shard_map/dot_general | solution.py:25
  431.9 16.0 %fusion.62 = bf16[2048,1408]{1,0:T(8,128)(2,1)S(1)} fusion(bf16[2048,2048]{1,0:T(8,128)(2,1)} %copy-done.2, bf16[2048,1408]{1,0:T(8,128)(2,1)S(1)} %bitcast.87), kind=kOutput, calls=%fused_computation.170 | convolution fusion | flops 11811160064 | bytes 19922944 | tf_op jit(solution)/shard_map/dot_general | solution.py:29
  461.2 9.6 %collective-permute-done.35 = bf16[256,1296]{0,1:T(8,128)(2,1)S(1)} collective-permute-done((bf16[256,1296]{0,1:T(8,128)(2,1)}, bf16[256,1296]{0,1:T(8,128)(2,1)S(1)}, u32[]{:S(2)}, u32[]{:S(2)}) %collective-permute-start.35) | collective-permute-done | bytes 663584 | tf_op jit(solution)/shard_map/ppermute | solution.py:53
  477.7 7.5 %convert_add_fusion.1.refs_1_ = f32[512,2048]{1,0:T(8,128)} fusion(bf16[512,2048]{1,0:T(8,128)(2,1)} %collective-permute-done.17, bf16[2048,1024]{1,0:T(8,128)(2,1)} %all-gather.5.cloned.1.call-done, bf16[2048,1024]{1,0:T(8,128)(2,1)} %copy-done.7), kind=kOutput, calls=%fused_computation.18 | convolution fusion | flops 2151677952 | bytes 11534336 | tf_op jit(solution)/shard_map/dot_general | solution.py:25
  503.5 6.9 %add_convert_fusion.1 = bf16[512,2048]{1,0:T(8,128)(2,1)} fusion(bf16[512,2048]{1,0:T(8,128)(2,1)} %collective-permute-done.15, bf16[2048,1024]{1,0:T(8,128)(2,1)} %all-gather.5.cloned.1.call-done, bf16[2048,1024]{1,0:T(8,128)(2,1)} %copy-done.7), kind=kOutput, calls=%fused_computation.19 | convolution fusion | flops 2152726528 | bytes 9437184 | tf_op jit(solution)/shard_map/dot_general | solution.py:25
  533.1 6.7 %collective-permute-done.38 = bf16[256,1296]{0,1:T(8,128)(2,1)S(1)} collective-permute-done((bf16[256,1296]{0,1:T(8,128)(2,1)S(1)}, bf16[256,1296]{0,1:T(8,128)(2,1)S(1)}, u32[]{:S(2)}, u32[]{:S(2)}) %collective-permute-start.38) | collective-permute-done | bytes 663584 | tf_op jit(solution)/shard_map/ppermute | solution.py:53
  555.3 8.3 %input_gradient.1 = bf16[512,2048]{1,0:T(8,128)(2,1)} custom-call(bf16[512,2048]{1,0:T(8,128)(2,1)} %u_ref.5, bf16[512,2048]{1,0:T(8,128)(2,1)} %cot_ref.3, f32[1,2048]{1,0:T(1,128)} %bitcast.104, bf16[512,2048]{1,0:T(8,128)(2,1)} %collective-permute-done.24.refs_0_, f32[512,2048]{1,0:T(8,128)} %convert_add_fusion.refs_1_), custom_call_target="tpu_custom_call" | custom-call | tf_op jit(solution)/shard_map/input_gradient/pallas_call | solution.py:528
  (320 shorter events, 214.9 us)
Async XLA Ops:
  7.2 193.6 %all-gather.3.cloned.1.call-start = ((), (), s32[]{:S(2)}) async-start(), calls=%async_computation.2 | async-start | bytes 4718592 | tf_op jit(solution)/shard_map/all_gather | solution.py:121
  16.5 211.8 %all-gather.5.cloned.1.call-start = ((), (), s32[]{:S(2)}) async-start(), calls=%async_computation.3 | async-start | bytes 4718592 | tf_op jit(solution)/shard_map/all_gather | solution.py:121
  24.1 49.4 %collective-permute-start = (bf16[512,2048]{1,0:T(8,128)(2,1)}, bf16[512,2048]{1,0:T(8,128)(2,1)}, u32[]{:S(2)}, u32[]{:S(2)}) collective-permute-start(bf16[512,2048]{1,0:T(8,128)(2,1)} %get-tuple-element.23), channel_id=1, source_target_pairs={{0,1},{1,0},{2,3},{3,2},{4,5},{5,4},{6,7},{7,6},{8,9},{9,8},{10,11... | collective-permute-start | bytes 6291464 | tf_op jit(solution)/shard_map/ppermute | solution.py:66
  26.9 36.9 %collective-permute-start.14 = (bf16[128,1024]{1,0:T(8,128)(2,1)S(1)}, bf16[128,1024]{1,0:T(8,128)(2,1)S(1)}, u32[]{:S(2)}, u32[]{:S(2)}) collective-permute-start(bf16[128,1024]{1,0:T(8,128)(2,1)S(1)} %bitcast.97), channel_id=1, source_target_pairs={{0,2},{2,0},{4,6},{6,4},{8,10},{10,8},{12,14},{14,12},{16,18},{18,... | collective-permute-start | bytes 786440 | tf_op jit(solution)/shard_map/ppermute | solution.py:53
  27.1 105.9 %collective-permute-start.18 = (bf16[512,2048]{1,0:T(8,128)(2,1)}, bf16[512,2048]{1,0:T(8,128)(2,1)}, u32[]{:S(2)}, u32[]{:S(2)}) collective-permute-start(bf16[512,2048]{1,0:T(8,128)(2,1)} %get-tuple-element.25), channel_id=1, source_target_pairs={{0,1},{1,0},{2,3},{3,2},{4,5},{5,4},{6,7},{7,6},{8,9},{9,8},{10,11... | collective-permute-start | bytes 6291464 | tf_op jit(solution)/shard_map/ppermute | solution.py:66
  32.0 31.4 %collective-permute-start.5 = (bf16[256,1296]{0,1:T(8,128)(2,1)S(1)}, bf16[256,1296]{0,1:T(8,128)(2,1)}, u32[]{:S(2)}, u32[]{:S(2)}) collective-permute-start(bf16[256,1296]{0,1:T(8,128)(2,1)S(1)} %copy.97), channel_id=1, source_target_pairs={{0,8},{2,10},{4,12},{6,14},{8,16},{10,18},{12,20},{14,22},{16,24},... | collective-permute-start | bytes 1990664 | tf_op jit(solution)/shard_map/ppermute | solution.py:53
  34.7 31.7 %collective-permute-start.4 = (bf16[256,1296]{0,1:T(8,128)(2,1)S(1)}, bf16[256,1296]{0,1:T(8,128)(2,1)S(1)}, u32[]{:S(2)}, u32[]{:S(2)}) collective-permute-start(bf16[256,1296]{0,1:T(8,128)(2,1)S(1)} %copy.97), channel_id=1, source_target_pairs={{0,4},{2,6},{4,0},{6,2},{8,12},{10,14},{12,8},{14,10},{16,20},{18,... | collective-permute-start | bytes 1990664 | tf_op jit(solution)/shard_map/ppermute | solution.py:53
  63.4 33.2 %collective-permute-start.7 = (bf16[256,1296]{0,1:T(8,128)(2,1)}, bf16[256,1296]{0,1:T(8,128)(2,1)}, u32[]{:S(2)}, u32[]{:S(2)}) collective-permute-start(bf16[256,1296]{0,1:T(8,128)(2,1)} %collective-permute-done.5), channel_id=1, source_target_pairs={{0,8},{2,10},{4,12},{6,14},{8,16},{10,18},{12,20},{14,22},{16,24},... | collective-permute-start | bytes 1990664 | tf_op jit(solution)/shard_map/ppermute | solution.py:53
  63.9 33.8 %collective-permute-start.6 = (bf16[256,1296]{0,1:T(8,128)(2,1)}, bf16[256,1296]{0,1:T(8,128)(2,1)}, u32[]{:S(2)}, u32[]{:S(2)}) collective-permute-start(bf16[256,1296]{0,1:T(8,128)(2,1)} %collective-permute-done.5), channel_id=1, source_target_pairs={{0,4},{2,6},{4,0},{6,2},{8,12},{10,14},{12,8},{14,10},{16,20},{18,... | collective-permute-start | bytes 1990664 | tf_op jit(solution)/shard_map/ppermute | solution.py:53
  66.4 85.2 %collective-permute-start.2 = (bf16[512,2048]{1,0:T(8,128)(2,1)}, bf16[512,2048]{1,0:T(8,128)(2,1)}, u32[]{:S(2)}, u32[]{:S(2)}) collective-permute-start(bf16[512,2048]{1,0:T(8,128)(2,1)} %get-tuple-element.23), channel_id=1, source_target_pairs={{0,2},{2,0},{4,6},{6,4},{8,10},{10,8},{12,14},{14,12},{16,18},{18,... | collective-permute-start | bytes 6291464 | tf_op jit(solution)/shard_map/ppermute | solution.py:53
  73.5 78.1 %collective-permute-start.1 = (bf16[512,2048]{1,0:T(8,128)(2,1)}, bf16[512,2048]{1,0:T(8,128)(2,1)}, u32[]{:S(2)}, u32[]{:S(2)}) collective-permute-start(bf16[512,2048]{1,0:T(8,128)(2,1)} %collective-permute-done), channel_id=1, source_target_pairs={{0,2},{2,0},{4,6},{6,4},{8,10},{10,8},{12,14},{14,12},{16,18},{18,... | collective-permute-start | bytes 6291464 | tf_op jit(solution)/shard_map/ppermute | solution.py:53
  74.4 499.3 %reduce-scatter.5.cloned.1.call-start = ((), (), s32[]{:S(2)}) async-start(), calls=%async_computation.5 | async-start | bytes 4718592 | tf_op jit(solution)/shard_map/reduce_scatter | solution.py:125
  96.5 31.3 %collective-permute-start.9 = (bf16[256,1296]{0,1:T(8,128)(2,1)}, bf16[256,1296]{0,1:T(8,128)(2,1)}, u32[]{:S(2)}, u32[]{:S(2)}) collective-permute-start(bf16[256,1296]{0,1:T(8,128)(2,1)} %collective-permute-done.7), channel_id=1, source_target_pairs={{0,8},{2,10},{4,12},{6,14},{8,16},{10,18},{12,20},{14,22},{16,24},... | collective-permute-start | bytes 1990664 | tf_op jit(solution)/shard_map/ppermute | solution.py:53
  97.7 35.4 %collective-permute-start.8 = (bf16[256,1296]{0,1:T(8,128)(2,1)}, bf16[256,1296]{0,1:T(8,128)(2,1)}, u32[]{:S(2)}, u32[]{:S(2)}) collective-permute-start(bf16[256,1296]{0,1:T(8,128)(2,1)} %collective-permute-done.7), channel_id=1, source_target_pairs={{0,4},{2,6},{4,0},{6,2},{8,12},{10,14},{12,8},{14,10},{16,20},{18,... | collective-permute-start | bytes 1990664 | tf_op jit(solution)/shard_map/ppermute | solution.py:53
  133.0 88.7 %collective-permute-start.20 = (bf16[512,2048]{1,0:T(8,128)(2,1)S(1)}, bf16[512,2048]{1,0:T(8,128)(2,1)}, u32[]{:S(2)}, u32[]{:S(2)}) collective-permute-start(bf16[512,2048]{1,0:T(8,128)(2,1)S(1)} %copy-done.11), channel_id=1, source_target_pairs={{0,2},{2,0},{4,6},{6,4},{8,10},{10,8},{12,14},{14,12},{16,18},{18,... | collective-permute-start | bytes 6291464 | tf_op jit(solution)/shard_map/ppermute | solution.py:53
  133.1 88.6 %collective-permute-start.19 = (bf16[512,2048]{1,0:T(8,128)(2,1)}, bf16[512,2048]{1,0:T(8,128)(2,1)}, u32[]{:S(2)}, u32[]{:S(2)}) collective-permute-start(bf16[512,2048]{1,0:T(8,128)(2,1)} %collective-permute-done.18), channel_id=1, source_target_pairs={{0,2},{2,0},{4,6},{6,4},{8,10},{10,8},{12,14},{14,12},{16,18},{18,... | collective-permute-start | bytes 6291464 | tf_op jit(solution)/shard_map/ppermute | solution.py:53
  279.4 296.8 %reduce-scatter.3.cloned.1.call-start = ((), (), s32[]{:S(2)}) async-start(), calls=%async_computation.4 | async-start | bytes 4718592 | tf_op jit(solution)/shard_map/reduce_scatter | solution.py:125
  344.9 128.7 %collective-permute-start.17 = (bf16[512,2048]{1,0:T(8,128)(2,1)}, bf16[512,2048]{1,0:T(8,128)(2,1)}, u32[]{:S(2)}, u32[]{:S(2)}) collective-permute-start(bf16[512,2048]{1,0:T(8,128)(2,1)} %convolution_convert_fusion.2), channel_id=1, source_target_pairs={{0,2},{2,0},{4,6},{6,4},{8,10},{10,8},{12,14},{14,12},{16,18},{18,... | collective-permute-start | bytes 6291464 | tf_op jit(solution)/shard_map/ppermute | solution.py:53
  431.7 67.4 %collective-permute-start.15 = (bf16[512,2048]{1,0:T(8,128)(2,1)}, bf16[512,2048]{1,0:T(8,128)(2,1)}, u32[]{:S(2)}, u32[]{:S(2)}) collective-permute-start(bf16[512,2048]{1,0:T(8,128)(2,1)} %convolution_convert_fusion.4), channel_id=1, source_target_pairs={{0,2},{2,0},{4,6},{6,4},{8,10},{10,8},{12,14},{14,12},{16,18},{18,... | collective-permute-start | bytes 6291464 | tf_op jit(solution)/shard_map/ppermute | solution.py:53
  447.9 107.4 %collective-permute-start.24 = (bf16[512,2048]{1,0:T(8,128)(2,1)S(1)}, bf16[512,2048]{1,0:T(8,128)(2,1)}, u32[]{:S(2)}, u32[]{:S(2)}) collective-permute-start(bf16[512,2048]{1,0:T(8,128)(2,1)S(1)} %copy-done.4), channel_id=1, source_target_pairs={{0,1},{1,0},{2,3},{3,2},{4,5},{5,4},{6,7},{7,6},{8,9},{9,8},{10,11... | collective-permute-start | bytes 6291464 | tf_op jit(solution)/shard_map/ppermute | solution.py:66
  459.0 30.2 %collective-permute-start.34 = (bf16[256,1296]{0,1:T(8,128)(2,1)}, bf16[256,1296]{0,1:T(8,128)(2,1)}, u32[]{:S(2)}, u32[]{:S(2)}) collective-permute-start(bf16[256,1296]{0,1:T(8,128)(2,1)} %copy.117), channel_id=1, source_target_pairs={{0,4},{2,6},{4,0},{6,2},{8,12},{10,14},{12,8},{14,10},{16,20},{18,... | collective-permute-start | bytes 1990664 | tf_op jit(solution)/shard_map/ppermute | solution.py:53
  489.2 41.7 %collective-permute-start.32 = (bf16[256,1296]{0,1:T(8,128)(2,1)}, bf16[256,1296]{0,1:T(8,128)(2,1)}, u32[]{:S(2)}, u32[]{:S(2)}) collective-permute-start(bf16[256,1296]{0,1:T(8,128)(2,1)} %copy.113), channel_id=1, source_target_pairs={{0,4},{2,6},{4,0},{6,2},{8,12},{10,14},{12,8},{14,10},{16,20},{18,... | collective-permute-start | bytes 1990664 | tf_op jit(solution)/shard_map/ppermute | solution.py:53
  510.4 39.8 %collective-permute-start.25 = (bf16[512,2048]{1,0:T(8,128)(2,1)}, bf16[512,2048]{1,0:T(8,128)(2,1)}, u32[]{:S(2)}, u32[]{:S(2)}) collective-permute-start(bf16[512,2048]{1,0:T(8,128)(2,1)} %get-tuple-element.102), channel_id=1, source_target_pairs={{0,2},{2,0},{4,6},{6,4},{8,10},{10,8},{12,14},{14,12},{16,18},{18,... | collective-permute-start | bytes 6291464 | tf_op jit(solution)/shard_map/ppermute | solution.py:53
  512.0 51.6 %collective-permute-start.16 = (bf16[512,2048]{1,0:T(8,128)(2,1)}, bf16[512,2048]{1,0:T(8,128)(2,1)}, u32[]{:S(2)}, u32[]{:S(2)}) collective-permute-start(bf16[512,2048]{1,0:T(8,128)(2,1)} %add_convert_fusion.1), channel_id=1, source_target_pairs={{0,1},{1,0},{2,3},{3,2},{4,5},{5,4},{6,7},{7,6},{8,9},{9,8},{10,11... | collective-permute-start | bytes 6291464 | tf_op jit(solution)/shard_map/ppermute | solution.py:66
  (57 other events, 704.0 us)
Sparse Core Ops, SparseCore 0:
  16.6 114.0 all-gather.2
  133.4 71.4 all-gather.4
  279.5 86.1 reduce-scatter.4
  369.7 91.1 reduce-scatter.2

commit v3 on v2

--- a/solution.py
+++ b/solution.py
@@ -15,6 +15,11 @@
 BF16 = jnp.bfloat16
 NEG = -1e30
 HIGH = lax.Precision.HIGHEST
+MICRO = 10**9
+
+
+def busy(flops, scale=1.0):
+    return pl.CostEstimate(flops=int(flops * scale), transcendentals=0, bytes_accessed=0)
 
 
 def dot_nn(a, b):
@@ -65,52 +70,124 @@
         pairs = [(i, (i + g) % self.n) for i in range(self.n)]
         return lax.ppermute(value, "fsdp", pairs)
 
-    def slot_chip(self, k):
-        f, s = k // self.zs, k % self.zs
+    def place(self, f, s):
         return ((self.z - s) % self.zs) * self.ys + (self.y - f) % self.ys
 
-    def all_sum(self, value, axis, bits):
-        for bit in bits:
-            size = self.dp if axis == "dp" else self.n
-            value = value + lax.ppermute(value, axis, [(i, i ^ bit) for i in range(size)])
+    def chip_sum(self, value):
+        pieces = jnp.zeros((self.slots,) + value.shape, value.dtype)
+        for s in range(self.zs):
+            for f in range(self.ys):
+                here = value
+                if s or f:
+                    here = self._dp(
+                        value, lambda z, y, c: ((z + s) % self.zs, (y + f) % self.ys, c)
+                    )
+                pieces = lax.dynamic_update_slice_in_dim(pieces, here[None], self.place(f, s), 0)
+        return jnp.sum(pieces, axis=0)
+
+    def chip_sum(self, value):
+        bit = 2
+        while bit < self.dp:
+            value = value + lax.ppermute(value, "dp", [(i, i ^ bit) for i in range(self.dp)])
+            bit *= 2
         return value
 
-    def dp_bits(self):
-        return [1 << i for i in range(1, self.dp.bit_length() - 1)]
-
-    def fsdp_bits(self):
-        return [1 << i for i in range(self.n.bit_length() - 1)]
-
-
-def gather_blocks(grid, block):
+    def group_parts(self, value):
+        near = [value] + [self.send_x(value, g) for g in range(1, self.n)]
+        pieces = jnp.zeros((self.n * 2,) + value.shape, value.dtype)
+        for g, here in enumerate(near):
+            place = ((self.j - g) % self.n) * 2
+            pieces = lax.dynamic_update_slice_in_dim(pieces, here[None], place + self.core, 0)
+            there = self.swap_core(here)
+            pieces = lax.dynamic_update_slice_in_dim(pieces, there[None], place + 1 - self.core, 0)
+        return pieces
+
+
+def gather_ring(grid, block):
     rows = block.shape[0]
     out = jnp.zeros((grid.slots * rows,) + block.shape[1:], block.dtype)
-    piece = block
+    along, crossed = [block], ()
     for s in range(grid.zs):
-        moved = grid.send_z(piece, 1) if s + 1 < grid.zs else None
-        for f in range(grid.ys):
-            here = grid.send_y(piece, f) if f else piece
-            out = lax.dynamic_update_slice_in_dim(
-                out, here, grid.slot_chip(f * grid.zs + s) * rows, 0
-            )
-        piece = moved
-    return out
-
-
-def scatter_blocks(grid, value):
-    rows = value.shape[0] // grid.slots
-    total = None
-    for s in range(grid.zs - 1, -1, -1):
-        piece = lambda f: lax.dynamic_slice_in_dim(
-            value, grid.slot_chip(f * grid.zs + s) * rows, rows, 0
-        )
-        part = piece(0).astype(F32)
-        for f in range(1, grid.ys):
-            part = part + grid.send_y(piece(f), -f).astype(F32)
-        if total is not None:
-            part = part + grid.send_z(total.astype(BF16), -1).astype(F32)
-        total = part
-    return total
+        piece = along[s]
+        waits = crossed
+        if waits:
+            piece = tie(piece, *waits)
+            along[s] = piece
+        if s + 1 < grid.zs:
+            along.append(grid.send_z(piece, 1))
+        crossed = tuple(grid.send_y(piece, f) for f in range(1, grid.ys))
+        for f, here in enumerate((piece,) + crossed):
+            out = lax.dynamic_update_slice_in_dim(out, here, grid.place(f, s) * rows, 0)
+    return along, out
+
+
+def add_kernel(place_ref, *refs):
+    total = refs[0][...].astype(F32)
+    for ref in refs[1:-1]:
+        total = total + ref[...].astype(F32)
+    refs[-1][...] = total.astype(refs[-1].dtype)
+
+
+def add_rows(place, value, moved, dtype):
+    rows, cols = value.shape[0], value.shape[1]
+    size = moved[0][2]
+    step = size // 2
+    spec = lambda block: pl.BlockSpec((step, cols), lambda i, _: (2 * block + i, 0))
+    return pl.pallas_call(
+        add_kernel,
+        grid_spec=pltpu.PrefetchScalarGridSpec(
+            num_scalar_prefetch=1,
+            grid=(2,),
+            in_specs=[pl.BlockSpec((step, cols), lambda i, at: (2 * at[0] + i, 0))]
+            + [spec(block) for _, block, _ in moved],
+            out_specs=pl.BlockSpec((step, cols), lambda i, _: (i, 0)),
+        ),
+        out_shape=jax.ShapeDtypeStruct((size, cols), dtype),
+        cost_estimate=busy(MICRO),
+        name="add_rows",
+    )(place, value, *[array for array, _, _ in moved])
+
+
+class ScatterX:
+    def __init__(self, grid, value):
+        self.grid, self.value = grid, value
+        self.rows = value.shape[0] // grid.slots
+        steps = list(range(grid.zs - 1, -1, -1))
+        cut = (grid.zs + 1) // 2
+        self.come = {}
+        for group in (steps[:cut], steps[cut:]):
+            arrived = [
+                grid.send_y(
+                    jnp.concatenate(
+                        [
+                            lax.dynamic_slice_in_dim(
+                                value, grid.place(f, s) * self.rows, self.rows, 0
+                            )
+                            for s in group
+                        ],
+                        axis=0,
+                    ),
+                    -f,
+                )
+                for f in range(1, grid.ys)
+            ]
+            for i, s in enumerate(group):
+                self.come[s] = [(array, i, self.rows) for array in arrived]
+        self.sums = []
+
+    def send(self, s, *waits):
+        place = self.grid.place(0, s).astype(jnp.int32).reshape(1)
+        part = add_rows(place, self.value, self.come[s], BF16 if s else F32)
+        if s:
+            part = self.grid.send_z(tie(part, *waits) if waits else part, -s)
+        self.sums.append(part)
+        return part
+
+    def total(self):
+        total = self.sums[-1].astype(F32)
+        for part in self.sums[:-1]:
+            total = total + part.astype(F32)
+        return total
 
 
 def core_groups(grid):
@@ -124,7 +201,7 @@
 def scatter_all(grid, value):
     return lax.psum_scatter(
         value, "dp", scatter_dimension=0, tiled=True, axis_index_groups=core_groups(grid)
-    ).astype(F32)
+    )
 
 
 def shift_down(value, by):
@@ -396,6 +473,7 @@
             jax.ShapeDtypeStruct((rows, inner), F32),
             jax.ShapeDtypeStruct((seqs * inner, LANES), BF16),
         ],
+        cost_estimate=busy(25 * MICRO),
         name="scan_forward",
     )(limits, xb, taps, heads, skip, *waits)
 
@@ -449,11 +527,13 @@
             jax.ShapeDtypeStruct((8, LANES), F32),
         ],
         input_output_aliases={8: 0} if aliased else {},
+        cost_estimate=busy(15 * count * MICRO),
         name="scan_backward",
     )(limits, xb, y, dy, s1, taps, heads, skip, *([d_xb] if aliased else []), *waits)
 
 
-def prepare_kernel(length_ref, u_ref, cot_ref, gain_ref, normed_ref, branch_ref):
+def prepare_kernel(length_ref, u_ref, cot_ref, gain_ref, *refs):
+    normed_ref, branch_ref = refs[-2:]
     rows, _ = u_ref.shape
     u = u_ref[...].astype(F32)
     rstd = lax.rsqrt(jnp.mean(u * u, axis=-1, keepdims=True) + 1e-05)
@@ -463,7 +543,7 @@
     branch_ref[...] = jnp.where(valid, cot_ref[...].astype(F32), 0.0).astype(BF16)
 
 
-def run_prepare(lengths, tokens, cotangent, gain):
+def run_prepare(lengths, tokens, cotangent, gain, waits):
     slot, width = tokens.shape
     step = slot // 4
     per = pl.BlockSpec((step, width), lambda i, *_: (i, 0))
@@ -472,12 +552,78 @@
         grid_spec=pltpu.PrefetchScalarGridSpec(
             num_scalar_prefetch=1,
             grid=(4,),
-            in_specs=[per, per, pl.BlockSpec((1, width), lambda i, *_: (0, 0))],
+            in_specs=[per, per, pl.BlockSpec((1, width), lambda i, *_: (0, 0))]
+            + [pl.BlockSpec(memory_space=pl.ANY)] * len(waits),
             out_specs=[per, per],
         ),
         out_shape=[jax.ShapeDtypeStruct((slot, width), BF16)] * 2,
+        cost_estimate=busy(5 * MICRO),
         name="prepare_rows",
-    )(lengths, tokens, cotangent, gain)
+    )(lengths, tokens, cotangent, gain, *waits)
+
+
+def back_kernel(waits, dz_ref, dxb_ref, wz_ref, wx_ref, normed_ref, *refs):
+    refs = refs[waits:]
+    part = dot_nt(dz_ref[...], wz_ref[...]) + dot_nt(dxb_ref[...], wx_ref[...])
+    slot = refs[0].shape[0]
+    for i, ref in enumerate(refs[:-1]):
+        ref[...] = part[i * slot : (i + 1) * slot].astype(BF16)
+    product = part * normed_ref[...].astype(F32)
+    refs[-1][...] = jnp.sum(product.reshape(-1, 8, product.shape[1]), axis=0)
+
+
+def run_back(dz, dxb, wz, wx, normed, slot, first, waits=()):
+    width, inner = wz.shape
+    cols = wx.shape[1]
+    step = 256
+    rows = 2 * slot
+    block = first // 2
+    tall = lambda size: pl.BlockSpec((rows, size), lambda i: (block, 0))
+    return pl.pallas_call(
+        functools.partial(back_kernel, len(waits)),
+        grid=(width // step,),
+        in_specs=[
+            tall(inner),
+            tall(cols),
+            pl.BlockSpec((step, inner), lambda i: (i, 0)),
+            pl.BlockSpec((step, cols), lambda i: (i, 0)),
+            pl.BlockSpec((rows, step), lambda i: (block, i)),
+        ]
+        + [pl.BlockSpec(memory_space=pl.ANY)] * len(waits),
+        out_specs=[pl.BlockSpec((slot, step), lambda i: (0, i))] * 2
+        + [pl.BlockSpec((8, step), lambda i: (0, i))],
+        out_shape=[jax.ShapeDtypeStruct((slot, width), BF16)] * 2
+        + [jax.ShapeDtypeStruct((8, width), F32)],
+        cost_estimate=busy(0),
+        name="normed_gradient",
+    )(dz, dxb, wz, wx, normed, *waits)
+
+
+def branch_kernel(waits, gnorm_ref, wo_ref, *refs):
+    refs = refs[waits:]
+    part = dot_nt(gnorm_ref[...], wo_ref[...])
+    slot = refs[0].shape[0]
+    for i, ref in enumerate(refs):
+        ref[...] = part[i * slot : (i + 1) * slot].astype(BF16)
+
+
+def run_branch(gnorm, wo, slot, first, waits=()):
+    width, inner = wo.shape
+    step = 256
+    block = first // 2
+    return pl.pallas_call(
+        functools.partial(branch_kernel, len(waits)),
+        grid=(width // step,),
+        in_specs=[
+            pl.BlockSpec((2 * slot, inner), lambda i: (block, 0)),
+            pl.BlockSpec((step, inner), lambda i: (i, 0)),
+        ]
+        + [pl.BlockSpec(memory_space=pl.ANY)] * len(waits),
+        out_specs=[pl.BlockSpec((slot, step), lambda i: (0, i))] * 2,
+        out_shape=[jax.ShapeDtypeStruct((slot, width), BF16)] * 2,
+        cost_estimate=busy(0),
+        name="branch_rows",
+    )(gnorm, wo, *waits)
 
 
 def output_kernel(count, length_ref, u_ref, *refs):
@@ -517,6 +663,7 @@
             out_specs=per,
         ),
         out_shape=jax.ShapeDtypeStruct((slot, width), BF16),
+        cost_estimate=busy(5 * MICRO),
         name="layer_output",
     )(lengths, tokens, *parts)
 
@@ -531,6 +678,7 @@
         in_specs=[per, per, pl.BlockSpec((1, width), lambda i: (0, 0))] + [per] * len(parts),
         out_specs=per,
         out_shape=jax.ShapeDtypeStruct((slot, width), BF16),
+        cost_estimate=busy(8 * MICRO),
         name="input_gradient",
     )(tokens, cotangent, gain, *parts)
 
@@ -566,7 +714,7 @@
     channel_base = part * inner
     head_base = part * heads
     cols = inner + 3 * LANES
-    sent = inner + state2 + heads
+    spare = cols - inner - state2 - heads
 
     def halves(value, axis):
         size = value.shape[axis] // 2
@@ -579,44 +727,41 @@
         second = jnp.where(core == 0, other, mine)
         return jnp.concatenate([first, second], axis=axis)
 
-    gain_row = norm_gain[None]
-    normed_own, d_branch_own = run_prepare(lengths, tokens, cotangent, gain_row)
-
+    def swapped(mine, other, *waits):
+        return by_core(mine, grid.swap_core(tie(other, *waits) if waits else other), 0)
+
+    fill = jnp.zeros((rows_d, spare), BF16)
     x_mine, x_other = halves(w_zx[:, 1], 1)
     t_mine, t_other = halves(w_dt, 1)
-    x_mine = jnp.concatenate([x_mine, w_bc, t_mine], axis=1)
-    x_other = jnp.concatenate([x_other, w_bc, t_other], axis=1)
-    block_x = by_core(x_mine, grid.swap_core(x_other), 0)
+    x_mine = jnp.concatenate([x_mine, w_bc, t_mine, fill], axis=1)
+    x_other = jnp.concatenate([x_other, w_bc, t_other, fill], axis=1)
+    block_x = swapped(x_mine, x_other)
+    gain_row = norm_gain[None]
+    normed_own, d_branch_own = run_prepare(
+        lengths, tokens, cotangent, gain_row, (x_other,)
+    )
     z_mine, z_other = halves(w_zx[:, 0], 1)
-    block_z = by_core(z_mine, grid.swap_core(z_other), 0)
+    block_z = swapped(z_mine, z_other, normed_own)
     o_mine, o_other = halves(w_out.T, 1)
-    block_o = by_core(o_mine, grid.swap_core(o_other), 0)
-    w_x = gather_blocks(grid, block_x)
-    w_z = gather_all(grid, block_z)
+    block_o = swapped(o_mine, o_other, normed_own)
+    arriving = [grid.send_x(normed_own, g) for g in range(1, n)]
+    along, w_x = gather_ring(grid, block_x)
+    arriving = [tie(value, along[-1]) for value in arriving]
+    w_z = gather_all(grid, tie(block_z, along[1]))
     w_o = gather_all(grid, block_o)
-    w_x = jnp.pad(w_x, ((0, 0), (0, cols - sent)))
 
     order = [(g, e) for g in range(n - 1, -1, -1) for e in (1, 0)]
     index = lax.axis_index("dp")
     owners = [(index + e * (1 - 2 * core)) * n + (j - g) % n for g, e in order]
 
-    def share(value):
-        near = [value] + [grid.send_x(value, g) for g in range(1, n)]
+    def share(value, arriving):
+        near = [value] + arriving
         far = [grid.swap_core(piece) for piece in near]
         pieces = [far[g] if e else near[g] for g, e in order]
         return lax.optimization_barrier(jnp.concatenate(pieces, axis=0))
 
-    def collect(parts):
-        kept = []
-        for i in range(0, len(parts), 2):
-            g = order[i][0]
-            there = grid.swap_core(parts[i])
-            both = parts[i + 1].astype(F32) + there.astype(F32)
-            kept.append(grid.send_x(both.astype(BF16), -g) if g else both)
-        return kept
-
-    normed = share(normed_own)
-    d_branch = share(d_branch_own)
+    normed = share(normed_own, arriving)
+    d_branch = share(d_branch_own, [grid.send_x(d_branch_own, g) for g in range(1, n)])
     seqs = len(owners)
     seq_width = jnp.stack([widths[o] for o in owners])
     used = seq_width * ((HEADS // 8) * HEAD_DIM)
@@ -662,9 +807,15 @@
 
     g_o_part = dot_tn(d_branch, gnorm).astype(BF16)
     g_o = scatter_all(grid, g_o_part)
+    w_o = tie(w_o, g_o_part)
     d_gnorm = dot_nn(d_branch, w_o)
     weighted = d_gnorm * own_gain
-    inner_sum = group_sum(jnp.sum(weighted * gated, axis=1))
+    inner_part = jnp.sum(weighted * gated, axis=1)
+    far = seqs - 2
+    out_far = [run_branch(gnorm, w_o, slot, i, (inner_part,)) for i in range(0, far, 2)]
+    inner_sum = group_sum(inner_part)
+    if out_far:
+        inner_sum = tie(inner_sum, *[rows for pair in out_far for rows in pair])
     pull = scale * scale * scale / counts * inner_sum
     d_gated = weighted * scale[:, None] - gated * pull[:, None]
     g_gate = jnp.sum(d_gnorm * gated * scale[:, None], axis=0)
@@ -674,85 +825,83 @@
     g_z_part = dot_tn(normed, d_z).astype(BF16)
     g_z = scatter_all(grid, g_z_part)
 
-    def back(i):
-        part = dot_nt(rows_of(d_z, i), w_z) + dot_nt(rows_of(d_xb, i), w_x)
-        return jnp.sum(part * rows_of(normed, i).astype(F32), axis=0), part.astype(BF16)
-
-    far = seqs - 2
+    cross = lambda values: [
+        grid.send_x(value, -order[2 * i][0]) for i, value in enumerate(values)
+    ]
     d_normed, branch, g_norm_part = [], [], 0.0
+    for out_there, out_here in out_far:
+        out_there = grid.swap_core(out_there)
+        branch.append((out_here.astype(F32) + out_there.astype(F32)).astype(BF16))
     d_xb, g_channels, g_heads = run_bwd(
-        limits, xb, y, d_y, s1, *scan, 0, far, None, (g_o_part, g_z_part)
-    )
-    ahead = [back(i) for i in range(far)]
+        limits, xb, y, d_y, s1, *scan, 0, far, None, (g_o_part, g_z_part, *branch)
+    )
+    branch = cross(branch)
     for i in range(0, far, 2):
-        both = ahead[i + 1][1].astype(F32) + grid.swap_core(ahead[i][1]).astype(F32)
-        d_normed.append(both.astype(BF16))
+        there, here, more = run_back(d_z, d_xb, w_z, w_x, normed, slot, i)
+        g_norm_part = g_norm_part + more
+        there = grid.swap_core(tie(there, *branch))
+        d_normed.append((here.astype(F32) + there.astype(F32)).astype(BF16))
     d_xb, more_channels, more_heads = run_bwd(
-        limits, xb, y, d_y, s1, *scan, far, 2, d_xb, tuple(d_normed)
-    )
-    d_normed = [grid.send_x(d_normed[i], -order[2 * i][0]) for i in range(len(d_normed))]
+        limits, xb, y, d_y, s1, *scan, far, 2, d_xb, (*d_normed, g_o)
+    )
+    d_normed = cross(d_normed)
     g_channels, g_heads = g_channels + more_channels, g_heads + more_heads
-    g_x_part = dot_tn(normed, d_xb)[:, :sent].astype(BF16)
-    g_x = scatter_blocks(grid, g_x_part)
-    out_rows = [dot_nt(rows_of(gnorm, i), w_o).astype(BF16) for i in range(seqs)]
-    branch = collect(out_rows)
-    ahead += [back(i) for i in range(far, seqs)]
-    d_normed.append(ahead[far + 1][1].astype(F32) + grid.swap_core(ahead[far][1]).astype(F32))
-    g_norm_part = sum(part[0] for part in ahead)
+    g_skip = g_channels[5, :inner].reshape(heads, HEAD_DIM).sum(axis=1)
+    mine = jnp.concatenate(
+        [
+            g_channels[:5].reshape(-1),
+            g_gate,
+            jnp.pad(jnp.concatenate([g_heads[0, :heads], g_heads[1, :heads], g_skip]), (0, -3 * heads % LANES)),
+        ]
+    )
+    g_x_part = dot_tn(normed, d_xb).astype(BF16)
+    to_x = ScatterX(grid, g_x_part)
+    there, here, more = run_back(
+        d_z, d_xb, w_z, w_x, normed, slot, far, (g_x_part,)
+    )
+    d_normed += [here, grid.swap_core(there)]
+    out_there, out_here = run_branch(gnorm, w_o, slot, far, (here,))
+    out_there = grid.swap_core(tie(out_there, *d_normed[: far // 2]))
+
+    def to_rows(value):
+        rows = lax.dynamic_slice_in_dim(value, core * rows_d, rows_d, 0)
+        other = lax.dynamic_slice_in_dim(value, (1 - core) * rows_d, rows_d, 0)
+        return rows, grid.swap_core(other)
+
+    o_rows = by_core(*to_rows(g_o.astype(F32)), 1).T
+    z_rows = by_core(*to_rows(g_z.astype(F32)), 1)
+    third = to_x.send(3, out_here, g_z)
+    to_x.send(2, out_here)
+    to_x.send(1)
+    to_x.send(0)
+    g_x = to_x.total()
+    small = mine.shape[0]
+    mine = jnp.concatenate([mine, jnp.sum(g_norm_part + more, axis=0)])
+    mine = jnp.pad(mine, (0, -mine.shape[0] % 1024)).reshape(-1, LANES)
+    mine = grid.chip_sum(tie(mine, third, o_rows, z_rows))
+    branch += [out_here, out_there]
 
     output = run_output(lengths, tokens, branch)
     input_grad = run_grad(tokens, cotangent, gain_row, d_normed)
 
-    def to_rows(value):
-        mine = lax.dynamic_slice_in_dim(value, core * rows_d, rows_d, 0)
-        other = lax.dynamic_slice_in_dim(value, (1 - core) * rows_d, rows_d, 0)
-        return mine, grid.swap_core(other)
-
-    z_rows = by_core(*to_rows(g_z), 1)
-    o_rows = by_core(*to_rows(g_o), 1)
     x_mine, x_recv = to_rows(g_x)
     x_rows = by_core(x_mine[:, :inner], x_recv[:, :inner], 1)
-    t_rows = by_core(x_mine[:, inner + state2 :], x_recv[:, inner + state2 :], 1)
+    t_rows = by_core(x_mine[:, inner + state2 : cols - spare], x_recv[:, inner + state2 : cols - spare], 1)
     bc_rows = (x_mine + x_recv)[:, inner : inner + state2]
     bc_sum = bc_rows
     for g in range(1, n):
         bc_sum = bc_sum + grid.send_x(bc_rows, g)
     g_w_zx = jnp.stack([z_rows, x_rows], axis=1)
 
-    g_skip = g_channels[5, :inner].reshape(heads, HEAD_DIM).sum(axis=1)
-    head_parts = jnp.stack([g_heads[0, :heads], g_heads[1, :heads], g_skip])
-    mine = [
-        g_channels[:5].reshape(-1),
-        g_gate,
-        g_norm_part / norm_gain,
-        head_parts.reshape(-1),
-    ]
-    sizes = [piece.shape[0] for piece in mine]
-    flat = jnp.concatenate(mine)
-    flat = jnp.pad(flat, (0, -flat.shape[0] % 1024)).reshape(-1, LANES)
-    flat = grid.all_sum(flat, "dp", grid.dp_bits()).reshape(-1)
-    own_conv = flat[: sizes[0]].reshape(5, cols)
-    own_gate = flat[sizes[0] : sizes[0] + sizes[1]]
-    own_norm = flat[sizes[0] + sizes[1] : sum(sizes[:3])]
-    own_heads_sum = flat[sum(sizes[:3]) : sum(sizes)].reshape(3, heads)
-    conv_rows = jnp.zeros((5, total), F32)
-    conv_rows = lax.dynamic_update_slice(conv_rows, own_conv[:, :inner], (0, channel_base))
-    conv_rows = lax.dynamic_update_slice(
-        conv_rows, own_conv[:, inner : inner + state2], (0, all_inner)
-    )
-    gate_row = lax.dynamic_update_slice(jnp.zeros((all_inner,), F32), own_gate, (channel_base,))
-    head_all = lax.dynamic_update_slice(
-        jnp.zeros((3, d_skip.shape[0]), F32), own_heads_sum, (0, head_base)
-    )
-    flat = jnp.concatenate([own_norm, conv_rows.reshape(-1), gate_row, head_all.reshape(-1)])
-    size = flat.shape[0]
-    flat = jnp.pad(flat, (0, -size % 1024)).reshape(-1, LANES)
-    flat = grid.all_sum(flat, "dp", [1])
-    flat = grid.all_sum(flat, "fsdp", grid.fsdp_bits()).reshape(-1)[:size]
-    ends = [width, width + 5 * total, width + 5 * total + all_inner]
-    g_norm, g_conv, g_gate, g_small = jnp.split(flat, ends)
-    g_conv = g_conv.reshape(5, total)
-    g_small = g_small.reshape(3, -1)
+    mine = grid.group_parts(mine).reshape(2 * n, -1)
+    conv = mine[:, : 5 * cols].reshape(2 * n, 5, cols)
+    conv_x = jnp.swapaxes(conv[:, :, :inner], 0, 1).reshape(5, all_inner)
+    conv_bc = jnp.sum(conv[:, :, inner : inner + state2], axis=0)
+    g_conv = jnp.concatenate([conv_x, conv_bc], axis=1)
+    g_gate = mine[:, 5 * cols : 5 * cols + inner].reshape(all_inner)
+    g_small = mine[:, 5 * cols + inner : 5 * cols + inner + 3 * heads].reshape(2 * n, 3, heads)
+    g_small = jnp.swapaxes(g_small, 0, 1).reshape(3, -1)
+    g_norm = jnp.sum(mine[:, small : small + width], axis=0) / norm_gain
     return (
         output,
         input_grad,
@@ -760,7 +909,7 @@
         g_w_zx,
         bc_sum,
         t_rows,
-        o_rows.T,
+        o_rows,
         g_conv[:4],
         g_conv[4],
         g_small[0],

time: 603 us -> 574 us (0.952)
  matrix products: 177 us -> 94.2 us
  Pallas kernels: 105 us -> 167 us
  local copies, waits for them, and re-layouts: 74.6 us -> 68.1 us
  starting transfers between devices: 38.8 us -> 45.2 us
    dot_general x12 -> x0, matrix products: 82.6 us -> none  [dot_nt(): lax.dot_general(a, b, (((1,), (1,)), ((), ())), preferred_element_type=F32)]
    pallas_call x0 -> x22, Pallas kernels: none -> 62 us  [the longest x2 33.7 us: run_back(): pl.pallas_call(functools.partial(back_kernel, len(waits)), grid=(width //...]
    ppermute x30, waiting for transfers between devices: 103 us -> 65.2 us  [_dp(): return lax.ppermute(value, 'dp', pairs)]
    reduce_scatter x2, waiting for transfers between devices: 0.04 us -> 19.5 us  [scatter_all(): lax.psum_scatter(value, 'dp', scatter_dimension=0, tiled=True, axis_index...]
    ppermute x14 -> x0, local copies, waits for them, and re-layouts: 18.3 us -> none  [_dp(): return lax.ppermute(value, 'dp', pairs)]
    unnamed x82 -> x101, local copies, waits for them, and re-layouts: 11.4 us -> 29.2 us
    add x7 -> x3, other arithmetic: 12.1 us -> 1.84 us  [the longest x1 1.83 us: total(): total = total + part.astype(F32)]
    ppermute x5 -> x3, starting transfers between devices: 3.69 us -> 11.8 us  [chip_sum(): lax.ppermute(value, 'dp', [(i, i ^ bit) for i in range(self.dp)])]
  transfers between devices with their start and end apart: 46 -> 45, of which waited for: 14 -> 17; matrix products, arithmetic and copies ran while one was open for 43% -> 31% of each run, Pallas kernels for 18% -> 29%
where the time goes in v3:
time: 574 us; the launch traced here: 567 us
  Pallas kernels  167 us (29%)
  waiting for transfers between devices  112 us (20%)
  matrix products  94.2 us (16%)
  local copies, waits for them, and re-layouts  68.1 us (12%)
  other arithmetic  64.4 us (11%)
  starting transfers between devices  45.2 us (8%)
  between operations  15.5 us (3%)
    ppermute x30, waiting for transfers between devices, _dp(): return lax.ppermute(value, 'dp', pairs)  65.2 us
    pallas_call x2, Pallas kernels, run_bwd(): pl.pallas_call(kernel, grid_spec=pltpu.PrefetchScalarGridSpec(num_scalar_...  60.9 us
    dot_general x3, matrix products, dot_nn(): lax.dot_general(a, b, (((1,), (0,)), ((), ())), preferred_element_type=F32)  53.1 us
    dot_general x3, matrix products, dot_tn(): lax.dot_general(a, b, (((0,), (0,)), ((), ())), preferred_element_type=F32)  41 us
    pallas_call x2, Pallas kernels, run_back(): pl.pallas_call(functools.partial(back_kernel, len(waits)), grid=(width //...  33.7 us
    unnamed x101, local copies, waits for them, and re-layouts  29.2 us
    pallas_call x1, Pallas kernels, run_fwd(): pl.pallas_call(functools.partial(fwd_kernel, len(waits)), grid_spec=pltpu...  25 us
    ppermute x30, starting transfers between devices, _dp(): return lax.ppermute(value, 'dp', pairs)  23.1 us
  transfers between devices with their start and end apart: 45, of which 17 were waited for; matrix products, arithmetic and copies ran while one was open for 31% of the time, Pallas kernels for 29%

profile of v3, /device:TPU:0, one launch (start us, length us, event | category | flops | bytes accessed | tf_op | source)
XLA Modules:
  0.0 566.7 jit_solution(264184903321905563)
XLA Ops:
  33.0 6.2 %collective-permute-done.3.refs_1_ = bf16[256,1408]{1,0:T(8,128)(2,1)S(1)} collective-permute-done((bf16[256,1408]{1,0:T(8,128)(2,1)S(1)}, bf16[256,1408]{1,0:T(8,128)(2,1)S(1)}, u32[]{:S(2)}, u32[]{:S(2)}) %collective-permute-start.3) | collective-permute-done | bytes 720928 | tf_op jit(solution)/shard_map/ppermute | solution.py:58
  53.3 14.4 %collective-permute-done.5.refs_1_ = bf16[256,1408]{1,0:T(8,128)(2,1)S(1)} collective-permute-done((bf16[256,1408]{1,0:T(8,128)(2,1)}, bf16[256,1408]{1,0:T(8,128)(2,1)S(1)}, u32[]{:S(2)}, u32[]{:S(2)}) %collective-permute-start.5) | collective-permute-done | bytes 720928 | tf_op jit(solution)/shard_map/ppermute | solution.py:58
  67.7 7.4 %collective-permute-done.4.refs_0_ = bf16[256,1408]{1,0:T(8,128)(2,1)S(1)} collective-permute-done((bf16[256,1408]{1,0:T(8,128)(2,1)}, bf16[256,1408]{1,0:T(8,128)(2,1)S(1)}, u32[]{:S(2)}, u32[]{:S(2)}) %collective-permute-start.4) | collective-permute-done | bytes 720928 | tf_op jit(solution)/shard_map/ppermute | solution.py:58
  92.9 14.8 %collective-permute-done.6.refs_0_ = bf16[256,1408]{1,0:T(8,128)(2,1)S(1)} collective-permute-done((bf16[256,1408]{1,0:T(8,128)(2,1)}, bf16[256,1408]{1,0:T(8,128)(2,1)S(1)}, u32[]{:S(2)}, u32[]{:S(2)}) %collective-permute-start.6) | collective-permute-done | bytes 720928 | tf_op jit(solution)/shard_map/ppermute | solution.py:58
  121.5 14.0 %collective-permute-done.15 = bf16[512,2048]{1,0:T(8,128)(2,1)} collective-permute-done((bf16[512,2048]{1,0:T(8,128)(2,1)}, bf16[512,2048]{1,0:T(8,128)(2,1)}, u32[]{:S(2)}, u32[]{:S(2)}) %collective-permute-start.15) | collective-permute-done | bytes 2097184 | tf_op jit(solution)/shard_map/ppermute | solution.py:71
  143.3 18.6 %fusion.15.xb_ref = f32[2048,1408]{1,0:T(8,128)} fusion(bf16[2048,2048]{1,0:T(8,128)(2,1)S(1)} %pad_maximum_fusion.normed_ref, bf16[2048,1408]{1,0:T(8,128)(2,1)} %constant_dynamic-update-slice_fusion.wx_ref), kind=kOutput, calls=%fused_computation.123 | convolution fusion | flops 11811160064 | bytes 25690112 | tf_op jit(solution)/shard_map/dot_general | solution.py:26
  162.5 25.0 %scan_forward.1 = (f32[2048,1024]{1,0:T(8,128)}, bf16[4096,128]{1,0:T(8,128)(2,1)}) custom-call(s32[4]{0:T(128)} %subtract_clamp_fusion.limit_ref, f32[2048,1408]{1,0:T(8,128)} %fusion.15.xb_ref, f32[8,1408]{1,0:T(8,128)} %select_maximum_fusion.taps_ref, f32[8,128]{1,0:T(8,128)} %select_maximum_fusion.2.heads_ref.refs_0_, ...), custom_call_target="tpu_custom_call" | custom-call | flops 24999999488 | tf_op jit(solution)/shard_map/scan_forward/pallas_call | solution.py:460
  187.6 18.3 %multiply_reduce_fusion.2 = (f32[2048]{0:T(1024)S(1)}, f32[2048,1024]{1,0:T(8,128)}, f32[2048,1024]{1,0:T(8,128)}) fusion(f32[2048,1024]{1,0:T(8,128)} %get-tuple-element.34.y_ref, bf16[2048,2048]{1,0:T(8,128)(2,1)} %copy-done.1, bf16[2048,1024]{1,0:T(8,128)(2,1)} %all-gather.3.cloned.1.call-done.wz_ref), kind=kOutput, calls=%fused_computation.8 | convolution fusion | flops 8604612608 | bytes 37756928 | tf_op jit(solution)/shard_map/dot_general | solution.py:26
  218.9 10.5 %convolution_convert_fusion.2.refs_1_.refs_2_ = bf16[2048,1024]{1,0:T(8,128)(2,1)} fusion(bf16[2048,2048]{1,0:T(8,128)(2,1)S(1)} %pad_maximum_fusion.1, bf16[2048,1024]{1,0:T(8,128)(2,1)S(1)} %multiply_convert_fusion.2.gnorm_ref), kind=kOutput, calls=%fused_computation.15 | convolution fusion | flops 8592031744 | bytes 16777216 | tf_op jit(solution)/shard_map/dot_general | solution.py:34
  229.4 16.3 %multiply_reduce_fusion = (f32[1024]{0:T(1024)S(1)}, f32[2048]{0:T(1024)S(1)}, f32[2048,1024]{1,0:T(8,128)}) fusion(f32[2048,1024]{1,0:T(8,128)} %get-tuple-element.115, f32[2048]{0:T(1024)S(1)} %add_rsqrt_fusion, f32[1024]{0:T(1024)S(1)} %dynamic_slice.111, bf16[2048,2048]{1,0:T(8,128)(2,1)} %copy-done.5, bf16[2048,1024]{1,0:T(8,128)(2,1)} %order.21.wo_ref), kind=kOutput, calls=%fused_computation.2 | convolution fusion | flops 8602514432 | bytes 29384704 | tf_op jit(solution)/shard_map/dot_general | solution.py:26
  248.0 9.8 %branch_rows.2 = (bf16[512,2048]{1,0:T(8,128)(2,1)}, bf16[512,2048]{1,0:T(8,128)(2,1)}) custom-call(bf16[2048,1024]{1,0:T(8,128)(2,1)} %copy-done.2, bf16[2048,1024]{1,0:T(8,128)(2,1)} %order.21.wo_ref, f32[2048]{0:T(1024)} %copy-done.32), custom_call_target="tpu_custom_call" | custom-call | tf_op jit(solution)/shard_map/branch_rows/pallas_call | solution.py:614
  259.3 14.6 %multiply_convert_fusion = (bf16[2048,1024]{1,0:T(8,128)(2,1)}, bf16[2048,1024]{1,0:T(8,128)(2,1)S(1)}) fusion(f32[2048,1024]{1,0:T(8,128)} %get-tuple-element.115, f32[2048]{0:T(1024)S(1)} %fusion.5, f32[2048]{0:T(1024)S(1)} %add_rsqrt_fusion, f32[2048,1024]{1,0:T(8,128)} %get-tuple-element.161, f32[1024]{0:T(1024)S(1)} %dynamic_slice.111, ...), kind=kLoop, calls=%fused_computation.3 | loop fusion | flops 35651584 | bytes 41963520 | tf_op jit(solution)/shard_map/convert_element_type | solution.py:823
  275.9 13.1 %convolution_convert_fusion.1.refs_3_ = bf16[2048,1024]{1,0:T(8,128)(2,1)} fusion(bf16[2048,2048]{1,0:T(8,128)(2,1)} %copy-done.1, bf16[2048,1024]{1,0:T(8,128)(2,1)S(1)} %get-tuple-element.117.dz_ref), kind=kOutput, calls=%fused_computation.14 | convolution fusion | flops 8592031744 | bytes 16777216 | tf_op jit(solution)/shard_map/dot_general | solution.py:34
  294.0 30.7 %scan_backward.2 = (bf16[2048,1408]{1,0:T(8,128)(2,1)}, f32[8,1408]{1,0:T(8,128)}, f32[8,128]{1,0:T(8,128)}) custom-call(s32[4]{0:T(128)} %subtract_clamp_fusion.limit_ref, f32[2048,1408]{1,0:T(8,128)} %fusion.15.xb_ref, f32[2048,1024]{1,0:T(8,128)} %get-tuple-element.34.y_ref, bf16[2048,1024]{1,0:T(8,128)(2,1)} %get-tuple-element.116.dy_ref, ...), custom_call_target="tpu_custom_call" | custom-call | flops 30000001024 | tf_op jit(solution)/shard_map/scan_backward/pallas_call | solution.py:503
  324.7 16.9 %normed_gradient.2 = (bf16[512,2048]{1,0:T(8,128)(2,1)}, bf16[512,2048]{1,0:T(8,128)(2,1)}, f32[8,2048]{1,0:T(8,128)}) custom-call(bf16[2048,1024]{1,0:T(8,128)(2,1)} %copy-done.3, bf16[2048,1408]{1,0:T(8,128)(2,1)} %get-tuple-element.39.dxb_ref.refs_2_, bf16[2048,1024]{1,0:T(8,128)(2,1)} %all-gather.3.cloned.1.call-done.wz_ref, ...), custom_call_target="tpu_custom_call" | custom-call | tf_op jit(solution)/shard_map/normed_gradient/pallas_call | solution.py:582
  359.1 30.2 %scan_backward.3 = (bf16[2048,1408]{1,0:T(8,128)(2,1)}, f32[8,1408]{1,0:T(8,128)}, f32[8,128]{1,0:T(8,128)}) custom-call(s32[4]{0:T(128)} %subtract_clamp_fusion.limit_ref, f32[2048,1408]{1,0:T(8,128)} %fusion.15.xb_ref, f32[2048,1024]{1,0:T(8,128)} %get-tuple-element.34.y_ref, ...), custom_call_target="tpu_custom_call", output_to_operand_aliasing={{0}: (8, {})} | custom-call | flops 30000001024 | tf_op jit(solution)/shard_map/scan_backward/pallas_call | solution.py:503
  389.3 17.4 %convolution_convert_fusion.refs_0_ = bf16[2048,1408]{1,0:T(8,128)(2,1)S(1)} fusion(bf16[2048,2048]{1,0:T(8,128)(2,1)} %copy-done.1, bf16[2048,1408]{1,0:T(8,128)(2,1)} %get-tuple-element.42.dxb_ref), kind=kOutput, calls=%fused_computation.11 | convolution fusion | flops 11814043648 | bytes 19922944 | tf_op jit(solution)/shard_map/dot_general | solution.py:34
  412.3 16.7 %normed_gradient.3 = (bf16[512,2048]{1,0:T(8,128)(2,1)}, bf16[512,2048]{1,0:T(8,128)(2,1)}, f32[8,2048]{1,0:T(8,128)}) custom-call(bf16[2048,1024]{1,0:T(8,128)(2,1)} %copy-done.3, bf16[2048,1408]{1,0:T(8,128)(2,1)} %get-tuple-element.42.dxb_ref, bf16[2048,1024]{1,0:T(8,128)(2,1)} %all-gather.3.cloned.1.call-done.wz_ref, ...), custom_call_target="tpu_custom_call" | custom-call | tf_op jit(solution)/shard_map/normed_gradient/pallas_call | solution.py:582
  430.4 9.9 %branch_rows.3 = (bf16[512,2048]{1,0:T(8,128)(2,1)}, bf16[512,2048]{1,0:T(8,128)(2,1)}) custom-call(bf16[2048,1024]{1,0:T(8,128)(2,1)} %copy-done.2, bf16[2048,1024]{1,0:T(8,128)(2,1)} %order.21.wo_ref, bf16[512,2048]{1,0:T(8,128)(2,1)} %get-tuple-element.43.refs_0_.refs_1_), custom_call_target="tpu_custom_call" | custom-call | tf_op jit(solution)/shard_map/branch_rows/pallas_call | solution.py:614
  442.7 14.4 %reduce-scatter.5.cloned.1.call-done.refs_2_ = bf16[256,1024]{1,0:T(8,128)(2,1)} async-done(((bf16[2048,1024]{1,0:T(8,128)(2,1)}), bf16[256,1024]{1,0:T(8,128)(2,1)}) %reduce-scatter.5.cloned.1.call-update) | async-done | bytes 524304 | tf_op jit(solution)/shard_map/reduce_scatter | solution.py:202
  475.3 10.3 %collective-permute-done.36.refs_1_ = bf16[512,1408]{1,0:T(8,128)(2,1)S(1)} collective-permute-done((bf16[512,1408]{1,0:T(8,128)(2,1)}, bf16[512,1408]{1,0:T(8,128)(2,1)S(1)}, u32[]{:S(2)}, u32[]{:S(2)}) %collective-permute-start.36) | collective-permute-done | bytes 1441824 | tf_op jit(solution)/shard_map/ppermute | solution.py:58
  497.9 8.5 %input_gradient.1 = bf16[512,2048]{1,0:T(8,128)(2,1)} custom-call(bf16[512,2048]{1,0:T(8,128)(2,1)} %u_ref.5, bf16[512,2048]{1,0:T(8,128)(2,1)} %cot_ref.3, f32[1,2048]{1,0:T(1,128)} %bitcast.105, bf16[512,2048]{1,0:T(8,128)(2,1)} %collective-permute-done.23.refs_1_.refs_0_, bf16[512,2048]{1,0:T(8,128)(2,1)} %get-tuple-element.43.refs_0_.refs_1_, ...), custom_call_target="tpu_custom_call" | custom-call | flops 8000000000 | tf_op jit(solution)/shard_map/input_gradient/pallas_call | solution.py:675
  512.1 11.2 %collective-permute-done.31 = f32[80,128]{1,0:T(8,128)S(1)} collective-permute-done((f32[80,128]{1,0:T(8,128)S(1)}, f32[80,128]{1,0:T(8,128)S(1)}, u32[]{:S(2)}, u32[]{:S(2)}) %collective-permute-start.31) | collective-permute-done | bytes 40992 | tf_op jit(solution)/shard_map/ppermute | solution.py:91
  523.3 11.5 %collective-permute-start.32 = (f32[80,128]{1,0:T(8,128)S(1)}, f32[80,128]{1,0:T(8,128)S(1)}, u32[]{:S(2)}, u32[]{:S(2)}) collective-permute-start(f32[80,128]{1,0:T(8,128)S(1)} %add.357), channel_id=1, source_target_pairs={{0,16},{2,18},{4,20},{6,22},{8,24},{10,26},{12,28},{14,30},{16,0},... | collective-permute-start | bytes 122888 | tf_op jit(solution)/shard_map/ppermute | solution.py:91
  (317 shorter events, 190.5 us)
Async XLA Ops:
  7.2 180.3 %all-gather.3.cloned.1.call-start = ((), (), s32[]{:S(2)}) async-start(), calls=%async_computation.2 | async-start | bytes 4718592 | tf_op jit(solution)/shard_map/all_gather | solution.py:198
  43.5 186.0 %all-gather.5.cloned.1.call-start = ((), (), s32[]{:S(2)}) async-start(), calls=%async_computation.3 | async-start | bytes 4718592 | tf_op jit(solution)/shard_map/all_gather | solution.py:198
  43.5 65.0 %collective-permute-start = (bf16[512,2048]{1,0:T(8,128)(2,1)}, bf16[512,2048]{1,0:T(8,128)(2,1)S(1)}, u32[]{:S(2)}, u32[]{:S(2)}) collective-permute-start(bf16[512,2048]{1,0:T(8,128)(2,1)} %get-tuple-element.33.refs_1_), channel_id=1, source_target_pairs={{0,1},{1,0},{2,3},{3,2},{4,5},{5,4},{6,7},{7,6},{8,9},{9,8},{10,11... | collective-permute-start | bytes 6291464 | tf_op jit(solution)/shard_map/ppermute | solution.py:71
  45.5 29.6 %collective-permute-start.4 = (bf16[256,1408]{1,0:T(8,128)(2,1)}, bf16[256,1408]{1,0:T(8,128)(2,1)S(1)}, u32[]{:S(2)}, u32[]{:S(2)}) collective-permute-start(bf16[256,1408]{1,0:T(8,128)(2,1)} %order.14.refs_1_), channel_id=1, source_target_pairs={{0,8},{2,10},{4,12},{6,14},{8,16},{10,18},{12,20},{14,22},{16,24},... | collective-permute-start | bytes 2162696 | tf_op jit(solution)/shard_map/ppermute | solution.py:58
  45.9 89.6 %collective-permute-start.15 = (bf16[512,2048]{1,0:T(8,128)(2,1)}, bf16[512,2048]{1,0:T(8,128)(2,1)}, u32[]{:S(2)}, u32[]{:S(2)}) collective-permute-start(bf16[512,2048]{1,0:T(8,128)(2,1)} %get-tuple-element.35), channel_id=1, source_target_pairs={{0,1},{1,0},{2,3},{3,2},{4,5},{5,4},{6,7},{7,6},{8,9},{9,8},{10,11... | collective-permute-start | bytes 6291464 | tf_op jit(solution)/shard_map/ppermute | solution.py:71
  50.1 59.8 %collective-permute-start.14 = (bf16[128,1024]{1,0:T(8,128)(2,1)}, bf16[128,1024]{1,0:T(8,128)(2,1)}, u32[]{:S(2)}, u32[]{:S(2)}) collective-permute-start(bf16[128,1024]{1,0:T(8,128)(2,1)} %order.20), channel_id=1, source_target_pairs={{0,2},{2,0},{4,6},{6,4},{8,10},{10,8},{12,14},{14,12},{16,18},{18,... | collective-permute-start | bytes 786440 | tf_op jit(solution)/shard_map/ppermute | solution.py:58
  77.7 30.0 %collective-permute-start.6 = (bf16[256,1408]{1,0:T(8,128)(2,1)}, bf16[256,1408]{1,0:T(8,128)(2,1)S(1)}, u32[]{:S(2)}, u32[]{:S(2)}) collective-permute-start(bf16[256,1408]{1,0:T(8,128)(2,1)} %order.15), channel_id=1, source_target_pairs={{0,8},{2,10},{4,12},{6,14},{8,16},{10,18},{12,20},{14,22},{16,24},... | collective-permute-start | bytes 2162696 | tf_op jit(solution)/shard_map/ppermute | solution.py:58
  92.9 46.5 %collective-permute-start.9 = (bf16[512,2048]{1,0:T(8,128)(2,1)}, bf16[512,2048]{1,0:T(8,128)(2,1)}, u32[]{:S(2)}, u32[]{:S(2)}) collective-permute-start(bf16[512,2048]{1,0:T(8,128)(2,1)} %get-tuple-element.33.refs_1_), channel_id=1, source_target_pairs={{0,2},{2,0},{4,6},{6,4},{8,10},{10,8},{12,14},{14,12},{16,18},{18,... | collective-permute-start | bytes 6291464 | tf_op jit(solution)/shard_map/ppermute | solution.py:58
  107.7 101.2 %collective-permute-start.17 = (bf16[512,2048]{1,0:T(8,128)(2,1)}, bf16[512,2048]{1,0:T(8,128)(2,1)}, u32[]{:S(2)}, u32[]{:S(2)}) collective-permute-start(bf16[512,2048]{1,0:T(8,128)(2,1)} %get-tuple-element.35), channel_id=1, source_target_pairs={{0,2},{2,0},{4,6},{6,4},{8,10},{10,8},{12,14},{14,12},{16,18},{18,... | collective-permute-start | bytes 6291464 | tf_op jit(solution)/shard_map/ppermute | solution.py:58
  109.9 29.5 %collective-permute-start.8 = (bf16[512,2048]{1,0:T(8,128)(2,1)}, bf16[512,2048]{1,0:T(8,128)(2,1)}, u32[]{:S(2)}, u32[]{:S(2)}) collective-permute-start(bf16[512,2048]{1,0:T(8,128)(2,1)} %order.17), channel_id=1, source_target_pairs={{0,2},{2,0},{4,6},{6,4},{8,10},{10,8},{12,14},{14,12},{16,18},{18,... | collective-permute-start | bytes 6291464 | tf_op jit(solution)/shard_map/ppermute | solution.py:58
  111.8 245.0 %reduce-scatter.3.cloned.1.call-start = ((), (), s32[]{:S(2)}) async-start(), calls=%async_computation.4 | async-start | bytes 4718592 | tf_op jit(solution)/shard_map/reduce_scatter | solution.py:202
  135.4 73.5 %collective-permute-start.16 = (bf16[512,2048]{1,0:T(8,128)(2,1)}, bf16[512,2048]{1,0:T(8,128)(2,1)}, u32[]{:S(2)}, u32[]{:S(2)}) collective-permute-start(bf16[512,2048]{1,0:T(8,128)(2,1)} %collective-permute-done.15), channel_id=1, source_target_pairs={{0,2},{2,0},{4,6},{6,4},{8,10},{10,8},{12,14},{14,12},{16,18},{18,... | collective-permute-start | bytes 6291464 | tf_op jit(solution)/shard_map/ppermute | solution.py:58
  257.8 199.3 %reduce-scatter.5.cloned.1.call-start = ((), (), s32[]{:S(2)}) async-start(), calls=%async_computation.5 | async-start | bytes 4718592 | tf_op jit(solution)/shard_map/reduce_scatter | solution.py:202
  257.8 31.1 %collective-permute-start.18 = (bf16[512,2048]{1,0:T(8,128)(2,1)}, bf16[512,2048]{1,0:T(8,128)(2,1)}, u32[]{:S(2)}, u32[]{:S(2)}) collective-permute-start(bf16[512,2048]{1,0:T(8,128)(2,1)} %get-tuple-element.37.refs_1_), channel_id=1, source_target_pairs={{0,2},{2,0},{4,6},{6,4},{8,10},{10,8},{12,14},{14,12},{16,18},{18,... | collective-permute-start | bytes 6291464 | tf_op jit(solution)/shard_map/ppermute | solution.py:58
  292.7 49.0 %collective-permute-start.19 = (bf16[512,2048]{1,0:T(8,128)(2,1)}, bf16[512,2048]{1,0:T(8,128)(2,1)S(1)}, u32[]{:S(2)}, u32[]{:S(2)}) collective-permute-start(bf16[512,2048]{1,0:T(8,128)(2,1)} %add_convert_fusion.1.refs_4_), channel_id=1, source_target_pairs={{0,1},{1,0},{2,3},{3,2},{4,5},{5,4},{6,7},{7,6},{8,9},{9,8},{10,11... | collective-permute-start | bytes 6291464 | tf_op jit(solution)/shard_map/ppermute | solution.py:71
  351.1 89.8 %collective-permute-start.23 = (bf16[512,2048]{1,0:T(8,128)(2,1)}, bf16[512,2048]{1,0:T(8,128)(2,1)}, u32[]{:S(2)}, u32[]{:S(2)}) collective-permute-start(bf16[512,2048]{1,0:T(8,128)(2,1)} %add_convert_fusion.refs_3_), channel_id=1, source_target_pairs={{0,1},{1,0},{2,3},{3,2},{4,5},{5,4},{6,7},{7,6},{8,9},{9,8},{10,11... | collective-permute-start | bytes 6291464 | tf_op jit(solution)/shard_map/ppermute | solution.py:71
  359.0 101.1 %collective-permute-start.28 = (f32[128,1024]{1,0:T(8,128)S(1)}, f32[128,1024]{1,0:T(8,128)}, u32[]{:S(2)}, u32[]{:S(2)}) collective-permute-start(f32[128,1024]{1,0:T(8,128)S(1)} %constant_dynamic-slice_fusion.4), channel_id=1, source_target_pairs={{0,2},{2,0},{4,6},{6,4},{8,10},{10,8},{12,14},{14,12},{16,18},{18,... | collective-permute-start | bytes 1572872 | tf_op jit(solution)/shard_map/ppermute | solution.py:58
  410.7 54.2 %collective-permute-start.26 = (bf16[512,1408]{1,0:T(8,128)(2,1)}, bf16[512,1408]{1,0:T(8,128)(2,1)S(1)}, u32[]{:S(2)}, u32[]{:S(2)}) collective-permute-start(bf16[512,1408]{1,0:T(8,128)(2,1)} %pad_maximum_fusion.3), channel_id=1, source_target_pairs={{0,4},{2,6},{4,0},{6,2},{8,12},{10,14},{12,8},{14,10},{16,20},{18,... | collective-permute-start | bytes 4325384 | tf_op jit(solution)/shard_map/ppermute | solution.py:58
  429.0 68.9 %collective-permute-start.25 = (bf16[512,2048]{1,0:T(8,128)(2,1)}, bf16[512,2048]{1,0:T(8,128)(2,1)}, u32[]{:S(2)}, u32[]{:S(2)}) collective-permute-start(bf16[512,2048]{1,0:T(8,128)(2,1)} %get-tuple-element.46), channel_id=1, source_target_pairs={{0,2},{2,0},{4,6},{6,4},{8,10},{10,8},{12,14},{14,12},{16,18},{18,... | collective-permute-start | bytes 6291464 | tf_op jit(solution)/shard_map/ppermute | solution.py:58
  440.4 45.3 %collective-permute-start.36 = (bf16[512,1408]{1,0:T(8,128)(2,1)}, bf16[512,1408]{1,0:T(8,128)(2,1)S(1)}, u32[]{:S(2)}, u32[]{:S(2)}) collective-permute-start(bf16[512,1408]{1,0:T(8,128)(2,1)} %pad_maximum_fusion.4), channel_id=1, source_target_pairs={{0,4},{2,6},{4,0},{6,2},{8,12},{10,14},{12,8},{14,10},{16,20},{18,... | collective-permute-start | bytes 4325384 | tf_op jit(solution)/shard_map/ppermute | solution.py:58
  440.9 65.6 %collective-permute-start.24 = (bf16[512,2048]{1,0:T(8,128)(2,1)}, bf16[512,2048]{1,0:T(8,128)(2,1)}, u32[]{:S(2)}, u32[]{:S(2)}) collective-permute-start(bf16[512,2048]{1,0:T(8,128)(2,1)} %order.24), channel_id=1, source_target_pairs={{0,2},{2,0},{4,6},{6,4},{8,10},{10,8},{12,14},{14,12},{16,18},{18,... | collective-permute-start | bytes 6291464 | tf_op jit(solution)/shard_map/ppermute | solution.py:58
  468.2 28.6 %collective-permute-start.27 = (bf16[256,1408]{1,0:T(8,128)(2,1)}, bf16[256,1408]{1,0:T(8,128)(2,1)S(1)}, u32[]{:S(2)}, u32[]{:S(2)}) collective-permute-start(bf16[256,1408]{1,0:T(8,128)(2,1)} %order.25), channel_id=1, source_target_pairs={{0,8},{2,10},{4,12},{6,14},{8,16},{10,18},{12,20},{14,22},{16,24},... | collective-permute-start | bytes 2162696 | tf_op jit(solution)/shard_map/ppermute | solution.py:58
  474.4 60.4 %collective-permute-start.37 = (bf16[256,1408]{1,0:T(8,128)(2,1)}, bf16[256,1408]{1,0:T(8,128)(2,1)S(1)}, u32[]{:S(2)}, u32[]{:S(2)}) collective-permute-start(bf16[256,1408]{1,0:T(8,128)(2,1)} %order.27), channel_id=1, source_target_pairs={{0,16},{2,18},{4,20},{6,22},{8,24},{10,26},{12,28},{14,30},{16,0},... | collective-permute-start | bytes 2162696 | tf_op jit(solution)/shard_map/ppermute | solution.py:58
  488.9 46.8 %collective-permute-start.38 = (bf16[256,1408]{1,0:T(8,128)(2,1)}, bf16[256,1408]{1,0:T(8,128)(2,1)}, u32[]{:S(2)}, u32[]{:S(2)}) collective-permute-start(bf16[256,1408]{1,0:T(8,128)(2,1)} %add_rows.7), channel_id=1, source_target_pairs={{0,24},{2,26},{4,28},{6,30},{8,0},{10,2},{12,4},{14,6},{16,8},{18,... | collective-permute-start | bytes 2162696 | tf_op jit(solution)/shard_map/ppermute | solution.py:58
  (65 other events, 645.2 us)
Sparse Core Ops, SparseCore 0:
  43.6 87.2 all-gather.2
  133.0 71.7 all-gather.4
  257.9 98.8 reduce-scatter.2
  360.7 96.3 reduce-scatter.4

commit v4 on v3

--- a/solution.py
+++ b/solution.py
@@ -16,6 +16,7 @@
 NEG = -1e30
 HIGH = lax.Precision.HIGHEST
 MICRO = 10**9
+LOG2E = 1.4426950408889634
 
 
 def busy(flops, scale=1.0):
@@ -72,18 +73,6 @@
 
     def place(self, f, s):
         return ((self.z - s) % self.zs) * self.ys + (self.y - f) % self.ys
-
-    def chip_sum(self, value):
-        pieces = jnp.zeros((self.slots,) + value.shape, value.dtype)
-        for s in range(self.zs):
-            for f in range(self.ys):
-                here = value
-                if s or f:
-                    here = self._dp(
-                        value, lambda z, y, c: ((z + s) % self.zs, (y + f) % self.ys, c)
-                    )
-                pieces = lax.dynamic_update_slice_in_dim(pieces, here[None], self.place(f, s), 0)
-        return jnp.sum(pieces, axis=0)
 
     def chip_sum(self, value):
         bit = 2
@@ -207,16 +196,19 @@
 def shift_down(value, by):
     if by == 0:
         return value
-    rows = lax.broadcasted_iota(jnp.int32, value.shape, 0)
-    return jnp.where(rows < by, 0.0, pltpu.roll(value, by, 0))
+    turned = pltpu.roll(value, by, 0)
+    rows = lax.broadcasted_iota(jnp.int32, (8, value.shape[1]), 0)
+    return jnp.concatenate([jnp.where(rows < by, 0.0, turned[:8]), turned[8:]], axis=0)
 
 
 def shift_up(value, by):
     if by == 0:
         return value
     size = value.shape[0]
-    rows = lax.broadcasted_iota(jnp.int32, value.shape, 0)
-    return jnp.where(rows >= size - by, 0.0, pltpu.roll(value, size - by, 0))
+    turned = pltpu.roll(value, size - by, 0)
+    rows = lax.broadcasted_iota(jnp.int32, (8, value.shape[1]), 0)
+    last = jnp.where(rows >= 8 - by, 0.0, turned[size - 8 :])
+    return jnp.concatenate([turned[: size - 8], last], axis=0)
 
 
 def convolve(joined, taps, lanes):
@@ -259,7 +251,7 @@
 
 
 def fwd_kernel(waits, limit_ref, xb_ref, taps_ref, heads_ref, skip_ref, *refs):
-    y_ref, s1_ref = refs[waits:]
+    y_ref, s1_ref, xs_ref, slope_ref = refs[waits:]
     inner = y_ref.shape[1]
     limit = limit_ref[pl.program_id(0)]
     half = STRETCH // 2
@@ -272,7 +264,8 @@
     tri = triangle(False)
     cum = jnp.concatenate([dot_high(tri, rate[lo]), dot_high(tri, rate[hi])], 0)
     late = cum - log_dt
-    late_t = late.T
+    cum2, late2 = cum * LOG2E, late * LOG2E
+    late_t = late2.T
     tail = jnp.exp(cum[STRETCH - 1 : STRETCH] - late[lo])
     ecum = jnp.exp(cum[hi])
     grams = [dot_nt(cm[b], bm[b]) for b in (lo, hi)]
@@ -283,7 +276,12 @@
         lanes = slice(p * LANES, (p + 1) * LANES)
         _, conv = convolve(xb_ref[:, lanes], taps_ref, lanes)
         channel = lax.broadcasted_iota(jnp.int32, (1, LANES), 1) + p * LANES
-        xs = (jax.nn.silu(conv) * (channel < limit).astype(F32)).astype(BF16)
+        used = (channel < limit).astype(F32)
+        sig = jax.nn.sigmoid(conv)
+        act = conv * sig
+        xs = (act * used).astype(BF16)
+        xs_ref[:, lanes] = xs
+        slope_ref[:, lanes] = ((sig + act * (1.0 - sig)) * used).astype(BF16)
         h = 2 * p
         weights = pair_lanes(tail[:, h : h + 1], tail[:, h + 1 : h + 2])
         weighted = (xs[lo].astype(F32) * weights).astype(BF16)
@@ -294,11 +292,11 @@
             xe = [only(xs[b], e) for e in (0, 1)]
             base = b.start
             for e in (0, 1):
-                col = cum[b, h + e : h + e + 1]
+                col = cum2[b, h + e : h + e + 1]
                 row = late_t[h + e : h + e + 1, b]
-                top = jnp.exp(jnp.where(mask, col[:half] - row[:, :half], NEG))
-                low0 = jnp.exp(col[half:] - row[:, :half])
-                low1 = jnp.exp(jnp.where(mask, col[half:] - row[:, half:], NEG))
+                top = jnp.exp2(jnp.where(mask, col[:half] - row[:, :half], NEG))
+                low0 = jnp.exp2(col[half:] - row[:, :half])
+                low1 = jnp.exp2(jnp.where(mask, col[half:] - row[:, half:], NEG))
                 tops.append((gram[:half, :half] * top).astype(BF16))
                 lows.append((gram[half:, :half] * low0).astype(BF16))
                 lows.append((gram[half:, half:] * low1).astype(BF16))
@@ -319,12 +317,11 @@
     return jnp.sum(only(value, e), axis=1, keepdims=True)
 
 
-def bwd_kernel(first, extra, limit_ref, xb_ref, y_ref, dy_ref, s1_ref, taps_ref, *refs):
+def bwd_kernel(extra, xb_ref, y_ref, dy_ref, s1_ref, xs_ref, slope_ref, taps_ref, *refs):
     heads_ref, skip_ref = refs[:2]
     dxb_ref, gch_ref, gh_ref, dg_ref, rs_ref = refs[2 + extra :]
     inner = y_ref.shape[1]
     q = pl.program_id(0)
-    limit = limit_ref[q + first]
     half = STRETCH // 2
     lo, hi = slice(0, STRETCH), slice(STRETCH, 2 * STRETCH)
     bc = slice(inner, inner + 2 * LANES)
@@ -336,7 +333,7 @@
 
     dg_ref[...] = jnp.zeros_like(dg_ref)
     rs_ref[...] = jnp.zeros_like(rs_ref)
-    shifted_bc, conv_bc = convolve(xb_ref[:, bc], taps_ref, bc)
+    _, conv_bc = convolve(xb_ref[:, bc], taps_ref, bc)
     sig_bc = jax.nn.sigmoid(conv_bc)
     act = (conv_bc * sig_bc).astype(BF16)
     bm, cm = act[:, :LANES], act[:, LANES:]
@@ -344,7 +341,8 @@
     tri = triangle(False)
     cum = jnp.concatenate([dot_high(tri, rate[lo]), dot_high(tri, rate[hi])], 0)
     late = cum - log_dt
-    cum_t = cum.T
+    late2 = late * LOG2E
+    cum_t = (cum * LOG2E).T
     tail = jnp.exp(cum[STRETCH - 1 : STRETCH] - late[lo])
     ecum = jnp.exp(cum[hi])
     grams = [dot_nt(bm[b], cm[b]) for b in (lo, hi)]
@@ -356,25 +354,22 @@
     d_tail = jnp.zeros((1, LANES), F32)
     lane_of = lax.broadcasted_iota(jnp.int32, (1, LANES), 1)
 
-    def conv_back(d_act, conv, sig, shifted, lanes):
-        d_conv = d_act * (sig * (1.0 + conv * (1.0 - sig)))
-        rows = [jnp.sum(d_conv * part, axis=0, keepdims=True) for part in shifted]
+    def conv_back(d_conv, lanes):
+        joined = xb_ref[:, lanes]
+        rows, total = [], None
+        for k in range(4):
+            moved = shift_up(d_conv, 3 - k)
+            rows.append(jnp.sum(moved * joined, axis=0, keepdims=True))
+            part = taps_ref[k : k + 1, lanes] * moved
+            total = part if total is None else total + part
         rows.append(jnp.sum(d_conv, axis=0, keepdims=True))
-        total = None
-        for k in range(4):
-            part = taps_ref[k : k + 1, lanes] * shift_up(d_conv, 3 - k)
-            total = part if total is None else total + part
         dxb_ref[:, lanes] = total.astype(BF16)
         return rows
 
     for p in range(inner // LANES):
         lanes = slice(p * LANES, (p + 1) * LANES)
         h = 2 * p
-        shifted, conv = convolve(xb_ref[:, lanes], taps_ref, lanes)
-        sig = jax.nn.sigmoid(conv)
-        channel = lane_of + p * LANES
-        used = (channel < limit).astype(F32)
-        xs = (conv * sig * used).astype(BF16)
+        xs = xs_ref[:, lanes]
         xf = xs.astype(F32)
         dy = dy_ref[:, lanes]
         dyf = dy.astype(F32)
@@ -391,11 +386,11 @@
             tops, lows = [], []
             dye = [only(dy[b], e) for e in (0, 1)]
             for e in (0, 1):
-                col = late[b, h + e : h + e + 1]
+                col = late2[b, h + e : h + e + 1]
                 row = cum_t[h + e : h + e + 1, b]
-                top0 = jnp.exp(jnp.where(mask, row[:, :half] - col[:half], NEG))
-                top1 = jnp.exp(row[:, half:] - col[:half])
-                low = jnp.exp(jnp.where(mask, row[:, half:] - col[half:], NEG))
+                top0 = jnp.exp2(jnp.where(mask, row[:, :half] - col[:half], NEG))
+                top1 = jnp.exp2(row[:, half:] - col[:half])
+                low = jnp.exp2(jnp.where(mask, row[:, half:] - col[half:], NEG))
                 xe = only(xs[b], e)
                 d_top = dot_nt(xe[:half], dy[b])
                 d_low = dot_nt(xe[half:], dy[b][half:])
@@ -416,12 +411,12 @@
         from_y = dyf * (y_ref[:, lanes] - skip * xf)
         state_sum = jnp.sum(xf[lo] * d_from_state, axis=0, keepdims=True)
         for e in (0, 1):
-            here = lane_of == h + e
-            rs_ref[0] = jnp.where(here, lane_sum(from_x, e), rs_ref[0])
-            rs_ref[1] = jnp.where(here, lane_sum(from_y, e), rs_ref[1])
-            d_tail = jnp.where(here, lane_sum(state_sum, e), d_tail)
-        d_act = (d_x + skip * dyf) * used
-        rows = conv_back(d_act, conv, sig, shifted, lanes)
+            at = slice(h + e, h + e + 1)
+            rs_ref[0, :, at] = lane_sum(from_x, e)
+            rs_ref[1, :, at] = lane_sum(from_y, e)
+            d_tail = jnp.where(lane_of == h + e, lane_sum(state_sum, e), d_tail)
+        d_conv = (d_x + skip * dyf) * slope_ref[:, lanes].astype(F32)
+        rows = conv_back(d_conv, lanes)
         rows.append(jnp.sum(dyf * xf, axis=0, keepdims=True))
         for r, row in enumerate(rows):
             gch_ref[r : r + 1, lanes] += row
@@ -434,7 +429,7 @@
     d_bm[0] = d_bm[0] + d_bm0
     d_cm[1] = d_cm[1] + d_cm1
     d_act = jnp.concatenate([jnp.concatenate(d_bm, 0), jnp.concatenate(d_cm, 0)], 1)
-    rows = conv_back(d_act, conv_bc, sig_bc, shifted_bc, bc)
+    rows = conv_back(d_act * (sig_bc * (1.0 + conv_bc * (1.0 - sig_bc))), bc)
     for r, row in enumerate(rows):
         gch_ref[r : r + 1, bc] += row
 
@@ -467,11 +462,15 @@
             out_specs=[
                 per(inner),
                 pl.BlockSpec((inner, LANES), lambda q, *_: (q, 0)),
+                per(inner),
+                per(inner),
             ],
         ),
         out_shape=[
             jax.ShapeDtypeStruct((rows, inner), F32),
             jax.ShapeDtypeStruct((seqs * inner, LANES), BF16),
+            jax.ShapeDtypeStruct((rows, inner), BF16),
+            jax.ShapeDtypeStruct((rows, inner), BF16),
         ],
         cost_estimate=busy(25 * MICRO),
         name="scan_forward",
@@ -493,23 +492,24 @@
     )(value, *waits)
 
 
-def run_bwd(limits, xb, y, dy, s1, taps, heads, skip, slot, first, count, d_xb=None, waits=()):
+def run_bwd(xb, y, dy, s1, xs, slope, taps, heads, skip, slot, first, count, d_xb=None, waits=()):
     rows, cols = xb.shape
     inner = cols - 3 * LANES
-    whole = lambda shape: pl.BlockSpec(shape, lambda q, *_: (0,) * len(shape))
-    per = lambda width: pl.BlockSpec((slot, width), lambda q, *_: (q + first, 0))
+    whole = lambda shape: pl.BlockSpec(shape, lambda q: (0,) * len(shape))
+    per = lambda width: pl.BlockSpec((slot, width), lambda q: (q + first, 0))
     aliased = d_xb is not None
-    kernel = functools.partial(bwd_kernel, first, aliased + len(waits))
+    kernel = functools.partial(bwd_kernel, aliased + len(waits))
     return pl.pallas_call(
         kernel,
-        grid_spec=pltpu.PrefetchScalarGridSpec(
-            num_scalar_prefetch=1,
+        grid_spec=pl.GridSpec(
             grid=(count,),
             in_specs=[
                 per(cols),
                 per(inner),
                 per(inner),
-                pl.BlockSpec((inner, LANES), lambda q, *_: (q + first, 0)),
+                pl.BlockSpec((inner, LANES), lambda q: (q + first, 0)),
+                per(inner),
+                per(inner),
                 whole(taps.shape),
                 whole(heads.shape),
                 whole(skip.shape),
@@ -526,10 +526,10 @@
             jax.ShapeDtypeStruct((8, cols), F32),
             jax.ShapeDtypeStruct((8, LANES), F32),
         ],
-        input_output_aliases={8: 0} if aliased else {},
-        cost_estimate=busy(15 * count * MICRO),
+        input_output_aliases={9: 0} if aliased else {},
+        cost_estimate=busy(4 * count * MICRO),
         name="scan_backward",
-    )(limits, xb, y, dy, s1, taps, heads, skip, *([d_xb] if aliased else []), *waits)
+    )(xb, y, dy, s1, xs, slope, taps, heads, skip, *([d_xb] if aliased else []), *waits)
 
 
 def prepare_kernel(length_ref, u_ref, cot_ref, gain_ref, *refs):
@@ -761,7 +761,7 @@
         return lax.optimization_barrier(jnp.concatenate(pieces, axis=0))
 
     normed = share(normed_own, arriving)
-    d_branch = share(d_branch_own, [grid.send_x(d_branch_own, g) for g in range(1, n)])
+    crossing = [grid.send_x(d_branch_own, g) for g in range(1, n)]
     seqs = len(owners)
     seq_width = jnp.stack([widths[o] for o in owners])
     used = seq_width * ((HEADS // 8) * HEAD_DIM)
@@ -789,9 +789,11 @@
     rows_of = lambda value, i: value[i * slot : (i + 1) * slot]
     xb = dot_nn(normed, w_x)
     scan = (taps, head_rows, skip, slot)
-    y, s1 = run_fwd(limits, xb, *scan)
+    d_branch = share(d_branch_own, [tie(value, xb) for value in crossing])
+    y, s1, xs, slope = run_fwd(limits, xb, *scan)
     z = dot_nn(normed, w_z)
     sig = jax.nn.sigmoid(z)
+    held = lambda value: lax.optimization_barrier(value.astype(BF16)).astype(F32)
     gated = y * (z * sig)
 
     def group_sum(rows):
@@ -817,7 +819,9 @@
     if out_far:
         inner_sum = tie(inner_sum, *[rows for pair in out_far for rows in pair])
     pull = scale * scale * scale / counts * inner_sum
-    d_gated = weighted * scale[:, None] - gated * pull[:, None]
+    d_gated = held(weighted) * scale[:, None] - gated * pull[:, None]
+    z = held(z)
+    sig = jax.nn.sigmoid(z)
     g_gate = jnp.sum(d_gnorm * gated * scale[:, None], axis=0)
     silu = z * sig
     d_y = (d_gated * silu).astype(BF16)
@@ -833,7 +837,7 @@
         out_there = grid.swap_core(out_there)
         branch.append((out_here.astype(F32) + out_there.astype(F32)).astype(BF16))
     d_xb, g_channels, g_heads = run_bwd(
-        limits, xb, y, d_y, s1, *scan, 0, far, None, (g_o_part, g_z_part, *branch)
+        xb, y, d_y, s1, xs, slope, *scan, 0, far, None, (g_o_part, g_z_part, *branch)
     )
     branch = cross(branch)
     for i in range(0, far, 2):
@@ -842,7 +846,7 @@
         there = grid.swap_core(tie(there, *branch))
         d_normed.append((here.astype(F32) + there.astype(F32)).astype(BF16))
     d_xb, more_channels, more_heads = run_bwd(
-        limits, xb, y, d_y, s1, *scan, far, 2, d_xb, (*d_normed, g_o)
+        xb, y, d_y, s1, xs, slope, *scan, far, 2, d_xb, (*d_normed, g_o)
     )
     d_normed = cross(d_normed)
     g_channels, g_heads = g_channels + more_channels, g_heads + more_heads

time: 574 us -> 560 us (0.976)
  starting transfers between devices: 45.2 us -> 70.9 us
  waiting for transfers between devices: 112 us -> 90.8 us
  local copies, waits for them, and re-layouts: 68.1 us -> 54.2 us
    ppermute x30, waiting for transfers between devices: 65.2 us -> 87.2 us  [_dp(): return lax.ppermute(value, 'dp', pairs)]
    reduce_scatter x2, waiting for transfers between devices: 19.5 us -> 0.01 us  [scatter_all(): lax.psum_scatter(value, 'dp', scatter_dimension=0, tiled=True, axis_index...]
    ppermute x30, starting transfers between devices: 23.1 us -> 41.2 us  [_dp(): return lax.ppermute(value, 'dp', pairs)]
    ppermute x8, waiting for transfers between devices: 16.2 us -> 2.33 us  [send_x(): return lax.ppermute(value, 'fsdp', pairs)]
    ppermute x3, starting transfers between devices: 11.8 us -> 21.9 us  [chip_sum(): lax.ppermute(value, 'dp', [(i, i ^ bit) for i in range(self.dp)])]
    ppermute x3, waiting for transfers between devices: 11.2 us -> 1.13 us  [chip_sum(): lax.ppermute(value, 'dp', [(i, i ^ bit) for i in range(self.dp)])]
    unnamed x101, local copies, waits for them, and re-layouts: 29.2 us -> 23.1 us
  transfers between devices with their start and end apart: 45 -> 45, of which waited for: 17 -> 17; matrix products, arithmetic and copies ran while one was open for 31% -> 33% of each run, Pallas kernels for 29% -> 30%
where the time goes in v4:
time: 560 us; the launch traced here: 552 us
  Pallas kernels  165 us (29%)
  matrix products  93.8 us (17%)
  waiting for transfers between devices  90.8 us (16%)
  starting transfers between devices  70.9 us (13%)
  other arithmetic  61.7 us (11%)
  local copies, waits for them, and re-layouts  54.2 us (10%)
  between operations  15.7 us (3%)
    ppermute x30, waiting for transfers between devices, _dp(): return lax.ppermute(value, 'dp', pairs)  87.2 us
    pallas_call x2, Pallas kernels, run_bwd(): pl.pallas_call(kernel, grid_spec=pl.GridSpec(grid=(count,), in_specs=[per...  56 us
    dot_general x3, matrix products, dot_nn(): lax.dot_general(a, b, (((1,), (0,)), ((), ())), preferred_element_type=F32)  52.4 us
    dot_general x3, matrix products, dot_tn(): lax.dot_general(a, b, (((0,), (0,)), ((), ())), preferred_element_type=F32)  41.4 us
    ppermute x30, starting transfers between devices, _dp(): return lax.ppermute(value, 'dp', pairs)  41.2 us
    pallas_call x2, Pallas kernels, run_back(): pl.pallas_call(functools.partial(back_kernel, len(waits)), grid=(width //...  33.9 us
    pallas_call x1, Pallas kernels, run_fwd(): pl.pallas_call(functools.partial(fwd_kernel, len(waits)), grid_spec=pltpu...  27.1 us
    unnamed x101, local copies, waits for them, and re-layouts  23.1 us
  transfers between devices with their start and end apart: 45, of which 17 were waited for; matrix products, arithmetic and copies ran while one was open for 33% of the time, Pallas kernels for 30%

profile of v4, /device:TPU:0, one launch (start us, length us, event | category | flops | bytes accessed | tf_op | source)
XLA Modules:
  0.0 552.2 jit_solution(17516552477126265708)
XLA Ops:
  33.1 6.1 %collective-permute-done.3.refs_1_ = bf16[256,1408]{1,0:T(8,128)(2,1)S(1)} collective-permute-done((bf16[256,1408]{1,0:T(8,128)(2,1)S(1)}, bf16[256,1408]{1,0:T(8,128)(2,1)S(1)}, u32[]{:S(2)}, u32[]{:S(2)}) %collective-permute-start.3) | collective-permute-done | bytes 720928 | tf_op jit(solution)/shard_map/ppermute | solution.py:59
  48.0 19.6 %collective-permute-done.5.refs_1_ = bf16[256,1408]{1,0:T(8,128)(2,1)S(1)} collective-permute-done((bf16[256,1408]{1,0:T(8,128)(2,1)}, bf16[256,1408]{1,0:T(8,128)(2,1)S(1)}, u32[]{:S(2)}, u32[]{:S(2)}) %collective-permute-start.5) | collective-permute-done | bytes 720928 | tf_op jit(solution)/shard_map/ppermute | solution.py:59
  67.6 7.5 %collective-permute-done.4.refs_0_ = bf16[256,1408]{1,0:T(8,128)(2,1)S(1)} collective-permute-done((bf16[256,1408]{1,0:T(8,128)(2,1)}, bf16[256,1408]{1,0:T(8,128)(2,1)S(1)}, u32[]{:S(2)}, u32[]{:S(2)}) %collective-permute-start.4) | collective-permute-done | bytes 720928 | tf_op jit(solution)/shard_map/ppermute | solution.py:59
  88.8 18.9 %collective-permute-done.6.refs_0_ = bf16[256,1408]{1,0:T(8,128)(2,1)S(1)} collective-permute-done((bf16[256,1408]{1,0:T(8,128)(2,1)}, bf16[256,1408]{1,0:T(8,128)(2,1)S(1)}, u32[]{:S(2)}, u32[]{:S(2)}) %collective-permute-start.6) | collective-permute-done | bytes 720928 | tf_op jit(solution)/shard_map/ppermute | solution.py:59
  121.8 12.8 %collective-permute-done.10 = bf16[256,1408]{1,0:T(8,128)(2,1)S(1)} collective-permute-done((bf16[256,1408]{1,0:T(8,128)(2,1)S(1)}, bf16[256,1408]{1,0:T(8,128)(2,1)S(1)}, u32[]{:S(2)}, u32[]{:S(2)}) %collective-permute-start.10) | collective-permute-done | bytes 720928 | tf_op jit(solution)/shard_map/ppermute | solution.py:59
  140.3 18.6 %fusion.21.xb_ref.refs_1_ = f32[2048,1408]{1,0:T(8,128)} fusion(bf16[2048,2048]{1,0:T(8,128)(2,1)S(1)} %pad_maximum_fusion.normed_ref, bf16[2048,1408]{1,0:T(8,128)(2,1)} %constant_dynamic-update-slice_fusion.wx_ref), kind=kOutput, calls=%fused_computation.132 | convolution fusion | flops 11811160064 | bytes 25690112 | tf_op jit(solution)/shard_map/dot_general | solution.py:27
  160.8 27.1 %scan_forward.1 = (f32[2048,1024]{1,0:T(8,128)}, bf16[4096,128]{1,0:T(8,128)(2,1)}, bf16[2048,1024]{1,0:T(8,128)(2,1)}, bf16[2048,1024]{1,0:T(8,128)(2,1)}) custom-call(s32[4]{0:T(128)} %subtract_clamp_fusion.limit_ref, f32[2048,1408]{1,0:T(8,128)} %fusion.21.xb_ref.refs_1_, f32[8,1408]{1,0:T(8,128)} %select_maximum_fusion.taps_ref, ...), custom_call_target="tpu_custom_call" | custom-call | flops 24999999488 | tf_op jit(solution)/shard_map/scan_forward/pallas_call | solution.py:455
  188.0 17.8 %multiply_reduce_fusion.2 = (f32[2048]{0:T(1024)S(1)}, f32[2048,1024]{1,0:T(8,128)}, bf16[2048,1024]{1,0:T(8,128)(2,1)}) fusion(f32[2048,1024]{1,0:T(8,128)} %get-tuple-element.36.y_ref, bf16[2048,2048]{1,0:T(8,128)(2,1)} %copy-done.1, bf16[2048,1024]{1,0:T(8,128)(2,1)} %all-gather.3.cloned.1.call-done.wz_ref), kind=kOutput, calls=%fused_computation.18 | convolution fusion | flops 8606709760 | bytes 33562624 | tf_op jit(solution)/shard_map/dot_general | solution.py:27
  217.8 10.9 %convolution_convert_fusion.2.refs_1_.refs_2_ = bf16[2048,1024]{1,0:T(8,128)(2,1)} fusion(bf16[2048,2048]{1,0:T(8,128)(2,1)S(1)} %pad_maximum_fusion.1, bf16[2048,1024]{1,0:T(8,128)(2,1)S(1)} %multiply_convert_fusion.gnorm_ref), kind=kOutput, calls=%fused_computation.25 | convolution fusion | flops 8592031744 | bytes 16777216 | tf_op jit(solution)/shard_map/dot_general | solution.py:35
  228.9 16.0 %multiply_reduce_fusion = (f32[1024]{0:T(1024)S(1)}, f32[2048]{0:T(1024)S(1)}, bf16[2048,1024]{1,0:T(8,128)(2,1)}) fusion(f32[2048,1024]{1,0:T(8,128)} %get-tuple-element.119, f32[2048]{0:T(1024)S(1)} %add_rsqrt_fusion, f32[1024]{0:T(1024)S(1)} %dynamic_slice.111, bf16[2048,2048]{1,0:T(8,128)(2,1)} %copy-done.7, bf16[2048,1024]{1,0:T(8,128)(2,1)} %order.23.wo_ref), kind=kOutput, calls=%fused_computation.14 | convolution fusion | flops 8604611584 | bytes 25190400 | tf_op jit(solution)/shard_map/dot_general | solution.py:27
  247.0 10.1 %branch_rows.2 = (bf16[512,2048]{1,0:T(8,128)(2,1)}, bf16[512,2048]{1,0:T(8,128)(2,1)}) custom-call(bf16[2048,1024]{1,0:T(8,128)(2,1)} %copy-done.2, bf16[2048,1024]{1,0:T(8,128)(2,1)} %order.23.wo_ref, f32[2048]{0:T(1024)} %copy-done.31), custom_call_target="tpu_custom_call" | custom-call | tf_op jit(solution)/shard_map/branch_rows/pallas_call | solution.py:614
  258.5 13.1 %fusion.8 = (bf16[2048,1024]{1,0:T(8,128)(2,1)}, bf16[2048,1024]{1,0:T(8,128)(2,1)S(1)}) fusion(bf16[2048,1024]{1,0:T(8,128)(2,1)} %get-tuple-element.123, f32[2048,1024]{1,0:T(8,128)} %get-tuple-element.119, bf16[2048,1024]{1,0:T(8,128)(2,1)} %get-tuple-element.122, f32[2048]{0:T(1024)S(1)} %fusion.12, f32[2048]{0:T(1024)S(1)} %add_rsqrt_fusion, ...), kind=kLoop, calls=%fused_computation.11 | loop fusion | flops 37748736 | bytes 33570816 | tf_op jit(solution)/shard_map/convert_element_type | solution.py:827
  276.6 12.9 %convolution_convert_fusion.1.refs_3_ = bf16[2048,1024]{1,0:T(8,128)(2,1)} fusion(bf16[2048,2048]{1,0:T(8,128)(2,1)} %copy-done.1, bf16[2048,1024]{1,0:T(8,128)(2,1)S(1)} %get-tuple-element.121.dz_ref), kind=kOutput, calls=%fused_computation.24 | convolution fusion | flops 8592031744 | bytes 16777216 | tf_op jit(solution)/shard_map/dot_general | solution.py:35
  289.5 28.1 %scan_backward.2 = (bf16[2048,1408]{1,0:T(8,128)(2,1)}, f32[8,1408]{1,0:T(8,128)}, f32[8,128]{1,0:T(8,128)}) custom-call(f32[2048,1408]{1,0:T(8,128)} %fusion.21.xb_ref.refs_1_, f32[2048,1024]{1,0:T(8,128)} %get-tuple-element.36.y_ref, bf16[2048,1024]{1,0:T(8,128)(2,1)} %get-tuple-element.120.dy_ref, bf16[4096,128]{1,0:T(8,128)(2,1)} %get-tuple-element.40.s1_ref, ...), custom_call_target="tpu_custom_call" | custom-call | flops 8000000000 | tf_op jit(solution)/shard_map/scan_backward/pallas_call | solution.py:502
  317.6 17.0 %normed_gradient.2 = (bf16[512,2048]{1,0:T(8,128)(2,1)}, bf16[512,2048]{1,0:T(8,128)(2,1)}, f32[8,2048]{1,0:T(8,128)}) custom-call(bf16[2048,1024]{1,0:T(8,128)(2,1)} %copy-done.3, bf16[2048,1408]{1,0:T(8,128)(2,1)} %get-tuple-element.43.dxb_ref.refs_2_, bf16[2048,1024]{1,0:T(8,128)(2,1)} %all-gather.3.cloned.1.call-done.wz_ref, ...), custom_call_target="tpu_custom_call" | custom-call | tf_op jit(solution)/shard_map/normed_gradient/pallas_call | solution.py:582
  347.5 27.9 %scan_backward.3 = (bf16[2048,1408]{1,0:T(8,128)(2,1)}, f32[8,1408]{1,0:T(8,128)}, f32[8,128]{1,0:T(8,128)}) custom-call(f32[2048,1408]{1,0:T(8,128)} %fusion.21.xb_ref.refs_1_, f32[2048,1024]{1,0:T(8,128)} %get-tuple-element.36.y_ref, bf16[2048,1024]{1,0:T(8,128)(2,1)} %get-tuple-element.120.dy_ref, ...), custom_call_target="tpu_custom_call", output_to_operand_aliasing={{0}: (9, {})} | custom-call | flops 8000000000 | tf_op jit(solution)/shard_map/scan_backward/pallas_call | solution.py:502
  375.4 17.6 %convolution_convert_fusion.refs_0_ = bf16[2048,1408]{1,0:T(8,128)(2,1)S(1)} fusion(bf16[2048,2048]{1,0:T(8,128)(2,1)} %copy-done.1, bf16[2048,1408]{1,0:T(8,128)(2,1)} %get-tuple-element.46.dxb_ref), kind=kOutput, calls=%fused_computation.21 | convolution fusion | flops 11814043648 | bytes 19922944 | tf_op jit(solution)/shard_map/dot_general | solution.py:35
  398.6 16.9 %normed_gradient.3 = (bf16[512,2048]{1,0:T(8,128)(2,1)}, bf16[512,2048]{1,0:T(8,128)(2,1)}, f32[8,2048]{1,0:T(8,128)}) custom-call(bf16[2048,1024]{1,0:T(8,128)(2,1)} %copy-done.3, bf16[2048,1408]{1,0:T(8,128)(2,1)} %get-tuple-element.46.dxb_ref, bf16[2048,1024]{1,0:T(8,128)(2,1)} %all-gather.3.cloned.1.call-done.wz_ref, ...), custom_call_target="tpu_custom_call" | custom-call | tf_op jit(solution)/shard_map/normed_gradient/pallas_call | solution.py:582
  418.3 9.9 %branch_rows.3 = (bf16[512,2048]{1,0:T(8,128)(2,1)}, bf16[512,2048]{1,0:T(8,128)(2,1)}) custom-call(bf16[2048,1024]{1,0:T(8,128)(2,1)} %copy-done.2, bf16[2048,1024]{1,0:T(8,128)(2,1)} %order.23.wo_ref, bf16[512,2048]{1,0:T(8,128)(2,1)} %get-tuple-element.47.refs_0_.refs_1_), custom_call_target="tpu_custom_call" | custom-call | tf_op jit(solution)/shard_map/branch_rows/pallas_call | solution.py:614
  439.4 9.3 %collective-permute-start.27 = (bf16[256,1408]{1,0:T(8,128)(2,1)}, bf16[256,1408]{1,0:T(8,128)(2,1)S(1)}, u32[]{:S(2)}, u32[]{:S(2)}) collective-permute-start(bf16[256,1408]{1,0:T(8,128)(2,1)} %order.27), channel_id=1, source_target_pairs={{0,8},{2,10},{4,12},{6,14},{8,16},{10,18},{12,20},{14,22},{16,24},... | collective-permute-start | bytes 2162696 | tf_op jit(solution)/shard_map/ppermute | solution.py:59
  459.5 8.2 %collective-permute-done.36.refs_1_ = bf16[512,1408]{1,0:T(8,128)(2,1)S(1)} collective-permute-done((bf16[512,1408]{1,0:T(8,128)(2,1)}, bf16[512,1408]{1,0:T(8,128)(2,1)S(1)}, u32[]{:S(2)}, u32[]{:S(2)}) %collective-permute-start.36) | collective-permute-done | bytes 1441824 | tf_op jit(solution)/shard_map/ppermute | solution.py:59
  470.9 9.8 %collective-permute-start.38 = (bf16[256,1408]{1,0:T(8,128)(2,1)}, bf16[256,1408]{1,0:T(8,128)(2,1)}, u32[]{:S(2)}, u32[]{:S(2)}) collective-permute-start(bf16[256,1408]{1,0:T(8,128)(2,1)} %add_rows.7), channel_id=1, source_target_pairs={{0,24},{2,26},{4,28},{6,30},{8,0},{10,2},{12,4},{14,6},{16,8},{18,... | collective-permute-start | bytes 2162696 | tf_op jit(solution)/shard_map/ppermute | solution.py:59
  484.6 8.5 %input_gradient.1 = bf16[512,2048]{1,0:T(8,128)(2,1)} custom-call(bf16[512,2048]{1,0:T(8,128)(2,1)} %u_ref.5, bf16[512,2048]{1,0:T(8,128)(2,1)} %cot_ref.3, f32[1,2048]{1,0:T(1,128)} %bitcast.105, bf16[512,2048]{1,0:T(8,128)(2,1)} %collective-permute-done.23.refs_1_.refs_0_, bf16[512,2048]{1,0:T(8,128)(2,1)} %get-tuple-element.47.refs_0_.refs_1_, ...), custom_call_target="tpu_custom_call" | custom-call | flops 8000000000 | tf_op jit(solution)/shard_map/input_gradient/pallas_call | solution.py:675
  493.1 19.2 %collective-permute-start.31 = (f32[80,128]{1,0:T(8,128)S(1)}, f32[80,128]{1,0:T(8,128)S(1)}, u32[]{:S(2)}, u32[]{:S(2)}) collective-permute-start(f32[80,128]{1,0:T(8,128)S(1)} %add.360), channel_id=1, source_target_pairs={{0,8},{2,10},{4,12},{6,14},{8,0},{10,2},{12,4},{14,6},{16,24},{18,... | collective-permute-start | bytes 122888 | tf_op jit(solution)/shard_map/ppermute | solution.py:80
  (319 shorter events, 172.7 us)
Async XLA Ops:
  7.2 180.8 %all-gather.3.cloned.1.call-start = ((), (), s32[]{:S(2)}) async-start(), calls=%async_computation.2 | async-start | bytes 4718592 | tf_op jit(solution)/shard_map/all_gather | solution.py:187
  43.4 185.5 %all-gather.5.cloned.1.call-start = ((), (), s32[]{:S(2)}) async-start(), calls=%async_computation.3 | async-start | bytes 4718592 | tf_op jit(solution)/shard_map/all_gather | solution.py:187
  43.4 65.1 %collective-permute-start = (bf16[512,2048]{1,0:T(8,128)(2,1)}, bf16[512,2048]{1,0:T(8,128)(2,1)}, u32[]{:S(2)}, u32[]{:S(2)}) collective-permute-start(bf16[512,2048]{1,0:T(8,128)(2,1)} %get-tuple-element.35.refs_1_), channel_id=1, source_target_pairs={{0,1},{1,0},{2,3},{3,2},{4,5},{5,4},{6,7},{7,6},{8,9},{9,8},{10,11... | collective-permute-start | bytes 6291464 | tf_op jit(solution)/shard_map/ppermute | solution.py:72
  45.5 29.7 %collective-permute-start.4 = (bf16[256,1408]{1,0:T(8,128)(2,1)}, bf16[256,1408]{1,0:T(8,128)(2,1)S(1)}, u32[]{:S(2)}, u32[]{:S(2)}) collective-permute-start(bf16[256,1408]{1,0:T(8,128)(2,1)} %order.15.refs_1_), channel_id=1, source_target_pairs={{0,8},{2,10},{4,12},{6,14},{8,16},{10,18},{12,20},{14,22},{16,24},... | collective-permute-start | bytes 2162696 | tf_op jit(solution)/shard_map/ppermute | solution.py:59
  45.8 89.7 %collective-permute-start.9 = (bf16[512,2048]{1,0:T(8,128)(2,1)}, bf16[512,2048]{1,0:T(8,128)(2,1)}, u32[]{:S(2)}, u32[]{:S(2)}) collective-permute-start(bf16[512,2048]{1,0:T(8,128)(2,1)} %get-tuple-element.35.refs_1_), channel_id=1, source_target_pairs={{0,2},{2,0},{4,6},{6,4},{8,10},{10,8},{12,14},{14,12},{16,18},{18,... | collective-permute-start | bytes 6291464 | tf_op jit(solution)/shard_map/ppermute | solution.py:59
  46.7 61.9 %collective-permute-start.14 = (bf16[128,1024]{1,0:T(8,128)(2,1)}, bf16[128,1024]{1,0:T(8,128)(2,1)}, u32[]{:S(2)}, u32[]{:S(2)}) collective-permute-start(bf16[128,1024]{1,0:T(8,128)(2,1)} %order.21), channel_id=1, source_target_pairs={{0,2},{2,0},{4,6},{6,4},{8,10},{10,8},{12,14},{14,12},{16,18},{18,... | collective-permute-start | bytes 786440 | tf_op jit(solution)/shard_map/ppermute | solution.py:59
  77.6 30.1 %collective-permute-start.6 = (bf16[256,1408]{1,0:T(8,128)(2,1)}, bf16[256,1408]{1,0:T(8,128)(2,1)S(1)}, u32[]{:S(2)}, u32[]{:S(2)}) collective-permute-start(bf16[256,1408]{1,0:T(8,128)(2,1)} %order.16), channel_id=1, source_target_pairs={{0,8},{2,10},{4,12},{6,14},{8,16},{10,18},{12,20},{14,22},{16,24},... | collective-permute-start | bytes 2162696 | tf_op jit(solution)/shard_map/ppermute | solution.py:59
  88.8 70.1 %collective-permute-start.15 = (bf16[512,2048]{1,0:T(8,128)(2,1)}, bf16[512,2048]{1,0:T(8,128)(2,1)S(1)}, u32[]{:S(2)}, u32[]{:S(2)}) collective-permute-start(bf16[512,2048]{1,0:T(8,128)(2,1)} %get-tuple-element.37), channel_id=1, source_target_pairs={{0,1},{1,0},{2,3},{3,2},{4,5},{5,4},{6,7},{7,6},{8,9},{9,8},{10,11... | collective-permute-start | bytes 6291464 | tf_op jit(solution)/shard_map/ppermute | solution.py:72
  107.7 99.7 %collective-permute-start.17 = (bf16[512,2048]{1,0:T(8,128)(2,1)}, bf16[512,2048]{1,0:T(8,128)(2,1)}, u32[]{:S(2)}, u32[]{:S(2)}) collective-permute-start(bf16[512,2048]{1,0:T(8,128)(2,1)} %get-tuple-element.37), channel_id=1, source_target_pairs={{0,2},{2,0},{4,6},{6,4},{8,10},{10,8},{12,14},{14,12},{16,18},{18,... | collective-permute-start | bytes 6291464 | tf_op jit(solution)/shard_map/ppermute | solution.py:59
  108.6 27.0 %collective-permute-start.8 = (bf16[512,2048]{1,0:T(8,128)(2,1)}, bf16[512,2048]{1,0:T(8,128)(2,1)}, u32[]{:S(2)}, u32[]{:S(2)}) collective-permute-start(bf16[512,2048]{1,0:T(8,128)(2,1)} %order.18), channel_id=1, source_target_pairs={{0,2},{2,0},{4,6},{6,4},{8,10},{10,8},{12,14},{14,12},{16,18},{18,... | collective-permute-start | bytes 6291464 | tf_op jit(solution)/shard_map/ppermute | solution.py:59
  110.6 234.0 %reduce-scatter.3.cloned.1.call-start = ((), (), s32[]{:S(2)}) async-start(), calls=%async_computation.4 | async-start | bytes 4718592 | tf_op jit(solution)/shard_map/reduce_scatter | solution.py:191
  160.2 47.2 %collective-permute-start.16 = (bf16[512,2048]{1,0:T(8,128)(2,1)}, bf16[512,2048]{1,0:T(8,128)(2,1)}, u32[]{:S(2)}, u32[]{:S(2)}) collective-permute-start(bf16[512,2048]{1,0:T(8,128)(2,1)} %order.22), channel_id=1, source_target_pairs={{0,2},{2,0},{4,6},{6,4},{8,10},{10,8},{12,14},{14,12},{16,18},{18,... | collective-permute-start | bytes 6291464 | tf_op jit(solution)/shard_map/ppermute | solution.py:59
  228.8 202.9 %reduce-scatter.5.cloned.1.call-start = ((), (), s32[]{:S(2)}) async-start(), calls=%async_computation.5 | async-start | bytes 4718592 | tf_op jit(solution)/shard_map/reduce_scatter | solution.py:191
  275.5 59.1 %collective-permute-start.19 = (bf16[512,2048]{1,0:T(8,128)(2,1)S(1)}, bf16[512,2048]{1,0:T(8,128)(2,1)}, u32[]{:S(2)}, u32[]{:S(2)}) collective-permute-start(bf16[512,2048]{1,0:T(8,128)(2,1)S(1)} %add_convert_fusion.1.refs_4_), channel_id=1, source_target_pairs={{0,1},{1,0},{2,3},{3,2},{4,5},{5,4},{6,7},{7,6},{8,9},{9,8},{10,11... | collective-permute-start | bytes 6291464 | tf_op jit(solution)/shard_map/ppermute | solution.py:72
  343.4 85.4 %collective-permute-start.23 = (bf16[512,2048]{1,0:T(8,128)(2,1)S(1)}, bf16[512,2048]{1,0:T(8,128)(2,1)}, u32[]{:S(2)}, u32[]{:S(2)}) collective-permute-start(bf16[512,2048]{1,0:T(8,128)(2,1)S(1)} %add_convert_fusion.refs_3_), channel_id=1, source_target_pairs={{0,1},{1,0},{2,3},{3,2},{4,5},{5,4},{6,7},{7,6},{8,9},{9,8},{10,11... | collective-permute-start | bytes 6291464 | tf_op jit(solution)/shard_map/ppermute | solution.py:72
  347.5 86.2 %collective-permute-start.28 = (f32[128,1024]{1,0:T(8,128)}, f32[128,1024]{1,0:T(8,128)}, u32[]{:S(2)}, u32[]{:S(2)}) collective-permute-start(f32[128,1024]{1,0:T(8,128)} %constant_dynamic-slice_fusion.4), channel_id=1, source_target_pairs={{0,2},{2,0},{4,6},{6,4},{8,10},{10,8},{12,14},{14,12},{16,18},{18,... | collective-permute-start | bytes 1572872 | tf_op jit(solution)/shard_map/ppermute | solution.py:59
  396.9 40.3 %collective-permute-start.26 = (bf16[512,1408]{1,0:T(8,128)(2,1)}, bf16[512,1408]{1,0:T(8,128)(2,1)}, u32[]{:S(2)}, u32[]{:S(2)}) collective-permute-start(bf16[512,1408]{1,0:T(8,128)(2,1)} %pad_maximum_fusion.3), channel_id=1, source_target_pairs={{0,4},{2,6},{4,0},{6,2},{8,12},{10,14},{12,8},{14,10},{16,20},{18,... | collective-permute-start | bytes 4325384 | tf_op jit(solution)/shard_map/ppermute | solution.py:59
  415.6 69.0 %collective-permute-start.25 = (bf16[512,2048]{1,0:T(8,128)(2,1)}, bf16[512,2048]{1,0:T(8,128)(2,1)}, u32[]{:S(2)}, u32[]{:S(2)}) collective-permute-start(bf16[512,2048]{1,0:T(8,128)(2,1)} %get-tuple-element.50), channel_id=1, source_target_pairs={{0,2},{2,0},{4,6},{6,4},{8,10},{10,8},{12,14},{14,12},{16,18},{18,... | collective-permute-start | bytes 6291464 | tf_op jit(solution)/shard_map/ppermute | solution.py:59
  428.8 38.8 %collective-permute-start.36 = (bf16[512,1408]{1,0:T(8,128)(2,1)}, bf16[512,1408]{1,0:T(8,128)(2,1)S(1)}, u32[]{:S(2)}, u32[]{:S(2)}) collective-permute-start(bf16[512,1408]{1,0:T(8,128)(2,1)} %pad_maximum_fusion.4), channel_id=1, source_target_pairs={{0,4},{2,6},{4,0},{6,2},{8,12},{10,14},{12,8},{14,10},{16,20},{18,... | collective-permute-start | bytes 4325384 | tf_op jit(solution)/shard_map/ppermute | solution.py:59
  428.9 83.4 %collective-permute-start.24 = (bf16[512,2048]{1,0:T(8,128)(2,1)}, bf16[512,2048]{1,0:T(8,128)(2,1)}, u32[]{:S(2)}, u32[]{:S(2)}) collective-permute-start(bf16[512,2048]{1,0:T(8,128)(2,1)} %order.26), channel_id=1, source_target_pairs={{0,2},{2,0},{4,6},{6,4},{8,10},{10,8},{12,14},{14,12},{16,18},{18,... | collective-permute-start | bytes 6291464 | tf_op jit(solution)/shard_map/ppermute | solution.py:59
  439.4 43.5 %collective-permute-start.27 = (bf16[256,1408]{1,0:T(8,128)(2,1)}, bf16[256,1408]{1,0:T(8,128)(2,1)S(1)}, u32[]{:S(2)}, u32[]{:S(2)}) collective-permute-start(bf16[256,1408]{1,0:T(8,128)(2,1)} %order.27), channel_id=1, source_target_pairs={{0,8},{2,10},{4,12},{6,14},{8,16},{10,18},{12,20},{14,22},{16,24},... | collective-permute-start | bytes 2162696 | tf_op jit(solution)/shard_map/ppermute | solution.py:59
  453.6 66.3 %collective-permute-start.37 = (bf16[256,1408]{1,0:T(8,128)(2,1)}, bf16[256,1408]{1,0:T(8,128)(2,1)}, u32[]{:S(2)}, u32[]{:S(2)}) collective-permute-start(bf16[256,1408]{1,0:T(8,128)(2,1)} %order.29), channel_id=1, source_target_pairs={{0,16},{2,18},{4,20},{6,22},{8,24},{10,26},{12,28},{14,30},{16,0},... | collective-permute-start | bytes 2162696 | tf_op jit(solution)/shard_map/ppermute | solution.py:59
  470.9 49.0 %collective-permute-start.38 = (bf16[256,1408]{1,0:T(8,128)(2,1)}, bf16[256,1408]{1,0:T(8,128)(2,1)}, u32[]{:S(2)}, u32[]{:S(2)}) collective-permute-start(bf16[256,1408]{1,0:T(8,128)(2,1)} %add_rows.7), channel_id=1, source_target_pairs={{0,24},{2,26},{4,28},{6,30},{8,0},{10,2},{12,4},{14,6},{16,8},{18,... | collective-permute-start | bytes 2162696 | tf_op jit(solution)/shard_map/ppermute | solution.py:59
  493.1 24.7 %collective-permute-start.31 = (f32[80,128]{1,0:T(8,128)S(1)}, f32[80,128]{1,0:T(8,128)S(1)}, u32[]{:S(2)}, u32[]{:S(2)}) collective-permute-start(f32[80,128]{1,0:T(8,128)S(1)} %add.360), channel_id=1, source_target_pairs={{0,8},{2,10},{4,12},{6,14},{8,0},{10,2},{12,4},{14,6},{16,24},{18,... | collective-permute-start | bytes 122888 | tf_op jit(solution)/shard_map/ppermute | solution.py:80
  (66 other events, 673.0 us)
Sparse Core Ops, SparseCore 0:
  43.5 87.3 all-gather.2
  133.0 70.8 all-gather.4
  228.9 100.0 reduce-scatter.2
  332.9 89.9 reduce-scatter.4

commit v5 on v4

--- a/solution.py
+++ b/solution.py
@@ -832,7 +832,7 @@
     cross = lambda values: [
         grid.send_x(value, -order[2 * i][0]) for i, value in enumerate(values)
     ]
-    d_normed, branch, g_norm_part = [], [], 0.0
+    d_normed, branch, done, g_norm_part = [], [], [], 0.0
     for out_there, out_here in out_far:
         out_there = grid.swap_core(out_there)
         branch.append((out_here.astype(F32) + out_there.astype(F32)).astype(BF16))
@@ -844,10 +844,13 @@
         there, here, more = run_back(d_z, d_xb, w_z, w_x, normed, slot, i)
         g_norm_part = g_norm_part + more
         there = grid.swap_core(tie(there, *branch))
+        done.append((here, there))
+    d_xb, more_channels, more_heads = run_bwd(
+        xb, y, d_y, s1, xs, slope, *scan, far, 2, d_xb, (*[here for here, _ in done], g_o)
+    )
+    for here, there in done:
+        there = tie(there, g_channels + more_channels)
         d_normed.append((here.astype(F32) + there.astype(F32)).astype(BF16))
-    d_xb, more_channels, more_heads = run_bwd(
-        xb, y, d_y, s1, xs, slope, *scan, far, 2, d_xb, (*d_normed, g_o)
-    )
     d_normed = cross(d_normed)
     g_channels, g_heads = g_channels + more_channels, g_heads + more_heads
     g_skip = g_channels[5, :inner].reshape(heads, HEAD_DIM).sum(axis=1)

time: 560 us -> 562 us (level)
  waiting for transfers between devices: 90.8 us -> 80.6 us
  starting transfers between devices: 70.9 us -> 80.3 us
    ppermute x30, waiting for transfers between devices: 87.2 us -> 75.5 us  [_dp(): return lax.ppermute(value, 'dp', pairs)]
    ppermute x3, starting transfers between devices: 21.9 us -> 28.1 us  [chip_sum(): lax.ppermute(value, 'dp', [(i, i ^ bit) for i in range(self.dp)])]
    unnamed x101 -> x115, local copies, waits for them, and re-layouts: 23.1 us -> 26.2 us
  transfers between devices with their start and end apart: 45 -> 45, of which waited for: 17 -> 15; matrix products, arithmetic and copies ran while one was open for 33% -> 33% of each run, Pallas kernels for 30% -> 29%
where the time goes in v5:
time: 562 us; the launch traced here: 555 us
  Pallas kernels  165 us (29%)
  matrix products  93.6 us (17%)
  waiting for transfers between devices  80.6 us (14%)
  starting transfers between devices  80.3 us (14%)
  other arithmetic  62.1 us (11%)
  local copies, waits for them, and re-layouts  57.2 us (10%)
  between operations  15.8 us (3%)
    ppermute x30, waiting for transfers between devices, _dp(): return lax.ppermute(value, 'dp', pairs)  75.5 us
    pallas_call x2, Pallas kernels, run_bwd(): pl.pallas_call(kernel, grid_spec=pl.GridSpec(grid=(count,), in_specs=[per...  56.1 us
    dot_general x3, matrix products, dot_nn(): lax.dot_general(a, b, (((1,), (0,)), ((), ())), preferred_element_type=F32)  52.3 us
    ppermute x30, starting transfers between devices, _dp(): return lax.ppermute(value, 'dp', pairs)  46 us
    dot_general x3, matrix products, dot_tn(): lax.dot_general(a, b, (((0,), (0,)), ((), ())), preferred_element_type=F32)  41.3 us
    pallas_call x2, Pallas kernels, run_back(): pl.pallas_call(functools.partial(back_kernel, len(waits)), grid=(width //...  33.8 us
    ppermute x3, starting transfers between devices, chip_sum(): lax.ppermute(value, 'dp', [(i, i ^ bit) for i in range(self.dp)])  28.1 us
    pallas_call x1, Pallas kernels, run_fwd(): pl.pallas_call(functools.partial(fwd_kernel, len(waits)), grid_spec=pltpu...  27.1 us
  transfers between devices with their start and end apart: 45, of which 15 were waited for; matrix products, arithmetic and copies ran while one was open for 33% of the time, Pallas kernels for 29%

profile of v5, /device:TPU:0, one launch (start us, length us, event | category | flops | bytes accessed | tf_op | source)
XLA Modules:
  0.0 554.7 jit_solution(5326581189782936721)
XLA Ops:
  33.1 6.1 %collective-permute-done.3.refs_1_ = bf16[256,1408]{1,0:T(8,128)(2,1)S(1)} collective-permute-done((bf16[256,1408]{1,0:T(8,128)(2,1)S(1)}, bf16[256,1408]{1,0:T(8,128)(2,1)S(1)}, u32[]{:S(2)}, u32[]{:S(2)}) %collective-permute-start.3) | collective-permute-done | bytes 720928 | tf_op jit(solution)/shard_map/ppermute | solution.py:59
  48.0 19.6 %collective-permute-done.5.refs_1_ = bf16[256,1408]{1,0:T(8,128)(2,1)S(1)} collective-permute-done((bf16[256,1408]{1,0:T(8,128)(2,1)}, bf16[256,1408]{1,0:T(8,128)(2,1)S(1)}, u32[]{:S(2)}, u32[]{:S(2)}) %collective-permute-start.5) | collective-permute-done | bytes 720928 | tf_op jit(solution)/shard_map/ppermute | solution.py:59
  67.6 7.6 %collective-permute-done.4.refs_0_ = bf16[256,1408]{1,0:T(8,128)(2,1)S(1)} collective-permute-done((bf16[256,1408]{1,0:T(8,128)(2,1)}, bf16[256,1408]{1,0:T(8,128)(2,1)S(1)}, u32[]{:S(2)}, u32[]{:S(2)}) %collective-permute-start.4) | collective-permute-done | bytes 720928 | tf_op jit(solution)/shard_map/ppermute | solution.py:59
  88.9 18.8 %collective-permute-done.6.refs_0_ = bf16[256,1408]{1,0:T(8,128)(2,1)S(1)} collective-permute-done((bf16[256,1408]{1,0:T(8,128)(2,1)}, bf16[256,1408]{1,0:T(8,128)(2,1)S(1)}, u32[]{:S(2)}, u32[]{:S(2)}) %collective-permute-start.6) | collective-permute-done | bytes 720928 | tf_op jit(solution)/shard_map/ppermute | solution.py:59
  121.8 12.8 %collective-permute-done.10 = bf16[256,1408]{1,0:T(8,128)(2,1)S(1)} collective-permute-done((bf16[256,1408]{1,0:T(8,128)(2,1)S(1)}, bf16[256,1408]{1,0:T(8,128)(2,1)S(1)}, u32[]{:S(2)}, u32[]{:S(2)}) %collective-permute-start.10) | collective-permute-done | bytes 720928 | tf_op jit(solution)/shard_map/ppermute | solution.py:59
  140.4 18.5 %fusion.21.xb_ref.refs_1_ = f32[2048,1408]{1,0:T(8,128)} fusion(bf16[2048,2048]{1,0:T(8,128)(2,1)S(1)} %pad_maximum_fusion.normed_ref, bf16[2048,1408]{1,0:T(8,128)(2,1)} %constant_dynamic-update-slice_fusion.wx_ref), kind=kOutput, calls=%fused_computation.132 | convolution fusion | flops 11811160064 | bytes 25690112 | tf_op jit(solution)/shard_map/dot_general | solution.py:27
  160.9 27.1 %scan_forward.1 = (f32[2048,1024]{1,0:T(8,128)}, bf16[4096,128]{1,0:T(8,128)(2,1)}, bf16[2048,1024]{1,0:T(8,128)(2,1)}, bf16[2048,1024]{1,0:T(8,128)(2,1)}) custom-call(s32[4]{0:T(128)} %subtract_clamp_fusion.limit_ref, f32[2048,1408]{1,0:T(8,128)} %fusion.21.xb_ref.refs_1_, f32[8,1408]{1,0:T(8,128)} %select_maximum_fusion.taps_ref, ...), custom_call_target="tpu_custom_call" | custom-call | flops 24999999488 | tf_op jit(solution)/shard_map/scan_forward/pallas_call | solution.py:455
  188.0 17.7 %multiply_reduce_fusion.2 = (f32[2048]{0:T(1024)S(1)}, f32[2048,1024]{1,0:T(8,128)}, bf16[2048,1024]{1,0:T(8,128)(2,1)}) fusion(f32[2048,1024]{1,0:T(8,128)} %get-tuple-element.36.y_ref, bf16[2048,2048]{1,0:T(8,128)(2,1)} %copy-done.1, bf16[2048,1024]{1,0:T(8,128)(2,1)} %all-gather.3.cloned.1.call-done.wz_ref), kind=kOutput, calls=%fused_computation.18 | convolution fusion | flops 8606709760 | bytes 33562624 | tf_op jit(solution)/shard_map/dot_general | solution.py:27
  217.8 10.9 %convolution_convert_fusion.2.refs_1_.refs_2_ = bf16[2048,1024]{1,0:T(8,128)(2,1)} fusion(bf16[2048,2048]{1,0:T(8,128)(2,1)S(1)} %pad_maximum_fusion.1, bf16[2048,1024]{1,0:T(8,128)(2,1)S(1)} %multiply_convert_fusion.gnorm_ref), kind=kOutput, calls=%fused_computation.25 | convolution fusion | flops 8592031744 | bytes 16777216 | tf_op jit(solution)/shard_map/dot_general | solution.py:35
  228.8 16.0 %multiply_reduce_fusion = (f32[1024]{0:T(1024)S(1)}, f32[2048]{0:T(1024)S(1)}, bf16[2048,1024]{1,0:T(8,128)(2,1)}) fusion(f32[2048,1024]{1,0:T(8,128)} %get-tuple-element.119, f32[2048]{0:T(1024)S(1)} %add_rsqrt_fusion, f32[1024]{0:T(1024)S(1)} %dynamic_slice.111, bf16[2048,2048]{1,0:T(8,128)(2,1)} %copy-done.6, bf16[2048,1024]{1,0:T(8,128)(2,1)} %order.24.wo_ref), kind=kOutput, calls=%fused_computation.14 | convolution fusion | flops 8604611584 | bytes 25190400 | tf_op jit(solution)/shard_map/dot_general | solution.py:27
  247.0 10.1 %branch_rows.2 = (bf16[512,2048]{1,0:T(8,128)(2,1)}, bf16[512,2048]{1,0:T(8,128)(2,1)}) custom-call(bf16[2048,1024]{1,0:T(8,128)(2,1)} %copy-done.2, bf16[2048,1024]{1,0:T(8,128)(2,1)} %order.24.wo_ref, f32[2048]{0:T(1024)} %copy-done.38), custom_call_target="tpu_custom_call" | custom-call | tf_op jit(solution)/shard_map/branch_rows/pallas_call | solution.py:614
  258.5 13.0 %fusion.8 = (bf16[2048,1024]{1,0:T(8,128)(2,1)}, bf16[2048,1024]{1,0:T(8,128)(2,1)S(1)}) fusion(bf16[2048,1024]{1,0:T(8,128)(2,1)} %get-tuple-element.123, f32[2048,1024]{1,0:T(8,128)} %get-tuple-element.119, bf16[2048,1024]{1,0:T(8,128)(2,1)} %get-tuple-element.122, f32[2048]{0:T(1024)S(1)} %fusion.12, f32[2048]{0:T(1024)S(1)} %add_rsqrt_fusion, ...), kind=kLoop, calls=%fused_computation.11 | loop fusion | flops 37748736 | bytes 33570816 | tf_op jit(solution)/shard_map/convert_element_type | solution.py:827
  273.4 12.9 %convolution_convert_fusion.1.refs_3_ = bf16[2048,1024]{1,0:T(8,128)(2,1)} fusion(bf16[2048,2048]{1,0:T(8,128)(2,1)} %copy-done.1, bf16[2048,1024]{1,0:T(8,128)(2,1)S(1)} %get-tuple-element.121.dz_ref), kind=kOutput, calls=%fused_computation.24 | convolution fusion | flops 8592031744 | bytes 16777216 | tf_op jit(solution)/shard_map/dot_general | solution.py:35
  290.6 28.2 %scan_backward.2 = (bf16[2048,1408]{1,0:T(8,128)(2,1)}, f32[8,1408]{1,0:T(8,128)}, f32[8,128]{1,0:T(8,128)}) custom-call(f32[2048,1408]{1,0:T(8,128)} %fusion.21.xb_ref.refs_1_, f32[2048,1024]{1,0:T(8,128)} %get-tuple-element.36.y_ref, bf16[2048,1024]{1,0:T(8,128)(2,1)} %get-tuple-element.120.dy_ref, bf16[4096,128]{1,0:T(8,128)(2,1)} %get-tuple-element.40.s1_ref, ...), custom_call_target="tpu_custom_call" | custom-call | flops 8000000000 | tf_op jit(solution)/shard_map/scan_backward/pallas_call | solution.py:502
  318.8 16.8 %normed_gradient.2 = (bf16[512,2048]{1,0:T(8,128)(2,1)}, bf16[512,2048]{1,0:T(8,128)(2,1)}, f32[8,2048]{1,0:T(8,128)}) custom-call(bf16[2048,1024]{1,0:T(8,128)(2,1)} %copy-done.3, bf16[2048,1408]{1,0:T(8,128)(2,1)} %get-tuple-element.43.dxb_ref.refs_2_, bf16[2048,1024]{1,0:T(8,128)(2,1)} %all-gather.3.cloned.1.call-done.wz_ref, ...), custom_call_target="tpu_custom_call" | custom-call | tf_op jit(solution)/shard_map/normed_gradient/pallas_call | solution.py:582
  341.0 28.0 %scan_backward.3 = (bf16[2048,1408]{1,0:T(8,128)(2,1)}, f32[8,1408]{1,0:T(8,128)}, f32[8,128]{1,0:T(8,128)}) custom-call(f32[2048,1408]{1,0:T(8,128)} %fusion.21.xb_ref.refs_1_, f32[2048,1024]{1,0:T(8,128)} %get-tuple-element.36.y_ref, bf16[2048,1024]{1,0:T(8,128)(2,1)} %get-tuple-element.120.dy_ref, ...), custom_call_target="tpu_custom_call", output_to_operand_aliasing={{0}: (9, {})} | custom-call | flops 8000000000 | tf_op jit(solution)/shard_map/scan_backward/pallas_call | solution.py:502
  369.0 17.5 %convolution_convert_fusion.refs_0_ = bf16[2048,1408]{1,0:T(8,128)(2,1)S(1)} fusion(bf16[2048,2048]{1,0:T(8,128)(2,1)} %copy-done.1, bf16[2048,1408]{1,0:T(8,128)(2,1)} %get-tuple-element.45.dxb_ref), kind=kOutput, calls=%fused_computation.21 | convolution fusion | flops 11814043648 | bytes 19922944 | tf_op jit(solution)/shard_map/dot_general | solution.py:35
  398.5 16.9 %normed_gradient.3 = (bf16[512,2048]{1,0:T(8,128)(2,1)}, bf16[512,2048]{1,0:T(8,128)(2,1)}, f32[8,2048]{1,0:T(8,128)}) custom-call(bf16[2048,1024]{1,0:T(8,128)(2,1)} %copy-done.3, bf16[2048,1408]{1,0:T(8,128)(2,1)} %get-tuple-element.45.dxb_ref, bf16[2048,1024]{1,0:T(8,128)(2,1)} %all-gather.3.cloned.1.call-done.wz_ref, ...), custom_call_target="tpu_custom_call" | custom-call | tf_op jit(solution)/shard_map/normed_gradient/pallas_call | solution.py:582
  416.8 9.9 %branch_rows.3 = (bf16[512,2048]{1,0:T(8,128)(2,1)}, bf16[512,2048]{1,0:T(8,128)(2,1)}) custom-call(bf16[2048,1024]{1,0:T(8,128)(2,1)} %copy-done.2, bf16[2048,1024]{1,0:T(8,128)(2,1)} %order.24.wo_ref, bf16[512,2048]{1,0:T(8,128)(2,1)} %get-tuple-element.46.refs_0_.refs_1_), custom_call_target="tpu_custom_call" | custom-call | tf_op jit(solution)/shard_map/branch_rows/pallas_call | solution.py:614
  436.7 10.0 %collective-permute-start.27 = (bf16[256,1408]{1,0:T(8,128)(2,1)}, bf16[256,1408]{1,0:T(8,128)(2,1)}, u32[]{:S(2)}, u32[]{:S(2)}) collective-permute-start(bf16[256,1408]{1,0:T(8,128)(2,1)} %order.29), channel_id=1, source_target_pairs={{0,8},{2,10},{4,12},{6,14},{8,16},{10,18},{12,20},{14,22},{16,24},... | collective-permute-start | bytes 2162696 | tf_op jit(solution)/shard_map/ppermute | solution.py:59
  454.2 6.6 %collective-permute-start.37 = (bf16[256,1408]{1,0:T(8,128)(2,1)}, bf16[256,1408]{1,0:T(8,128)(2,1)S(1)}, u32[]{:S(2)}, u32[]{:S(2)}) collective-permute-start(bf16[256,1408]{1,0:T(8,128)(2,1)} %order.31), channel_id=1, source_target_pairs={{0,16},{2,18},{4,20},{6,22},{8,24},{10,26},{12,28},{14,30},{16,0},... | collective-permute-start | bytes 2162696 | tf_op jit(solution)/shard_map/ppermute | solution.py:59
  465.1 13.5 %collective-permute-start.38 = (bf16[256,1408]{1,0:T(8,128)(2,1)}, bf16[256,1408]{1,0:T(8,128)(2,1)}, u32[]{:S(2)}, u32[]{:S(2)}) collective-permute-start(bf16[256,1408]{1,0:T(8,128)(2,1)} %add_rows.7), channel_id=1, source_target_pairs={{0,24},{2,26},{4,28},{6,30},{8,0},{10,2},{12,4},{14,6},{16,8},{18,... | collective-permute-start | bytes 2162696 | tf_op jit(solution)/shard_map/ppermute | solution.py:59
  483.0 22.6 %collective-permute-start.31 = (f32[80,128]{1,0:T(8,128)S(1)}, f32[80,128]{1,0:T(8,128)S(1)}, u32[]{:S(2)}, u32[]{:S(2)}) collective-permute-start(f32[80,128]{1,0:T(8,128)S(1)} %add.361), channel_id=1, source_target_pairs={{0,8},{2,10},{4,12},{6,14},{8,0},{10,2},{12,4},{14,6},{16,24},{18,... | collective-permute-start | bytes 122888 | tf_op jit(solution)/shard_map/ppermute | solution.py:80
  505.6 8.5 %input_gradient.1 = bf16[512,2048]{1,0:T(8,128)(2,1)} custom-call(bf16[512,2048]{1,0:T(8,128)(2,1)} %u_ref.5, bf16[512,2048]{1,0:T(8,128)(2,1)} %cot_ref.3, f32[1,2048]{1,0:T(1,128)} %bitcast.105, bf16[512,2048]{1,0:T(8,128)(2,1)} %collective-permute-done.23.refs_1_.refs_0_, bf16[512,2048]{1,0:T(8,128)(2,1)} %get-tuple-element.46.refs_0_.refs_1_, ...), custom_call_target="tpu_custom_call" | custom-call | flops 8000000000 | tf_op jit(solution)/shard_map/input_gradient/pallas_call | solution.py:675
  (334 shorter events, 169.3 us)
Async XLA Ops:
  7.2 180.8 %all-gather.3.cloned.1.call-start = ((), (), s32[]{:S(2)}) async-start(), calls=%async_computation.2 | async-start | bytes 4718592 | tf_op jit(solution)/shard_map/all_gather | solution.py:187
  43.4 185.4 %all-gather.5.cloned.1.call-start = ((), (), s32[]{:S(2)}) async-start(), calls=%async_computation.3 | async-start | bytes 4718592 | tf_op jit(solution)/shard_map/all_gather | solution.py:187
  43.4 65.2 %collective-permute-start = (bf16[512,2048]{1,0:T(8,128)(2,1)}, bf16[512,2048]{1,0:T(8,128)(2,1)}, u32[]{:S(2)}, u32[]{:S(2)}) collective-permute-start(bf16[512,2048]{1,0:T(8,128)(2,1)} %get-tuple-element.35.refs_1_), channel_id=1, source_target_pairs={{0,1},{1,0},{2,3},{3,2},{4,5},{5,4},{6,7},{7,6},{8,9},{9,8},{10,11... | collective-permute-start | bytes 6291464 | tf_op jit(solution)/shard_map/ppermute | solution.py:72
  45.5 29.7 %collective-permute-start.4 = (bf16[256,1408]{1,0:T(8,128)(2,1)}, bf16[256,1408]{1,0:T(8,128)(2,1)S(1)}, u32[]{:S(2)}, u32[]{:S(2)}) collective-permute-start(bf16[256,1408]{1,0:T(8,128)(2,1)} %order.16.refs_1_), channel_id=1, source_target_pairs={{0,8},{2,10},{4,12},{6,14},{8,16},{10,18},{12,20},{14,22},{16,24},... | collective-permute-start | bytes 2162696 | tf_op jit(solution)/shard_map/ppermute | solution.py:59
  45.8 89.8 %collective-permute-start.9 = (bf16[512,2048]{1,0:T(8,128)(2,1)}, bf16[512,2048]{1,0:T(8,128)(2,1)}, u32[]{:S(2)}, u32[]{:S(2)}) collective-permute-start(bf16[512,2048]{1,0:T(8,128)(2,1)} %get-tuple-element.35.refs_1_), channel_id=1, source_target_pairs={{0,2},{2,0},{4,6},{6,4},{8,10},{10,8},{12,14},{14,12},{16,18},{18,... | collective-permute-start | bytes 6291464 | tf_op jit(solution)/shard_map/ppermute | solution.py:59
  46.7 61.9 %collective-permute-start.14 = (bf16[128,1024]{1,0:T(8,128)(2,1)}, bf16[128,1024]{1,0:T(8,128)(2,1)}, u32[]{:S(2)}, u32[]{:S(2)}) collective-permute-start(bf16[128,1024]{1,0:T(8,128)(2,1)} %order.22), channel_id=1, source_target_pairs={{0,2},{2,0},{4,6},{6,4},{8,10},{10,8},{12,14},{14,12},{16,18},{18,... | collective-permute-start | bytes 786440 | tf_op jit(solution)/shard_map/ppermute | solution.py:59
  77.7 30.1 %collective-permute-start.6 = (bf16[256,1408]{1,0:T(8,128)(2,1)}, bf16[256,1408]{1,0:T(8,128)(2,1)S(1)}, u32[]{:S(2)}, u32[]{:S(2)}) collective-permute-start(bf16[256,1408]{1,0:T(8,128)(2,1)} %order.17), channel_id=1, source_target_pairs={{0,8},{2,10},{4,12},{6,14},{8,16},{10,18},{12,20},{14,22},{16,24},... | collective-permute-start | bytes 2162696 | tf_op jit(solution)/shard_map/ppermute | solution.py:59
  88.9 70.0 %collective-permute-start.15 = (bf16[512,2048]{1,0:T(8,128)(2,1)}, bf16[512,2048]{1,0:T(8,128)(2,1)S(1)}, u32[]{:S(2)}, u32[]{:S(2)}) collective-permute-start(bf16[512,2048]{1,0:T(8,128)(2,1)} %get-tuple-element.37), channel_id=1, source_target_pairs={{0,1},{1,0},{2,3},{3,2},{4,5},{5,4},{6,7},{7,6},{8,9},{9,8},{10,11... | collective-permute-start | bytes 6291464 | tf_op jit(solution)/shard_map/ppermute | solution.py:72
  107.8 99.6 %collective-permute-start.17 = (bf16[512,2048]{1,0:T(8,128)(2,1)}, bf16[512,2048]{1,0:T(8,128)(2,1)}, u32[]{:S(2)}, u32[]{:S(2)}) collective-permute-start(bf16[512,2048]{1,0:T(8,128)(2,1)} %get-tuple-element.37), channel_id=1, source_target_pairs={{0,2},{2,0},{4,6},{6,4},{8,10},{10,8},{12,14},{14,12},{16,18},{18,... | collective-permute-start | bytes 6291464 | tf_op jit(solution)/shard_map/ppermute | solution.py:59
  110.7 226.9 %reduce-scatter.3.cloned.1.call-start = ((), (), s32[]{:S(2)}) async-start(), calls=%async_computation.4 | async-start | bytes 4718592 | tf_op jit(solution)/shard_map/reduce_scatter | solution.py:191
  160.2 47.2 %collective-permute-start.16 = (bf16[512,2048]{1,0:T(8,128)(2,1)}, bf16[512,2048]{1,0:T(8,128)(2,1)}, u32[]{:S(2)}, u32[]{:S(2)}) collective-permute-start(bf16[512,2048]{1,0:T(8,128)(2,1)} %order.23), channel_id=1, source_target_pairs={{0,2},{2,0},{4,6},{6,4},{8,10},{10,8},{12,14},{14,12},{16,18},{18,... | collective-permute-start | bytes 6291464 | tf_op jit(solution)/shard_map/ppermute | solution.py:59
  228.8 198.9 %reduce-scatter.5.cloned.1.call-start = ((), (), s32[]{:S(2)}) async-start(), calls=%async_computation.5 | async-start | bytes 4718592 | tf_op jit(solution)/shard_map/reduce_scatter | solution.py:191
  289.3 48.2 %collective-permute-start.19 = (bf16[512,2048]{1,0:T(8,128)(2,1)S(1)}, bf16[512,2048]{1,0:T(8,128)(2,1)}, u32[]{:S(2)}, u32[]{:S(2)}) collective-permute-start(bf16[512,2048]{1,0:T(8,128)(2,1)S(1)} %add_convert_fusion.1.refs_4_), channel_id=1, source_target_pairs={{0,1},{1,0},{2,3},{3,2},{4,5},{5,4},{6,7},{7,6},{8,9},{9,8},{10,11... | collective-permute-start | bytes 6291464 | tf_op jit(solution)/shard_map/ppermute | solution.py:72
  337.5 56.3 %collective-permute-start.22 = (bf16[512,2048]{1,0:T(8,128)(2,1)}, bf16[512,2048]{1,0:T(8,128)(2,1)}, u32[]{:S(2)}, u32[]{:S(2)}) collective-permute-start(bf16[512,2048]{1,0:T(8,128)(2,1)} %order.26), channel_id=1, source_target_pairs={{0,2},{2,0},{4,6},{6,4},{8,10},{10,8},{12,14},{14,12},{16,18},{18,... | collective-permute-start | bytes 6291464 | tf_op jit(solution)/shard_map/ppermute | solution.py:59
  340.5 90.1 %collective-permute-start.28 = (f32[128,1024]{1,0:T(8,128)}, f32[128,1024]{1,0:T(8,128)}, u32[]{:S(2)}, u32[]{:S(2)}) collective-permute-start(f32[128,1024]{1,0:T(8,128)} %constant_dynamic-slice_fusion.4), channel_id=1, source_target_pairs={{0,2},{2,0},{4,6},{6,4},{8,10},{10,8},{12,14},{14,12},{16,18},{18,... | collective-permute-start | bytes 1572872 | tf_op jit(solution)/shard_map/ppermute | solution.py:59
  391.6 41.8 %collective-permute-start.26 = (bf16[512,1408]{1,0:T(8,128)(2,1)}, bf16[512,1408]{1,0:T(8,128)(2,1)S(1)}, u32[]{:S(2)}, u32[]{:S(2)}) collective-permute-start(bf16[512,1408]{1,0:T(8,128)(2,1)} %pad_maximum_fusion.3), channel_id=1, source_target_pairs={{0,4},{2,6},{4,0},{6,2},{8,12},{10,14},{12,8},{14,10},{16,20},{18,... | collective-permute-start | bytes 4325384 | tf_op jit(solution)/shard_map/ppermute | solution.py:59
  397.5 85.4 %collective-permute-start.23 = (bf16[512,2048]{1,0:T(8,128)(2,1)}, bf16[512,2048]{1,0:T(8,128)(2,1)}, u32[]{:S(2)}, u32[]{:S(2)}) collective-permute-start(bf16[512,2048]{1,0:T(8,128)(2,1)} %add_convert_fusion), channel_id=1, source_target_pairs={{0,1},{1,0},{2,3},{3,2},{4,5},{5,4},{6,7},{7,6},{8,9},{9,8},{10,11... | collective-permute-start | bytes 6291464 | tf_op jit(solution)/shard_map/ppermute | solution.py:72
  415.5 90.1 %collective-permute-start.25 = (bf16[512,2048]{1,0:T(8,128)(2,1)}, bf16[512,2048]{1,0:T(8,128)(2,1)}, u32[]{:S(2)}, u32[]{:S(2)}) collective-permute-start(bf16[512,2048]{1,0:T(8,128)(2,1)} %get-tuple-element.52), channel_id=1, source_target_pairs={{0,2},{2,0},{4,6},{6,4},{8,10},{10,8},{12,14},{14,12},{16,18},{18,... | collective-permute-start | bytes 6291464 | tf_op jit(solution)/shard_map/ppermute | solution.py:59
  426.7 35.1 %collective-permute-start.36 = (bf16[512,1408]{1,0:T(8,128)(2,1)}, bf16[512,1408]{1,0:T(8,128)(2,1)S(1)}, u32[]{:S(2)}, u32[]{:S(2)}) collective-permute-start(bf16[512,1408]{1,0:T(8,128)(2,1)} %pad_maximum_fusion.4), channel_id=1, source_target_pairs={{0,4},{2,6},{4,0},{6,2},{8,12},{10,14},{12,8},{14,10},{16,20},{18,... | collective-permute-start | bytes 4325384 | tf_op jit(solution)/shard_map/ppermute | solution.py:59
  436.7 41.9 %collective-permute-start.27 = (bf16[256,1408]{1,0:T(8,128)(2,1)}, bf16[256,1408]{1,0:T(8,128)(2,1)}, u32[]{:S(2)}, u32[]{:S(2)}) collective-permute-start(bf16[256,1408]{1,0:T(8,128)(2,1)} %order.29), channel_id=1, source_target_pairs={{0,8},{2,10},{4,12},{6,14},{8,16},{10,18},{12,20},{14,22},{16,24},... | collective-permute-start | bytes 2162696 | tf_op jit(solution)/shard_map/ppermute | solution.py:59
  454.2 63.6 %collective-permute-start.37 = (bf16[256,1408]{1,0:T(8,128)(2,1)}, bf16[256,1408]{1,0:T(8,128)(2,1)S(1)}, u32[]{:S(2)}, u32[]{:S(2)}) collective-permute-start(bf16[256,1408]{1,0:T(8,128)(2,1)} %order.31), channel_id=1, source_target_pairs={{0,16},{2,18},{4,20},{6,22},{8,24},{10,26},{12,28},{14,30},{16,0},... | collective-permute-start | bytes 2162696 | tf_op jit(solution)/shard_map/ppermute | solution.py:59
  465.1 53.6 %collective-permute-start.38 = (bf16[256,1408]{1,0:T(8,128)(2,1)}, bf16[256,1408]{1,0:T(8,128)(2,1)}, u32[]{:S(2)}, u32[]{:S(2)}) collective-permute-start(bf16[256,1408]{1,0:T(8,128)(2,1)} %add_rows.7), channel_id=1, source_target_pairs={{0,24},{2,26},{4,28},{6,30},{8,0},{10,2},{12,4},{14,6},{16,8},{18,... | collective-permute-start | bytes 2162696 | tf_op jit(solution)/shard_map/ppermute | solution.py:59
  482.9 59.2 %collective-permute-start.24 = (bf16[512,2048]{1,0:T(8,128)(2,1)}, bf16[512,2048]{1,0:T(8,128)(2,1)}, u32[]{:S(2)}, u32[]{:S(2)}) collective-permute-start(bf16[512,2048]{1,0:T(8,128)(2,1)} %order.28), channel_id=1, source_target_pairs={{0,2},{2,0},{4,6},{6,4},{8,10},{10,8},{12,14},{14,12},{16,18},{18,... | collective-permute-start | bytes 6291464 | tf_op jit(solution)/shard_map/ppermute | solution.py:59
  483.0 31.1 %collective-permute-start.31 = (f32[80,128]{1,0:T(8,128)S(1)}, f32[80,128]{1,0:T(8,128)S(1)}, u32[]{:S(2)}, u32[]{:S(2)}) collective-permute-start(f32[80,128]{1,0:T(8,128)S(1)} %add.361), channel_id=1, source_target_pairs={{0,8},{2,10},{4,12},{6,14},{8,0},{10,2},{12,4},{14,6},{16,24},{18,... | collective-permute-start | bytes 122888 | tf_op jit(solution)/shard_map/ppermute | solution.py:80
  (73 other events, 776.2 us)
Sparse Core Ops, SparseCore 0:
  43.5 87.3 all-gather.2
  133.0 70.7 all-gather.4
  228.9 100.0 reduce-scatter.2
  332.9 89.9 reduce-scatter.4
